TPU v7x, 32 devices: a whole 2x2x4 slice. The times are simulated.
32 devices in a mesh: group: 2 (over y), tm: 16 (over z, x, core).
Axes of the slice: x: 2, y: 2, z: 4, core: 2. Of those that a mesh axis runs over, the one named last changes fastest.
Arguments:
- features: bfloat16 [64, 192, 8, 256], P(('group', 'tm')), parts along dimension 0, may hold values from -6 to 6
- video_frames: int32 [16], P('group'), parts along dimension 0, may hold values from 1 to 16, 32 in all
- gain_first: float32 [192], replicated, may hold values from 0.1 to 1.9
- conv_first: bfloat16 [3, 3, 3, 192, 192], replicated, may hold values from -0.078125 to 0.078125
- gain_second: float32 [192], replicated, may hold values from 0.1 to 1.9
- conv_second: bfloat16 [3, 3, 3, 192, 192], replicated, may hold values from -0.078125 to 0.078125
Outputs:
- block_out: bfloat16 [64, 192, 8, 256], P(('group', 'tm')), parts along dimension 0
There are 2 independent parts, one for each index of `group`. A program takes and returns all parts, laid end to end along the dimension named above; an argument that names none is the same for every part. Nothing has to cross between parts.
Inputs may be any that keep to these rules, and one draw needn't show every extreme that they name: `video_frames`: each video's frame count; they sum to 32 and the largest is exactly 16.
All inputs are finite; a program needn't handle non-finite values.
Results may differ from a plain program's by a relative error of at most 0.0039.
Values may be sent and summed in bfloat16 or wider, within the bound.
No kernel may reach another device: no remote copies, remote signals or barrier semaphores. Data moves between devices by JAX's collectives and lax.ppermute only.
A program may use at most 128 MiB of HBM per device.

v0:
```python
import jax
import jax.numpy as jnp
from jax import lax
from jax.experimental import pallas as pl
from jax.experimental.pallas import tpu as pltpu
from jax.sharding import PartitionSpec as P

C = 192
ROWS = 8
COLS = 256
HALF = 128
SLAB = 3 * C
DEPTH = 9 * C
EPS = 1e-06
VMEM_LIMIT = 48 * 1024 * 1024
F32 = jnp.float32
BF16 = jnp.bfloat16


def shifted(value, axis):
    count = lax.axis_size(axis)
    return lax.ppermute(value, axis, [(i, i + 1) for i in range(count - 1)])


def tap_masks(frames_ref, first):
    def step(v, carry):
        begin, start0, start1 = carry
        start0 = jnp.where(begin <= first, begin, start0)
        start1 = jnp.where(begin <= first + 1, begin, start1)
        return begin + frames_ref[v], start0, start1

    zero = jnp.int32(0)
    _, start0, start1 = lax.fori_loop(0, frames_ref.shape[0], step, (zero, zero, zero))
    return tuple(
        jnp.where(test, 1.0, 0.0).astype(F32)
        for test in (
            first - 1 >= start0,
            first - 2 >= start0,
            first >= start1,
            first - 1 >= start1,
        )
    )


def first_frame():
    return 2 * lax.axis_index("tm")


def transpose_weights(w_ref, wt_ref):
    for k in range(3):
        wt_ref[k * C : (k + 1) * C, :] = w_ref[k * DEPTH : (k + 1) * DEPTH, :].T


def put_row(x_ref, row, values):
    base = (row + 1) * SLAB
    cols = lax.broadcasted_iota(jnp.int32, (C, COLS), 1)
    left = jnp.where(cols == 0, 0.0, pltpu.roll(values, 1, 1))
    right = jnp.where(cols == COLS - 1, 0.0, pltpu.roll(values, COLS - 1, 1))
    x_ref[base : base + C, :] = left.astype(BF16)
    x_ref[base + C : base + 2 * C, :] = values.astype(BF16)
    x_ref[base + 2 * C : base + 3 * C, :] = right.astype(BF16)


def clear_edges(x_ref):
    zeros = jnp.zeros((SLAB, COLS), BF16)
    x_ref[0:SLAB, :] = zeros
    x_ref[(ROWS + 1) * SLAB : (ROWS + 2) * SLAB, :] = zeros


def activate_features(f_ref, gain_ref, t_ref, x_ref):
    def squares(b, total):
        v = f_ref[0, pl.ds(b * 16, 16)].astype(F32)
        return total + jnp.sum(v * v, axis=0)

    total = lax.fori_loop(0, C // 16, squares, jnp.zeros((ROWS, COLS), F32))
    inverse = lax.rsqrt(total * (1.0 / C) + EPS)

    def act(b, _):
        for j in range(8):
            c = b * 8 + j
            u = f_ref[0, c].astype(F32) * inverse * gain_ref[c]
            u = u * jax.nn.sigmoid(u)
            at = pl.multiple_of(c * ROWS, ROWS)
            t_ref[0, pl.ds(at, ROWS), :] = u[:, :HALF]
            t_ref[1, pl.ds(at, ROWS), :] = u[:, HALF:]
        return 0

    lax.fori_loop(0, C // 8, act, 0)
    clear_edges(x_ref)
    for row in range(ROWS):
        put_row(
            x_ref,
            row,
            jnp.concatenate(
                [t_ref[h, pl.ds(row, C, stride=ROWS), :] for h in range(2)], axis=1
            ),
        )


def slab_of(s_ref, x_ref):
    clear_edges(x_ref)
    for row in range(ROWS):
        put_row(x_ref, row, s_ref[row].astype(F32))


def product(wt_ref, lo, hi, x_ref, row):
    return jnp.dot(
        wt_ref[lo * C : hi * C, :],
        x_ref[row * SLAB : row * SLAB + DEPTH, :],
        preferred_element_type=F32,
    )


def spread_gain(gain_ref, g_ref):
    def step(b, _):
        for j in range(8):
            c = b * 8 + j
            g_ref[pl.ds(c, 1), :] = jnp.full((1, COLS), gain_ref[c], F32)
        return 0

    lax.fori_loop(0, C // 8, step, 0)


def second_activation(values, g_ref):
    mean_square = jnp.sum(values * values, axis=0, keepdims=True) * (1.0 / C)
    u = values * lax.rsqrt(mean_square + EPS) * g_ref[...]
    return (u * jax.nn.sigmoid(u)).astype(BF16)


def to_output(t_ref, f_ref, o_ref):
    def step(b, _):
        for j in range(8):
            c = b * 8 + j
            at = pl.multiple_of(c * ROWS, ROWS)
            v = jnp.concatenate(
                [t_ref[h, pl.ds(at, ROWS), :] for h in range(2)], axis=1
            )
            o_ref[0, c] = (f_ref[0, c].astype(F32) + v).astype(BF16)
        return 0

    lax.fori_loop(0, C // 8, step, 0)


def put_transposed(t_ref, row, values):
    t_ref[0, pl.ds(row, C, stride=ROWS), :] = values[:, :HALF]
    t_ref[1, pl.ds(row, C, stride=ROWS), :] = values[:, HALF:]


def local_first(f0_ref, f1_ref, w_ref, gain_ref, frames_ref, o_ref, wt_ref, t_ref, x_ref):
    _, _, v11, _ = tap_masks(frames_ref, first_frame())
    transpose_weights(w_ref, wt_ref)
    activate_features(f0_ref, gain_ref, t_ref, x_ref)
    for row in range(ROWS):
        d = product(wt_ref, 0, 2, x_ref, row)
        o_ref[0, row] = d[:C]
        o_ref[1, row] = v11 * d[C:]
    activate_features(f1_ref, gain_ref, t_ref, x_ref)
    for row in range(ROWS):
        o_ref[1, row] += product(wt_ref, 0, 1, x_ref, row)


def halo_first(
    h_ref, o_ref, wt_ref, gain_ref, gain2_ref, frames_ref, p_ref, s_ref, t_ref, x_ref, g_ref
):
    v01, _, _, v12 = tap_masks(frames_ref, first_frame())
    spread_gain(gain2_ref, g_ref)
    activate_features(h_ref, gain_ref, t_ref, x_ref)
    for row in range(ROWS):
        d = product(wt_ref, 1, 3, x_ref, row)
        p_ref[row] = o_ref[0, row] + v01 * d[:C]
        s_ref[row] = second_activation(o_ref[1, row] + v12 * d[C:], g_ref)


def halo_second(
    h_ref, p_ref, wt_ref, gain_ref, gain2_ref, frames_ref, s_ref, t_ref, x_ref, g_ref
):
    _, v02, _, _ = tap_masks(frames_ref, first_frame())
    spread_gain(gain2_ref, g_ref)
    activate_features(h_ref, gain_ref, t_ref, x_ref)
    for row in range(ROWS):
        d = product(wt_ref, 2, 3, x_ref, row)
        s_ref[row] = second_activation(p_ref[row] + v02 * d, g_ref)


def local_second(s0_ref, s1_ref, w_ref, frames_ref, o_ref, wt_ref, x_ref):
    _, _, v11, _ = tap_masks(frames_ref, first_frame())
    transpose_weights(w_ref, wt_ref)
    slab_of(s0_ref, x_ref)
    for row in range(ROWS):
        d = product(wt_ref, 0, 2, x_ref, row)
        o_ref[0, row] = d[:C]
        o_ref[1, row] = v11 * d[C:]
    slab_of(s1_ref, x_ref)
    for row in range(ROWS):
        o_ref[1, row] += product(wt_ref, 0, 1, x_ref, row)


def last_frame(h_ref, o_ref, wt_ref, f_ref, frames_ref, p_ref, out_ref, t_ref, x_ref):
    v01, _, _, v12 = tap_masks(frames_ref, first_frame())
    slab_of(h_ref, x_ref)
    for row in range(ROWS):
        d = product(wt_ref, 1, 3, x_ref, row)
        p_ref[row] = o_ref[0, row] + v01 * d[:C]
        put_transposed(t_ref, row, o_ref[1, row] + v12 * d[C:])
    to_output(t_ref, f_ref, out_ref)


def other_frame(h_ref, p_ref, wt_ref, f_ref, frames_ref, _, out_ref, t_ref, x_ref):
    _, v02, _, _ = tap_masks(frames_ref, first_frame())
    slab_of(h_ref, x_ref)
    for row in range(ROWS):
        d = product(wt_ref, 2, 3, x_ref, row)
        put_transposed(t_ref, row, p_ref[row] + v02 * d)
    to_output(t_ref, f_ref, out_ref)


VM = pl.BlockSpec(memory_space=pltpu.VMEM)
SM = pl.BlockSpec(memory_space=pltpu.SMEM)
ANY = pl.BlockSpec(memory_space=pl.ANY)
NATURAL = pltpu.VMEM((2, C * ROWS, HALF), F32)
SLABS = pltpu.VMEM(((ROWS + 2) * SLAB, COLS), BF16)
GAINS = pltpu.VMEM((C, COLS), F32)
PAIR = jax.ShapeDtypeStruct((2, ROWS, C, COLS), F32)
ONE = jax.ShapeDtypeStruct((ROWS, C, COLS), F32)
ACT = jax.ShapeDtypeStruct((ROWS, C, COLS), BF16)
TURNED = jax.ShapeDtypeStruct((3 * C, DEPTH), BF16)


def frame(i):
    return pl.BlockSpec((1, C, ROWS, COLS), lambda _: (i, 0, 0, 0))


def call(kernel, in_specs, out_specs, out_shape, scratch, name, aliases=None):
    return pl.pallas_call(
        kernel,
        grid=(1,),
        in_specs=in_specs,
        out_specs=out_specs,
        out_shape=out_shape,
        scratch_shapes=scratch,
        input_output_aliases=aliases or {},
        compiler_params=pltpu.CompilerParams(vmem_limit_bytes=VMEM_LIMIT),
        name=name,
    )


def per_device(features, video_frames, gain_first, conv_first, gain_second, conv_second):
    w1 = conv_first.reshape(3 * DEPTH, C)
    w2 = conv_second.reshape(3 * DEPTH, C)
    whole = jax.ShapeDtypeStruct(features.shape, BF16)
    before = shifted(features[1:], "tm")
    earlier = shifted(features[:1], "tm")

    sums, wt1 = call(
        local_first, [frame(0), frame(1), VM, SM, SM], [VM, VM], [PAIR, TURNED],
        [NATURAL, SLABS], "local_first",
    )(features, features, w1, gain_first, video_frames)
    part, s1 = call(
        halo_first, [VM, VM, VM, SM, SM, SM], [VM, VM], [ONE, ACT],
        [NATURAL, SLABS, GAINS], "halo_first",
    )(before, sums, wt1, gain_first, gain_second, video_frames)
    s_before = shifted(s1, "tm")
    s0 = call(
        halo_second, [VM, VM, VM, SM, SM, SM], VM, ACT,
        [NATURAL, SLABS, GAINS], "halo_second",
    )(earlier, part, wt1, gain_first, gain_second, video_frames)
    s_earlier = shifted(s0, "tm")
    sums2, wt2 = call(
        local_second, [VM, VM, VM, SM], [VM, VM], [PAIR, TURNED],
        [SLABS], "local_second",
    )(s0, s1, w2, video_frames)
    part2, out = call(
        last_frame, [VM, VM, VM, frame(1), SM], [VM, frame(1)], [ONE, whole],
        [NATURAL, SLABS], "last_frame",
    )(s_before, sums2, wt2, features, video_frames)
    return call(
        other_frame, [VM, VM, VM, frame(0), SM, ANY], frame(0), whole,
        [NATURAL, SLABS], "other_frame", {5: 0},
    )(s_earlier, part2, wt2, features, video_frames, out)


def solution(mesh):
    in_specs = (P(("group", "tm"), None, None, None), P("group"), P(), P(), P(), P())
    out_specs = P(("group", "tm"), None, None, None)
    return jax.shard_map(
        per_device, mesh=mesh, in_specs=in_specs, out_specs=out_specs, check_vma=False
    )
```

profile of v0, /device:TPU:0, one launch (start us, length us, event | category | flops | bytes accessed | tf_op | source)
XLA Modules:
  0.0 53.3 jit_solution(12739967407555870210)
XLA Ops:
  0.0 0.0 copy-start
  0.0 0.0 copy-start.1
  0.0 0.0 copy-start.2
  0.0 1.6 %fusion = (bf16[1,192,8,256]{3,2,1,0:T(8,128)(2,1)S(1)}, bf16[1,192,8,256]{3,2,1,0:T(8,128)(2,1)S(1)}) fusion(bf16[2,192,8,256]{3,2,1,0:T(8,128)(2,1)} %f_ref.3), kind=kLoop, calls=%fused_computation | loop fusion | bytes 3145728 | tf_op jit(solution)/shard_map/slice | solution.py:251
  1.6 2.4 %collective-permute-start.1 = (bf16[1,192,8,256]{3,2,1,0:T(8,128)(2,1)S(1)}, bf16[1,192,8,256]{3,2,1,0:T(8,128)(2,1)S(1)}, u32[]{:S(2)}, u32[]{:S(2)}) collective-permute-start(bf16[1,192,8,256]{3,2,1,0:T(8,128)(2,1)S(1)} %get-tuple-element.21), channel_id=1, source_target_pairs={{0,1},{1,2},{2,3},{3,4},{4,5},{5,6},{6,7},{7,8},{8,9},{9,10},{10,1... | collective-permute-start | bytes 2359304 | tf_op jit(solution)/shard_map/ppermute | solution.py:22
  4.0 4.5 %collective-permute-start = (bf16[1,192,8,256]{3,2,1,0:T(8,128)(2,1)S(1)}, bf16[1,192,8,256]{3,2,1,0:T(8,128)(2,1)S(1)}, u32[]{:S(2)}, u32[]{:S(2)}) collective-permute-start(bf16[1,192,8,256]{3,2,1,0:T(8,128)(2,1)S(1)} %get-tuple-element.22), channel_id=1, source_target_pairs={{0,1},{1,2},{2,3},{3,4},{4,5},{5,6},{6,7},{7,8},{8,9},{9,10},{10,1... | collective-permute-start | bytes 2359304 | tf_op jit(solution)/shard_map/ppermute | solution.py:22
  8.5 0.0 copy-done
  8.5 0.0 copy-done.1
  8.6 0.0 copy-done.2
  8.6 0.0 copy-start.3
  8.6 10.6 %local_first.1 = (f32[2,8,192,256]{3,2,1,0:T(8,128)}, bf16[576,1728]{1,0:T(8,128)(2,1)S(1)}) custom-call(bf16[2,192,8,256]{3,2,1,0:T(8,128)(2,1)S(1)} %copy-done, bf16[2,192,8,256]{3,2,1,0:T(8,128)(2,1)S(1)} %copy-done, bf16[5184,192]{1,0:T(8,128)(2,1)} %bitcast.2, f32[192]{0:T(256)S(1)} %copy-done.2, s32[8]{0:T(128)S(1)} %copy-done.1), custom_call_target="tpu_custom_call" | custom-call | tf_op jit(solution)/shard_map/local_first/pallas_call | solution.py:254
  19.2 0.0 collective-permute-done.1.h_ref
  19.2 0.0 copy-done.3
  19.2 6.5 %halo_first.1 = (f32[8,192,256]{2,1,0:T(8,128)S(1)}, bf16[8,192,256]{2,1,0:T(8,128)(2,1)S(1)}) custom-call(bf16[1,192,8,256]{3,2,1,0:T(8,128)(2,1)S(1)} %collective-permute-done.1.h_ref, f32[2,8,192,256]{3,2,1,0:T(8,128)} %get-tuple-element.13.o_ref, bf16[576,1728]{1,0:T(8,128)(2,1)S(1)} %get-tuple-element.14.wt_ref, f32[192]{0:T(256)S(1)} %copy-done.2, ...), custom_call_target="tpu_custom_call" | custom-call | tf_op jit(solution)/shard_map/halo_first/pallas_call | solution.py:258
  25.7 1.9 %collective-permute-start.3 = (bf16[8,192,256]{2,1,0:T(8,128)(2,1)S(1)}, bf16[8,192,256]{2,1,0:T(8,128)(2,1)S(1)}, u32[]{:S(2)}, u32[]{:S(2)}) collective-permute-start(bf16[8,192,256]{2,1,0:T(8,128)(2,1)S(1)} %get-tuple-element.16.s1_ref), channel_id=1, source_target_pairs={{0,1},{1,2},{2,3},{3,4},{4,5},{5,6},{6,7},{7,8},{8,9},{9,10},{10,1... | collective-permute-start | bytes 2359304 | tf_op jit(solution)/shard_map/ppermute | solution.py:22
  27.7 0.0 collective-permute-done.h_ref
  27.7 3.9 %halo_second.1.s0_ref = bf16[8,192,256]{2,1,0:T(8,128)(2,1)S(1)} custom-call(bf16[1,192,8,256]{3,2,1,0:T(8,128)(2,1)S(1)} %collective-permute-done.h_ref, f32[8,192,256]{2,1,0:T(8,128)S(1)} %get-tuple-element.15.p_ref, bf16[576,1728]{1,0:T(8,128)(2,1)S(1)} %get-tuple-element.14.wt_ref, f32[192]{0:T(256)S(1)} %copy-done.2, f32[192]{0:T(256)S(1)} %copy-done.3, ...), custom_call_target="tpu_custom_call" | custom-call | tf_op jit(solution)/shard_map/halo_second/pallas_call | solution.py:263
  31.6 3.7 %collective-permute-start.2 = (bf16[8,192,256]{2,1,0:T(8,128)(2,1)S(1)}, bf16[8,192,256]{2,1,0:T(8,128)(2,1)S(1)}, u32[]{:S(2)}, u32[]{:S(2)}) collective-permute-start(bf16[8,192,256]{2,1,0:T(8,128)(2,1)S(1)} %halo_second.1.s0_ref), channel_id=1, source_target_pairs={{0,1},{1,2},{2,3},{3,4},{4,5},{5,6},{6,7},{7,8},{8,9},{9,10},{10,1... | collective-permute-start | bytes 2359304 | tf_op jit(solution)/shard_map/ppermute | solution.py:22
  35.3 8.1 %local_second.1 = (f32[2,8,192,256]{3,2,1,0:T(8,128)}, bf16[576,1728]{1,0:T(8,128)(2,1)S(1)}) custom-call(bf16[8,192,256]{2,1,0:T(8,128)(2,1)S(1)} %halo_second.1.s0_ref, bf16[8,192,256]{2,1,0:T(8,128)(2,1)S(1)} %get-tuple-element.16.s1_ref, bf16[5184,192]{1,0:T(8,128)(2,1)} %bitcast.3, s32[8]{0:T(128)S(1)} %copy-done.1), custom_call_target="tpu_custom_call" | custom-call | tf_op jit(solution)/shard_map/local_second/pallas_call | solution.py:268
  43.4 0.0 collective-permute-done.3.h_ref
  43.4 6.4 %last_frame.1 = (f32[8,192,256]{2,1,0:T(8,128)S(1)}, bf16[2,192,8,256]{3,2,1,0:T(8,128)(2,1)}) custom-call(bf16[8,192,256]{2,1,0:T(8,128)(2,1)S(1)} %collective-permute-done.3.h_ref, f32[2,8,192,256]{3,2,1,0:T(8,128)} %get-tuple-element.17.o_ref, bf16[576,1728]{1,0:T(8,128)(2,1)S(1)} %get-tuple-element.18.wt_ref, bf16[2,192,8,256]{3,2,1,0:T(8,128)(2,1)S(1)} %copy-done, ...), custom_call_target="tpu_custom_call" | custom-call | tf_op jit(solution)/shard_map/last_frame/pallas_call | solution.py:272
  49.8 0.0 collective-permute-done.2.h_ref
  49.8 3.5 %other_frame.1 = bf16[2,192,8,256]{3,2,1,0:T(8,128)(2,1)} custom-call(bf16[8,192,256]{2,1,0:T(8,128)(2,1)S(1)} %collective-permute-done.2.h_ref, f32[8,192,256]{2,1,0:T(8,128)S(1)} %get-tuple-element.19.p_ref, bf16[576,1728]{1,0:T(8,128)(2,1)S(1)} %get-tuple-element.18.wt_ref, bf16[2,192,8,256]{3,2,1,0:T(8,128)(2,1)S(1)} %copy-done, ...), custom_call_target="tpu_custom_call", output_to_operand_aliasing={{}: (5, {})} | custom-call | tf_op jit(solution)/shard_map/other_frame/pallas_call | solution.py:276
Async XLA Ops:
  0.0 8.5 %copy-start = (bf16[2,192,8,256]{3,2,1,0:T(8,128)(2,1)S(1)}, bf16[2,192,8,256]{3,2,1,0:T(8,128)(2,1)}, u32[]{:S(2)}) copy-start(bf16[2,192,8,256]{3,2,1,0:T(8,128)(2,1)} %f_ref.3) | copy-start | bytes 4718596
  0.0 8.5 %copy-start.1 = (s32[8]{0:T(128)S(1)}, s32[8]{0:T(128)}, u32[]{:S(2)}) copy-start(s32[8]{0:T(128)} %frames_ref.11) | copy-start | bytes 100
  0.0 8.6 %copy-start.2 = (f32[192]{0:T(256)S(1)}, f32[192]{0:T(256)}, u32[]{:S(2)}) copy-start(f32[192]{0:T(256)} %gain_ref.5) | copy-start | bytes 2308
  1.6 17.6 %collective-permute-start.1 = (bf16[1,192,8,256]{3,2,1,0:T(8,128)(2,1)S(1)}, bf16[1,192,8,256]{3,2,1,0:T(8,128)(2,1)S(1)}, u32[]{:S(2)}, u32[]{:S(2)}) collective-permute-start(bf16[1,192,8,256]{3,2,1,0:T(8,128)(2,1)S(1)} %get-tuple-element.21), channel_id=1, source_target_pairs={{0,1},{1,2},{2,3},{3,4},{4,5},{5,6},{6,7},{7,8},{8,9},{9,10},{10,1... | collective-permute-start | bytes 2359304 | tf_op jit(solution)/shard_map/ppermute | solution.py:22
  4.0 23.6 %collective-permute-start = (bf16[1,192,8,256]{3,2,1,0:T(8,128)(2,1)S(1)}, bf16[1,192,8,256]{3,2,1,0:T(8,128)(2,1)S(1)}, u32[]{:S(2)}, u32[]{:S(2)}) collective-permute-start(bf16[1,192,8,256]{3,2,1,0:T(8,128)(2,1)S(1)} %get-tuple-element.22), channel_id=1, source_target_pairs={{0,1},{1,2},{2,3},{3,4},{4,5},{5,6},{6,7},{7,8},{8,9},{9,10},{10,1... | collective-permute-start | bytes 2359304 | tf_op jit(solution)/shard_map/ppermute | solution.py:22
  8.6 10.6 %copy-start.3 = (f32[192]{0:T(256)S(1)}, f32[192]{0:T(256)}, u32[]{:S(2)}) copy-start(f32[192]{0:T(256)} %gain2_ref.3) | copy-start | bytes 2308
  25.7 17.7 %collective-permute-start.3 = (bf16[8,192,256]{2,1,0:T(8,128)(2,1)S(1)}, bf16[8,192,256]{2,1,0:T(8,128)(2,1)S(1)}, u32[]{:S(2)}, u32[]{:S(2)}) collective-permute-start(bf16[8,192,256]{2,1,0:T(8,128)(2,1)S(1)} %get-tuple-element.16.s1_ref), channel_id=1, source_target_pairs={{0,1},{1,2},{2,3},{3,4},{4,5},{5,6},{6,7},{7,8},{8,9},{9,10},{10,1... | collective-permute-start | bytes 2359304 | tf_op jit(solution)/shard_map/ppermute | solution.py:22
  31.6 18.2 %collective-permute-start.2 = (bf16[8,192,256]{2,1,0:T(8,128)(2,1)S(1)}, bf16[8,192,256]{2,1,0:T(8,128)(2,1)S(1)}, u32[]{:S(2)}, u32[]{:S(2)}) collective-permute-start(bf16[8,192,256]{2,1,0:T(8,128)(2,1)S(1)} %halo_second.1.s0_ref), channel_id=1, source_target_pairs={{0,1},{1,2},{2,3},{3,4},{4,5},{5,6},{6,7},{7,8},{8,9},{9,10},{10,1... | collective-permute-start | bytes 2359304 | tf_op jit(solution)/shard_map/ppermute | solution.py:22
where the time goes:
time: 53.6 us; the launch traced here: 53.3 us
  Pallas kernels  39 us (73%)
  starting transfers between devices  12.6 us (24%)
  local copies, waits for them, and re-layouts  1.61 us (3%)
    ppermute x4, starting transfers between devices, shifted(): return lax.ppermute(value, axis, [(i, i + 1) for i in range(count - 1)])  12.6 us
    pallas_call x1, Pallas kernels, per_device(): call(local_first, [frame(0), frame(1), VM, SM, SM], [VM, VM], [PAIR, TURN...  10.6 us
    pallas_call x1, Pallas kernels, per_device(): call(local_second, [VM, VM, VM, SM], [VM, VM], [PAIR, TURNED], [SLABS], '...  8.07 us
    pallas_call x1, Pallas kernels, per_device(): call(halo_first, [VM, VM, VM, SM, SM, SM], [VM, VM], [ONE, ACT], [NATURAL...  6.54 us
    pallas_call x1, Pallas kernels, per_device(): call(last_frame, [VM, VM, VM, frame(1), SM], [VM, frame(1)], [ONE, whole]...  6.39 us
    pallas_call x1, Pallas kernels, per_device(): call(halo_second, [VM, VM, VM, SM, SM, SM], VM, ACT, [NATURAL, SLABS, GAI...  3.9 us
    pallas_call x1, Pallas kernels, per_device(): call(other_frame, [VM, VM, VM, frame(0), SM, ANY], frame(0), whole, [NATU...  3.51 us
    slice x1, local copies, waits for them, and re-layouts, per_device(): before = shifted(features[1:], 'tm')  1.59 us
  transfers between devices with their start and end apart: 4, of which 0 were waited for; matrix products, arithmetic and copies ran while one was open for 0% of the time, Pallas kernels for 67%

commit v1 on v0

v1 whole, which is shorter than its diff:
```python
import jax
import jax.numpy as jnp
from jax import lax
from jax.experimental import pallas as pl
from jax.experimental.pallas import tpu as pltpu
from jax.sharding import PartitionSpec as P

C = 192
ROWS = 8
COLS = 256
HALF = 128
TAPS = 3
SLAB = 3 * C
DEPTH = 9 * C
PIECE = 384
PARTS = 4
EPS = 1e-06
VMEM_LIMIT = 16 * 1024 * 1024
F32 = jnp.float32
BF16 = jnp.bfloat16


def shifted(value, axis):
    count = lax.axis_size(axis)
    return lax.ppermute(value, axis, [(i, i + 1) for i in range(count - 1)])


def tap_masks(frames_ref):
    first = 2 * lax.axis_index("tm")

    def step(v, carry):
        begin, start0, start1 = carry
        start0 = jnp.where(begin <= first, begin, start0)
        start1 = jnp.where(begin <= first + 1, begin, start1)
        return begin + frames_ref[v], start0, start1

    zero = jnp.int32(0)
    _, start0, start1 = lax.fori_loop(0, frames_ref.shape[0], step, (zero, zero, zero))
    return tuple(
        jnp.where(test, 1.0, 0.0).astype(F32)
        for test in (
            first - 1 >= start0,
            first - 2 >= start0,
            first >= start1,
            first - 1 >= start1,
        )
    )


def turn_pieces(w_ref, wt_ref, taps):
    def turn(k, lo, hi):
        wt_ref[k * C : (k + 1) * C, lo:hi] = w_ref[k * DEPTH + lo : k * DEPTH + hi, :].T

    return [
        (lambda k=k, lo=lo: turn(k, lo, min(lo + PIECE, DEPTH)))
        for k in taps
        for lo in range(0, DEPTH, PIECE)
    ]


def put_row(x_ref, row, values):
    base = (row + 1) * SLAB
    cols = lax.broadcasted_iota(jnp.int32, (C, COLS), 1)
    left = jnp.where(cols == 0, 0.0, pltpu.roll(values, 1, 1))
    right = jnp.where(cols == COLS - 1, 0.0, pltpu.roll(values, COLS - 1, 1))
    x_ref[base : base + C, :] = left.astype(BF16)
    x_ref[base + C : base + 2 * C, :] = values.astype(BF16)
    x_ref[base + 2 * C : base + 3 * C, :] = right.astype(BF16)


def clear_edges(x_ref):
    zeros = jnp.zeros((SLAB, COLS), BF16)
    x_ref[0:SLAB, :] = zeros
    x_ref[(ROWS + 1) * SLAB : (ROWS + 2) * SLAB, :] = zeros


def put(x_ref, a_ref, row):
    if row < ROWS:
        put_row(x_ref, row, a_ref[row].astype(F32))


def product(wt_ref, lo, hi, x_ref, row):
    return jnp.dot(
        wt_ref[lo * C : hi * C, :],
        x_ref[row * SLAB : row * SLAB + DEPTH, :],
        preferred_element_type=F32,
    )


def activation(index):
    def kernel(f_ref, gain_ref, a_ref, t_ref):
        def squares(b, total):
            v = f_ref[index, pl.ds(b * 16, 16)].astype(F32)
            return total + jnp.sum(v * v, axis=0)

        total = lax.fori_loop(0, C // 16, squares, jnp.zeros((ROWS, COLS), F32))
        inverse = lax.rsqrt(total * (1.0 / C) + EPS)

        def act(b, _):
            for j in range(16):
                c = b * 16 + j
                u = f_ref[index, c].astype(F32) * inverse * gain_ref[c]
                u = u * jax.nn.sigmoid(u)
                at = pl.multiple_of(c * ROWS, ROWS)
                t_ref[0, pl.ds(at, ROWS), :] = u[:, :HALF]
                t_ref[1, pl.ds(at, ROWS), :] = u[:, HALF:]
            return 0

        lax.fori_loop(0, C // 16, act, 0)
        for row in range(ROWS):
            for h in range(2):
                a_ref[row, :, h * HALF : (h + 1) * HALF] = t_ref[
                    h, pl.ds(row, C, stride=ROWS), :
                ].astype(BF16)

    return kernel


def spread_gain(gain_ref, g_ref):
    def step(b, _):
        for j in range(8):
            c = b * 8 + j
            g_ref[pl.ds(c, 1), :] = jnp.full((1, COLS), gain_ref[c], F32)
        return 0

    lax.fori_loop(0, C // 8, step, 0)


def second_activation(values, g_ref):
    mean_square = jnp.sum(values * values, axis=0, keepdims=True) * (1.0 / C)
    u = values * lax.rsqrt(mean_square + EPS) * g_ref[...]
    return (u * jax.nn.sigmoid(u)).astype(BF16)


def put_transposed(t_ref, row, values):
    t_ref[0, pl.ds(row, C, stride=ROWS), :] = values[:, :HALF]
    t_ref[1, pl.ds(row, C, stride=ROWS), :] = values[:, HALF:]


def write_frame(index, t_ref, f_ref, buf_ref, out_ref, sems):
    step = C // PARTS

    def piece(p):
        span = pl.ds(p * step, step)
        return pltpu.make_async_copy(buf_ref.at[span], out_ref.at[index, span], sems.at[p])

    for p in range(PARTS):

        def add(b, _):
            for j in range(16):
                c = p * step + b * 16 + j
                at = pl.multiple_of(c * ROWS, ROWS)
                v = jnp.concatenate([t_ref[h, pl.ds(at, ROWS), :] for h in range(2)], axis=1)
                buf_ref[c] = (f_ref[index, c].astype(F32) + v).astype(BF16)
            return 0

        lax.fori_loop(0, step // 16, add, 0)
        piece(p).start()
    for p in range(PARTS):
        piece(p).wait()


def both_frames(a0_ref, a1_ref, v11, wt_ref, o0_ref, o1_ref, x0_ref, x1_ref, extra):
    clear_edges(x0_ref)
    clear_edges(x1_ref)
    put(x0_ref, a0_ref, 0)
    put(x0_ref, a0_ref, 1)
    extra = list(extra)
    share = -(-len(extra) // ROWS)
    for row in range(ROWS):
        d = product(wt_ref, 0, 2, x0_ref, row)
        put(x0_ref, a0_ref, row + 2)
        put(x1_ref, a1_ref, row)
        for step in extra[row * share : (row + 1) * share]:
            step()
        o0_ref[row] = d[:C]
        o1_ref[row] = v11 * d[C:]
    for row in range(ROWS):
        o1_ref[row] += product(wt_ref, 0, 1, x1_ref, row)


def local_first(
    a0_ref, a1_ref, w1_ref, w2_ref, frames_ref, o0_ref, o1_ref, wt1_ref, wt2_ref, x0_ref, x1_ref
):
    _, _, v11, _ = tap_masks(frames_ref)
    for step in turn_pieces(w1_ref, wt1_ref, (0, 1)):
        step()
    later = turn_pieces(w1_ref, wt1_ref, (2,)) + turn_pieces(w2_ref, wt2_ref, (0, 1, 2))
    both_frames(a0_ref, a1_ref, v11, wt1_ref, o0_ref, o1_ref, x0_ref, x1_ref, later)


def local_second(a0_ref, a1_ref, wt_ref, frames_ref, o0_ref, o1_ref, x0_ref, x1_ref):
    _, _, v11, _ = tap_masks(frames_ref)
    both_frames(a0_ref, a1_ref, v11, wt_ref, o0_ref, o1_ref, x0_ref, x1_ref, ())


def halo_first(h_ref, o0_ref, o1_ref, wt_ref, gain_ref, frames_ref, p_ref, s_ref, x_ref, g_ref):
    v01, _, _, v12 = tap_masks(frames_ref)
    spread_gain(gain_ref, g_ref)
    clear_edges(x_ref)
    put(x_ref, h_ref, 0)
    put(x_ref, h_ref, 1)
    for row in range(ROWS):
        d = product(wt_ref, 1, 3, x_ref, row)
        put(x_ref, h_ref, row + 2)
        p_ref[row] = o0_ref[row] + v01 * d[:C]
        s_ref[row] = second_activation(o1_ref[row] + v12 * d[C:], g_ref)


def halo_second(h_ref, p_ref, wt_ref, gain_ref, frames_ref, s_ref, x_ref, g_ref):
    _, v02, _, _ = tap_masks(frames_ref)
    spread_gain(gain_ref, g_ref)
    clear_edges(x_ref)
    put(x_ref, h_ref, 0)
    put(x_ref, h_ref, 1)
    for row in range(ROWS):
        d = product(wt_ref, 2, 3, x_ref, row)
        put(x_ref, h_ref, row + 2)
        s_ref[row] = second_activation(p_ref[row] + v02 * d, g_ref)


def last_frame(
    h_ref, o0_ref, o1_ref, wt_ref, f_ref, frames_ref, p_ref, out_ref, t_ref, x_ref, buf_ref, sems
):
    v01, _, _, v12 = tap_masks(frames_ref)
    clear_edges(x_ref)
    put(x_ref, h_ref, 0)
    put(x_ref, h_ref, 1)
    for row in range(ROWS):
        d = product(wt_ref, 1, 3, x_ref, row)
        put(x_ref, h_ref, row + 2)
        p_ref[row] = o0_ref[row] + v01 * d[:C]
        put_transposed(t_ref, row, o1_ref[row] + v12 * d[C:])
    write_frame(1, t_ref, f_ref, buf_ref, out_ref, sems)


def other_frame(
    h_ref, p_ref, wt_ref, f_ref, frames_ref, _, out_ref, t_ref, x_ref, buf_ref, sems
):
    _, v02, _, _ = tap_masks(frames_ref)
    clear_edges(x_ref)
    put(x_ref, h_ref, 0)
    put(x_ref, h_ref, 1)
    for row in range(ROWS):
        d = product(wt_ref, 2, 3, x_ref, row)
        put(x_ref, h_ref, row + 2)
        put_transposed(t_ref, row, p_ref[row] + v02 * d)
    write_frame(0, t_ref, f_ref, buf_ref, out_ref, sems)


VM = pl.BlockSpec(memory_space=pltpu.VMEM)
SM = pl.BlockSpec(memory_space=pltpu.SMEM)
ANY = pl.BlockSpec(memory_space=pl.ANY)
NATURAL = pltpu.VMEM((2, C * ROWS, HALF), F32)
SLABS = pltpu.VMEM(((ROWS + 2) * SLAB, COLS), BF16)
GAINS = pltpu.VMEM((C, COLS), F32)
FRAME = pltpu.VMEM((C, ROWS, COLS), BF16)
SEMS = pltpu.SemaphoreType.DMA((PARTS,))
SUM = jax.ShapeDtypeStruct((ROWS, C, COLS), F32)
ACT = jax.ShapeDtypeStruct((ROWS, C, COLS), BF16)
TURNED = jax.ShapeDtypeStruct((TAPS * C, DEPTH), BF16)


def call(kernel, in_specs, out_specs, out_shape, scratch, name, aliases=None):
    return pl.pallas_call(
        kernel,
        in_specs=in_specs,
        out_specs=out_specs,
        out_shape=out_shape,
        scratch_shapes=scratch,
        input_output_aliases=aliases or {},
        compiler_params=pltpu.CompilerParams(vmem_limit_bytes=VMEM_LIMIT),
        name=name,
    )


def per_device(features, video_frames, gain_first, conv_first, gain_second, conv_second):
    w1 = conv_first.reshape(TAPS * DEPTH, C)
    w2 = conv_second.reshape(TAPS * DEPTH, C)
    whole = jax.ShapeDtypeStruct(features.shape, BF16)

    a1, a0 = (
        call(activation(i), [VM, SM], VM, ACT, [NATURAL], f"activation_{i}")(features, gain_first)
        for i in (1, 0)
    )
    a_before = shifted(a1, "tm")
    a_earlier = shifted(a0, "tm")
    o0, o1, wt1, wt2 = call(
        local_first, [VM] * 4 + [SM], [VM] * 4, [SUM, SUM, TURNED, TURNED],
        [SLABS, SLABS], "local_first",
    )(a0, a1, w1, w2, video_frames)
    part, s1 = call(
        halo_first, [VM] * 4 + [SM, SM], [VM, VM], [SUM, ACT], [SLABS, GAINS], "halo_first",
    )(a_before, o0, o1, wt1, gain_second, video_frames)
    s_before = shifted(s1, "tm")
    s0 = call(
        halo_second, [VM] * 3 + [SM, SM], VM, ACT, [SLABS, GAINS], "halo_second",
    )(a_earlier, part, wt1, gain_second, video_frames)
    s_earlier = shifted(s0, "tm")
    q0, q1 = call(
        local_second, [VM] * 3 + [SM], [VM] * 2, [SUM, SUM], [SLABS, SLABS], "local_second",
    )(s0, s1, wt2, video_frames)
    part2, out = call(
        last_frame, [VM] * 5 + [SM], [VM, ANY], [SUM, whole],
        [NATURAL, SLABS, FRAME, SEMS], "last_frame",
    )(s_before, q0, q1, wt2, features, video_frames)
    return call(
        other_frame, [VM] * 4 + [SM, ANY], ANY, whole,
        [NATURAL, SLABS, FRAME, SEMS], "other_frame", {5: 0},
    )(s_earlier, part2, wt2, features, video_frames, out)


def solution(mesh):
    in_specs = (P(("group", "tm"), None, None, None), P("group"), P(), P(), P(), P())
    out_specs = P(("group", "tm"), None, None, None)
    return jax.shard_map(
        per_device, mesh=mesh, in_specs=in_specs, out_specs=out_specs, check_vma=False
    )
```

time: 53.6 us -> 48.6 us (0.907)
  the two profiles are of different devices: /device:TPU:0 before, /device:TPU:8 now
where the time goes in v1:
time: 48.6 us; the launch traced here: 48.4 us
  Pallas kernels  29.1 us (60%)
  starting transfers between devices  9.44 us (19%)
  waiting for transfers between devices  5.7 us (12%)
  local copies, waits for them, and re-layouts  3.85 us (8%)
    ppermute x4, starting transfers between devices, shifted(): return lax.ppermute(value, axis, [(i, i + 1) for i in range(count - 1)])  9.44 us
    ppermute x4, waiting for transfers between devices, shifted(): return lax.ppermute(value, axis, [(i, i + 1) for i in range(count - 1)])  5.7 us
    pallas_call x1, Pallas kernels, per_device(): call(local_first, [VM] * 4 + [SM], [VM] * 4, [SUM, SUM, TURNED, TURNED],...  5.32 us
    pallas_call x1, Pallas kernels, per_device(): call(local_second, [VM] * 3 + [SM], [VM] * 2, [SUM, SUM], [SLABS, SLABS],...  5.19 us
    pallas_call x1, Pallas kernels, per_device(): call(last_frame, [VM] * 5 + [SM], [VM, ANY], [SUM, whole], [NATURAL, SLAB...  4.82 us
    pallas_call x1, Pallas kernels, per_device(): call(halo_first, [VM] * 4 + [SM, SM], [VM, VM], [SUM, ACT], [SLABS, GAINS...  4.37 us
    unnamed x14, local copies, waits for them, and re-layouts  3.85 us
    pallas_call x1, Pallas kernels, per_device(): call(other_frame, [VM] * 4 + [SM, ANY], ANY, whole, [NATURAL, SLABS, FRAM...  3.35 us
  transfers between devices with their start and end apart: 4, of which 3 were waited for; matrix products, arithmetic and copies ran while one was open for 0% of the time, Pallas kernels for 50%

profile of v1, /device:TPU:8, one launch (start us, length us, event | category | flops | bytes accessed | tf_op | source)
XLA Modules:
  0.0 48.4 jit_solution(1132549593962337106)
XLA Ops:
  0.0 1.4 %copy-done = bf16[2,192,8,256]{3,2,1,0:T(8,128)(2,1)S(1)} copy-done((bf16[2,192,8,256]{3,2,1,0:T(8,128)(2,1)S(1)}, bf16[2,192,8,256]{3,2,1,0:T(8,128)(2,1)}, u32[]{:S(2)}) %copy-start) | copy-done | bytes 1572888
  1.4 0.7 %copy-done.5 = f32[192]{0:T(256)S(1)} copy-done((f32[192]{0:T(256)S(1)}, f32[192]{0:T(256)}, u32[]{:S(2)}) %copy-start.5) | copy-done | bytes 792
  2.1 1.5 %activation_1.1.a1_ref = bf16[8,192,256]{2,1,0:T(8,128)(2,1)S(1)} custom-call(bf16[2,192,8,256]{3,2,1,0:T(8,128)(2,1)S(1)} %copy-done, f32[192]{0:T(256)S(1)} %copy-done.5), custom_call_target="tpu_custom_call" | custom-call | tf_op jit(solution)/shard_map/activation_1/pallas_call | solution.py:283
  3.6 0.0 copy-start.4
  3.6 1.9 %collective-permute-start.1 = (bf16[8,192,256]{2,1,0:T(8,128)(2,1)S(1)}, bf16[8,192,256]{2,1,0:T(8,128)(2,1)S(1)}, u32[]{:S(2)}, u32[]{:S(2)}) collective-permute-start(bf16[8,192,256]{2,1,0:T(8,128)(2,1)S(1)} %activation_1.1.a1_ref), channel_id=1, source_target_pairs={{0,1},{1,2},{2,3},{3,4},{4,5},{5,6},{6,7},{7,8},{8,9},{9,10},{10,1... | collective-permute-start | bytes 2359304 | tf_op jit(solution)/shard_map/ppermute | solution.py:25
  5.6 1.5 %activation_0.1.a0_ref = bf16[8,192,256]{2,1,0:T(8,128)(2,1)S(1)} custom-call(bf16[2,192,8,256]{3,2,1,0:T(8,128)(2,1)S(1)} %copy-done, f32[192]{0:T(256)S(1)} %copy-done.5), custom_call_target="tpu_custom_call" | custom-call | tf_op jit(solution)/shard_map/activation_0/pallas_call | solution.py:283
  7.1 3.5 %collective-permute-start = (bf16[8,192,256]{2,1,0:T(8,128)(2,1)S(1)}, bf16[8,192,256]{2,1,0:T(8,128)(2,1)S(1)}, u32[]{:S(2)}, u32[]{:S(2)}) collective-permute-start(bf16[8,192,256]{2,1,0:T(8,128)(2,1)S(1)} %activation_0.1.a0_ref), channel_id=1, source_target_pairs={{0,1},{1,2},{2,3},{3,4},{4,5},{5,6},{6,7},{7,8},{8,9},{9,10},{10,1... | collective-permute-start | bytes 2359304 | tf_op jit(solution)/shard_map/ppermute | solution.py:25
  10.6 0.0 copy-done.2
  10.6 0.0 copy-done.4
  10.6 0.0 copy-start.3
  10.6 1.7 %copy-done.3 = bf16[3,3,3,192,192]{4,3,2,1,0:T(8,128)(2,1)S(1)} copy-done((bf16[3,3,3,192,192]{4,3,2,1,0:T(8,128)(2,1)S(1)}, bf16[3,3,3,192,192]{4,3,2,1,0:T(8,128)(2,1)}, u32[]{:S(2)}) %copy-start.3) | copy-done | bytes 1990680
  12.4 5.3 %local_first.1 = (f32[8,192,256]{2,1,0:T(8,128)S(1)}, f32[8,192,256]{2,1,0:T(8,128)S(1)}, bf16[576,1728]{1,0:T(8,128)(2,1)S(1)}, bf16[576,1728]{1,0:T(8,128)(2,1)S(1)}) custom-call(bf16[8,192,256]{2,1,0:T(8,128)(2,1)S(1)} %activation_0.1.a0_ref, bf16[8,192,256]{2,1,0:T(8,128)(2,1)S(1)} %activation_1.1.a1_ref, bf16[5184,192]{1,0:T(8,128)(2,1)S(1)} %bitcast.2, ...), custom_call_target="tpu_custom_call" | custom-call | tf_op jit(solution)/shard_map/local_first/pallas_call | solution.py:288
  17.7 0.1 collective-permute-done.1.h_ref
  17.9 4.4 %halo_first.1 = (f32[8,192,256]{2,1,0:T(8,128)S(1)}, bf16[8,192,256]{2,1,0:T(8,128)(2,1)S(1)}) custom-call(bf16[8,192,256]{2,1,0:T(8,128)(2,1)S(1)} %collective-permute-done.1.h_ref, f32[8,192,256]{2,1,0:T(8,128)S(1)} %get-tuple-element.15.o0_ref, f32[8,192,256]{2,1,0:T(8,128)S(1)} %get-tuple-element.16.o1_ref, ...), custom_call_target="tpu_custom_call" | custom-call | tf_op jit(solution)/shard_map/halo_first/pallas_call | solution.py:292
  22.2 1.9 %collective-permute-start.3 = (bf16[8,192,256]{2,1,0:T(8,128)(2,1)S(1)}, bf16[8,192,256]{2,1,0:T(8,128)(2,1)S(1)}, u32[]{:S(2)}, u32[]{:S(2)}) collective-permute-start(bf16[8,192,256]{2,1,0:T(8,128)(2,1)S(1)} %get-tuple-element.19.a1_ref), channel_id=1, source_target_pairs={{0,1},{1,2},{2,3},{3,4},{4,5},{5,6},{6,7},{7,8},{8,9},{9,10},{10,1... | collective-permute-start | bytes 2359304 | tf_op jit(solution)/shard_map/ppermute | solution.py:25
  24.2 2.1 %collective-permute-done.h_ref = bf16[8,192,256]{2,1,0:T(8,128)(2,1)S(1)} collective-permute-done((bf16[8,192,256]{2,1,0:T(8,128)(2,1)S(1)}, bf16[8,192,256]{2,1,0:T(8,128)(2,1)S(1)}, u32[]{:S(2)}, u32[]{:S(2)}) %collective-permute-start) | collective-permute-done | bytes 786464 | tf_op jit(solution)/shard_map/ppermute | solution.py:25
  26.3 3.0 %halo_second.1.a0_ref = bf16[8,192,256]{2,1,0:T(8,128)(2,1)S(1)} custom-call(bf16[8,192,256]{2,1,0:T(8,128)(2,1)S(1)} %collective-permute-done.h_ref, f32[8,192,256]{2,1,0:T(8,128)S(1)} %get-tuple-element.18.p_ref, bf16[576,1728]{1,0:T(8,128)(2,1)S(1)} %get-tuple-element.17.wt_ref, f32[192]{0:T(256)S(1)} %copy-done.6, s32[8]{0:T(128)S(1)} %copy-done.4), custom_call_target="tpu_custom_call" | custom-call | tf_op jit(solution)/shard_map/halo_second/pallas_call | solution.py:296
  29.2 2.1 %collective-permute-start.2 = (bf16[8,192,256]{2,1,0:T(8,128)(2,1)S(1)}, bf16[8,192,256]{2,1,0:T(8,128)(2,1)S(1)}, u32[]{:S(2)}, u32[]{:S(2)}) collective-permute-start(bf16[8,192,256]{2,1,0:T(8,128)(2,1)S(1)} %halo_second.1.a0_ref), channel_id=1, source_target_pairs={{0,1},{1,2},{2,3},{3,4},{4,5},{5,6},{6,7},{7,8},{8,9},{9,10},{10,1... | collective-permute-start | bytes 2359304 | tf_op jit(solution)/shard_map/ppermute | solution.py:25
  31.4 0.0 copy-start.1
  31.4 5.2 %local_second.1 = (f32[8,192,256]{2,1,0:T(8,128)S(1)}, f32[8,192,256]{2,1,0:T(8,128)S(1)}) custom-call(bf16[8,192,256]{2,1,0:T(8,128)(2,1)S(1)} %halo_second.1.a0_ref, bf16[8,192,256]{2,1,0:T(8,128)(2,1)S(1)} %get-tuple-element.19.a1_ref, bf16[576,1728]{1,0:T(8,128)(2,1)S(1)} %get-tuple-element.20.wt_ref, s32[8]{0:T(128)S(1)} %copy-done.4), custom_call_target="tpu_custom_call" | custom-call | tf_op jit(solution)/shard_map/local_second/pallas_call | solution.py:300
  36.6 0.0 collective-permute-done.3.h_ref
  36.6 4.8 %last_frame.1 = (f32[8,192,256]{2,1,0:T(8,128)S(1)}, bf16[2,192,8,256]{3,2,1,0:T(8,128)(2,1)}) custom-call(bf16[8,192,256]{2,1,0:T(8,128)(2,1)S(1)} %collective-permute-done.3.h_ref, f32[8,192,256]{2,1,0:T(8,128)S(1)} %get-tuple-element.21.o0_ref, f32[8,192,256]{2,1,0:T(8,128)S(1)} %get-tuple-element.22.o1_ref, ...), custom_call_target="tpu_custom_call" | custom-call | tf_op jit(solution)/shard_map/last_frame/pallas_call | solution.py:303
  41.4 3.5 %collective-permute-done.2.h_ref = bf16[8,192,256]{2,1,0:T(8,128)(2,1)S(1)} collective-permute-done((bf16[8,192,256]{2,1,0:T(8,128)(2,1)S(1)}, bf16[8,192,256]{2,1,0:T(8,128)(2,1)S(1)}, u32[]{:S(2)}, u32[]{:S(2)}) %collective-permute-start.2) | collective-permute-done | bytes 786464 | tf_op jit(solution)/shard_map/ppermute | solution.py:25
  44.9 3.3 %other_frame.1 = bf16[2,192,8,256]{3,2,1,0:T(8,128)(2,1)} custom-call(bf16[8,192,256]{2,1,0:T(8,128)(2,1)S(1)} %collective-permute-done.2.h_ref, f32[8,192,256]{2,1,0:T(8,128)S(1)} %get-tuple-element.23.p_ref, bf16[576,1728]{1,0:T(8,128)(2,1)S(1)} %get-tuple-element.20.wt_ref, ...), custom_call_target="tpu_custom_call", output_to_operand_aliasing={{}: (5, {})} | custom-call | tf_op jit(solution)/shard_map/other_frame/pallas_call | solution.py:307
  (6 shorter events, 0.0 us)
Async XLA Ops:
  0.0 1.4 %copy-start = (bf16[2,192,8,256]{3,2,1,0:T(8,128)(2,1)S(1)}, bf16[2,192,8,256]{3,2,1,0:T(8,128)(2,1)}, u32[]{:S(2)}) copy-start(bf16[2,192,8,256]{3,2,1,0:T(8,128)(2,1)} %f_ref.7) | copy-start | bytes 4718596
  1.4 0.7 %copy-start.5 = (f32[192]{0:T(256)S(1)}, f32[192]{0:T(256)}, u32[]{:S(2)}) copy-start(f32[192]{0:T(256)} %gain_ref.5) | copy-start | bytes 2308
  2.1 8.5 %copy-start.2 = (bf16[3,3,3,192,192]{4,3,2,1,0:T(8,128)(2,1)S(1)}, bf16[3,3,3,192,192]{4,3,2,1,0:T(8,128)(2,1)}, u32[]{:S(2)}) copy-start(bf16[3,3,3,192,192]{4,3,2,1,0:T(8,128)(2,1)} %param.9) | copy-start | bytes 5971972
  3.6 7.0 %copy-start.4 = (s32[8]{0:T(128)S(1)}, s32[8]{0:T(128)}, u32[]{:S(2)}) copy-start(s32[8]{0:T(128)} %frames_ref.11) | copy-start | bytes 100
  3.6 14.2 %collective-permute-start.1 = (bf16[8,192,256]{2,1,0:T(8,128)(2,1)S(1)}, bf16[8,192,256]{2,1,0:T(8,128)(2,1)S(1)}, u32[]{:S(2)}, u32[]{:S(2)}) collective-permute-start(bf16[8,192,256]{2,1,0:T(8,128)(2,1)S(1)} %activation_1.1.a1_ref), channel_id=1, source_target_pairs={{0,1},{1,2},{2,3},{3,4},{4,5},{5,6},{6,7},{7,8},{8,9},{9,10},{10,1... | collective-permute-start | bytes 2359304 | tf_op jit(solution)/shard_map/ppermute | solution.py:25
  7.1 19.2 %collective-permute-start = (bf16[8,192,256]{2,1,0:T(8,128)(2,1)S(1)}, bf16[8,192,256]{2,1,0:T(8,128)(2,1)S(1)}, u32[]{:S(2)}, u32[]{:S(2)}) collective-permute-start(bf16[8,192,256]{2,1,0:T(8,128)(2,1)S(1)} %activation_0.1.a0_ref), channel_id=1, source_target_pairs={{0,1},{1,2},{2,3},{3,4},{4,5},{5,6},{6,7},{7,8},{8,9},{9,10},{10,1... | collective-permute-start | bytes 2359304 | tf_op jit(solution)/shard_map/ppermute | solution.py:25
  10.6 1.8 %copy-start.3 = (bf16[3,3,3,192,192]{4,3,2,1,0:T(8,128)(2,1)S(1)}, bf16[3,3,3,192,192]{4,3,2,1,0:T(8,128)(2,1)}, u32[]{:S(2)}) copy-start(bf16[3,3,3,192,192]{4,3,2,1,0:T(8,128)(2,1)} %param.11) | copy-start | bytes 5971972
  12.4 5.5 %copy-start.6 = (f32[192]{0:T(256)S(1)}, f32[192]{0:T(256)}, u32[]{:S(2)}) copy-start(f32[192]{0:T(256)} %gain_ref.7) | copy-start | bytes 2308
  22.2 14.3 %collective-permute-start.3 = (bf16[8,192,256]{2,1,0:T(8,128)(2,1)S(1)}, bf16[8,192,256]{2,1,0:T(8,128)(2,1)S(1)}, u32[]{:S(2)}, u32[]{:S(2)}) collective-permute-start(bf16[8,192,256]{2,1,0:T(8,128)(2,1)S(1)} %get-tuple-element.19.a1_ref), channel_id=1, source_target_pairs={{0,1},{1,2},{2,3},{3,4},{4,5},{5,6},{6,7},{7,8},{8,9},{9,10},{10,1... | collective-permute-start | bytes 2359304 | tf_op jit(solution)/shard_map/ppermute | solution.py:25
  29.2 15.6 %collective-permute-start.2 = (bf16[8,192,256]{2,1,0:T(8,128)(2,1)S(1)}, bf16[8,192,256]{2,1,0:T(8,128)(2,1)S(1)}, u32[]{:S(2)}, u32[]{:S(2)}) collective-permute-start(bf16[8,192,256]{2,1,0:T(8,128)(2,1)S(1)} %halo_second.1.a0_ref), channel_id=1, source_target_pairs={{0,1},{1,2},{2,3},{3,4},{4,5},{5,6},{6,7},{7,8},{8,9},{9,10},{10,1... | collective-permute-start | bytes 2359304 | tf_op jit(solution)/shard_map/ppermute | solution.py:25
  31.4 5.2 %copy-start.1 = (bf16[2,192,8,256]{3,2,1,0:T(8,128)(2,1)S(1)}, bf16[2,192,8,256]{3,2,1,0:T(8,128)(2,1)}, u32[]{:S(2)}) copy-start(bf16[2,192,8,256]{3,2,1,0:T(8,128)(2,1)} %f_ref.7) | copy-start | bytes 4718596

commit v2 on v1

--- a/solution.py
+++ b/solution.py
@@ -88,27 +88,44 @@
 
 
 def activation(index):
-    def kernel(f_ref, gain_ref, a_ref, t_ref):
-        def squares(b, total):
-            v = f_ref[index, pl.ds(b * 16, 16)].astype(F32)
-            return total + jnp.sum(v * v, axis=0)
-
-        total = lax.fori_loop(0, C // 16, squares, jnp.zeros((ROWS, COLS), F32))
-        inverse = lax.rsqrt(total * (1.0 / C) + EPS)
-
-        def act(b, _):
-            for j in range(16):
-                c = b * 16 + j
-                u = f_ref[index, c].astype(F32) * inverse * gain_ref[c]
-                u = u * jax.nn.sigmoid(u)
-                at = pl.multiple_of(c * ROWS, ROWS)
-                t_ref[0, pl.ds(at, ROWS), :] = u[:, :HALF]
-                t_ref[1, pl.ds(at, ROWS), :] = u[:, HALF:]
-            return 0
-
-        lax.fori_loop(0, C // 16, act, 0)
-        for row in range(ROWS):
-            for h in range(2):
+    def kernel(f_ref, gain_any, a_ref, raw_ref, gain_ref, t_ref, sems):
+        copies = [
+            pltpu.make_async_copy(
+                f_ref.at[index, pl.ds(q * C // 2, C // 2), :, pl.ds(h * HALF, HALF)],
+                raw_ref.at[h, pl.ds(q * C // 2, C // 2)],
+                sems.at[2 * h + q],
+            )
+            for h in range(2)
+            for q in range(2)
+        ]
+        gains = pltpu.make_async_copy(gain_any, gain_ref, sems.at[4])
+        copies[0].start()
+        copies[1].start()
+        gains.start()
+        copies[2].start()
+        copies[3].start()
+        for h in range(2):
+            copies[2 * h].wait()
+            copies[2 * h + 1].wait()
+
+            def squares(b, total):
+                v = raw_ref[h, pl.ds(b * 16, 16)].astype(F32)
+                return total + jnp.sum(v * v, axis=0)
+
+            total = lax.fori_loop(0, C // 16, squares, jnp.zeros((ROWS, HALF), F32))
+            inverse = lax.rsqrt(total * (1.0 / C) + EPS)
+            if h == 0:
+                gains.wait()
+
+            def act(b, _):
+                for j in range(16):
+                    c = b * 16 + j
+                    u = raw_ref[h, c].astype(F32) * inverse * gain_ref[c]
+                    t_ref[h, pl.ds(pl.multiple_of(c * ROWS, ROWS), ROWS), :] = u * jax.nn.sigmoid(u)
+                return 0
+
+            lax.fori_loop(0, C // 16, act, 0)
+            for row in range(ROWS):
                 a_ref[row, :, h * HALF : (h + 1) * HALF] = t_ref[
                     h, pl.ds(row, C, stride=ROWS), :
                 ].astype(BF16)
@@ -165,46 +182,70 @@
     clear_edges(x1_ref)
     put(x0_ref, a0_ref, 0)
     put(x0_ref, a0_ref, 1)
-    extra = list(extra)
-    share = -(-len(extra) // ROWS)
     for row in range(ROWS):
         d = product(wt_ref, 0, 2, x0_ref, row)
         put(x0_ref, a0_ref, row + 2)
         put(x1_ref, a1_ref, row)
-        for step in extra[row * share : (row + 1) * share]:
+        for step in extra.get(row, ()):
             step()
         o0_ref[row] = d[:C]
         o1_ref[row] = v11 * d[C:]
     for row in range(ROWS):
-        o1_ref[row] += product(wt_ref, 0, 1, x1_ref, row)
+        d = product(wt_ref, 0, 1, x1_ref, row)
+        for step in extra.get(ROWS + row, ()):
+            step()
+        o1_ref[row] += d
 
 
 def local_first(
-    a0_ref, a1_ref, w1_ref, w2_ref, frames_ref, o0_ref, o1_ref, wt1_ref, wt2_ref, x0_ref, x1_ref
+    a0_ref, a1_ref, w1_ref, w2_any, frames_ref,
+    o0_ref, o1_ref, wt1_ref, wt2_ref, x0_ref, x1_ref, w2_ref, sems,
 ):
+    third = TAPS * DEPTH // 3
+    loads = [
+        pltpu.make_async_copy(
+            w2_any.at[pl.ds(k * third, third)], w2_ref.at[pl.ds(k * third, third)], sems.at[k]
+        )
+        for k in range(3)
+    ]
+    for load in loads:
+        load.start()
     _, _, v11, _ = tap_masks(frames_ref)
     for step in turn_pieces(w1_ref, wt1_ref, (0, 1)):
         step()
-    later = turn_pieces(w1_ref, wt1_ref, (2,)) + turn_pieces(w2_ref, wt2_ref, (0, 1, 2))
-    both_frames(a0_ref, a1_ref, v11, wt1_ref, o0_ref, o1_ref, x0_ref, x1_ref, later)
+    extra = {i: [step] for i, step in enumerate(turn_pieces(w1_ref, wt1_ref, (2,)))}
+    later = turn_pieces(w2_ref, wt2_ref, (0, 1, 2))
+    first = len(extra)
+    for i, step in enumerate(later):
+        extra.setdefault(first + i * (2 * ROWS - first) // len(later), []).append(step)
+    for k in range(3):
+        at = first + k * 5 * (2 * ROWS - first) // len(later)
+        steps = extra[at]
+        steps.insert(steps.index(later[5 * k]), loads[k].wait)
+    both_frames(a0_ref, a1_ref, v11, wt1_ref, o0_ref, o1_ref, x0_ref, x1_ref, extra)
 
 
 def local_second(a0_ref, a1_ref, wt_ref, frames_ref, o0_ref, o1_ref, x0_ref, x1_ref):
     _, _, v11, _ = tap_masks(frames_ref)
-    both_frames(a0_ref, a1_ref, v11, wt_ref, o0_ref, o1_ref, x0_ref, x1_ref, ())
-
-
-def halo_first(h_ref, o0_ref, o1_ref, wt_ref, gain_ref, frames_ref, p_ref, s_ref, x_ref, g_ref):
-    v01, _, _, v12 = tap_masks(frames_ref)
+    both_frames(a0_ref, a1_ref, v11, wt_ref, o0_ref, o1_ref, x0_ref, x1_ref, {})
+
+
+def halo_first(h_ref, o1_ref, wt_ref, gain_ref, frames_ref, s_ref, x_ref, g_ref):
+    _, _, _, v12 = tap_masks(frames_ref)
     spread_gain(gain_ref, g_ref)
     clear_edges(x_ref)
     put(x_ref, h_ref, 0)
     put(x_ref, h_ref, 1)
     for row in range(ROWS):
-        d = product(wt_ref, 1, 3, x_ref, row)
+        d = product(wt_ref, 2, 3, x_ref, row)
         put(x_ref, h_ref, row + 2)
-        p_ref[row] = o0_ref[row] + v01 * d[:C]
-        s_ref[row] = second_activation(o1_ref[row] + v12 * d[C:], g_ref)
+        s_ref[row] = second_activation(o1_ref[row] + v12 * d, g_ref)
+
+
+def halo_middle(o0_ref, x_ref, wt_ref, frames_ref, p_ref):
+    v01, _, _, _ = tap_masks(frames_ref)
+    for row in range(ROWS):
+        p_ref[row] = o0_ref[row] + v01 * product(wt_ref, 1, 2, x_ref, row)
 
 
 def halo_second(h_ref, p_ref, wt_ref, gain_ref, frames_ref, s_ref, x_ref, g_ref):
@@ -251,14 +292,23 @@
 VM = pl.BlockSpec(memory_space=pltpu.VMEM)
 SM = pl.BlockSpec(memory_space=pltpu.SMEM)
 ANY = pl.BlockSpec(memory_space=pl.ANY)
+HBM = pl.BlockSpec(memory_space=pltpu.HBM)
 NATURAL = pltpu.VMEM((2, C * ROWS, HALF), F32)
 SLABS = pltpu.VMEM(((ROWS + 2) * SLAB, COLS), BF16)
 GAINS = pltpu.VMEM((C, COLS), F32)
 FRAME = pltpu.VMEM((C, ROWS, COLS), BF16)
 SEMS = pltpu.SemaphoreType.DMA((PARTS,))
+RAW = pltpu.VMEM((2, C, ROWS, HALF), BF16)
+GAIN = pltpu.SMEM((C,), F32)
+WEIGHTS = pltpu.VMEM((TAPS * DEPTH, C), BF16)
+SLAB_ARRAY = jax.ShapeDtypeStruct(((ROWS + 2) * SLAB, COLS), BF16)
 SUM = jax.ShapeDtypeStruct((ROWS, C, COLS), F32)
 ACT = jax.ShapeDtypeStruct((ROWS, C, COLS), BF16)
 TURNED = jax.ShapeDtypeStruct((TAPS * C, DEPTH), BF16)
+
+
+def stay(value):
+    return pltpu.with_memory_space_constraint(value, pltpu.HBM)
 
 
 def call(kernel, in_specs, out_specs, out_shape, scratch, name, aliases=None):
@@ -280,19 +330,25 @@
     whole = jax.ShapeDtypeStruct(features.shape, BF16)
 
     a1, a0 = (
-        call(activation(i), [VM, SM], VM, ACT, [NATURAL], f"activation_{i}")(features, gain_first)
+        call(
+            activation(i), [HBM, HBM], VM, ACT, [RAW, GAIN, NATURAL, pltpu.SemaphoreType.DMA((5,))],
+            f"activation_{i}",
+        )(stay(features), stay(gain_first))
         for i in (1, 0)
     )
     a_before = shifted(a1, "tm")
     a_earlier = shifted(a0, "tm")
     o0, o1, wt1, wt2 = call(
-        local_first, [VM] * 4 + [SM], [VM] * 4, [SUM, SUM, TURNED, TURNED],
-        [SLABS, SLABS], "local_first",
-    )(a0, a1, w1, w2, video_frames)
-    part, s1 = call(
-        halo_first, [VM] * 4 + [SM, SM], [VM, VM], [SUM, ACT], [SLABS, GAINS], "halo_first",
-    )(a_before, o0, o1, wt1, gain_second, video_frames)
+        local_first, [VM] * 3 + [HBM, SM], [VM] * 4, [SUM, SUM, TURNED, TURNED],
+        [SLABS, SLABS, WEIGHTS, pltpu.SemaphoreType.DMA((3,))], "local_first",
+    )(a0, a1, w1, stay(w2), video_frames)
+    s1, x = call(
+        halo_first, [VM] * 3 + [SM, SM], [VM, VM], [ACT, SLAB_ARRAY], [GAINS], "halo_first",
+    )(a_before, o1, wt1, gain_second, video_frames)
     s_before = shifted(s1, "tm")
+    part = call(
+        halo_middle, [VM] * 3 + [SM], VM, SUM, [], "halo_middle",
+    )(o0, x, wt1, video_frames)
     s0 = call(
         halo_second, [VM] * 3 + [SM, SM], VM, ACT, [SLABS, GAINS], "halo_second",
     )(a_earlier, part, wt1, gain_second, video_frames)

time: 48.6 us -> 46.2 us (0.951)
  local copies, waits for them, and re-layouts: 3.85 us -> 0.02 us
  Pallas kernels: 29.1 us -> 32.8 us
  waiting for transfers between devices: 5.7 us -> 3.01 us
    unnamed x14 -> x8, local copies, waits for them, and re-layouts: 3.85 us -> 0.02 us
    pallas_call x4 -> x5, Pallas kernels: 12.8 us -> 16.5 us  [the longest x1 6.24 us: per_device(): call(local_first, [VM] * 3 + [HBM, SM], [VM] * 4, [SUM, SUM, TURNED, TURN...]
    ppermute x4, waiting for transfers between devices: 5.7 us -> 3.01 us  [shifted(): return lax.ppermute(value, axis, [(i, i + 1) for i in range(count - 1)])]
  transfers between devices with their start and end apart: 4 -> 4, of which waited for: 3 -> 2; matrix products, arithmetic and copies ran while one was open for 0% -> 0% of each run, Pallas kernels for 50% -> 58%
where the time goes in v2:
time: 46.2 us; the launch traced here: 46 us
  Pallas kernels  32.8 us (71%)
  starting transfers between devices  9.86 us (21%)
  waiting for transfers between devices  3.01 us (7%)
    ppermute x4, starting transfers between devices, shifted(): return lax.ppermute(value, axis, [(i, i + 1) for i in range(count - 1)])  9.86 us
    pallas_call x1, Pallas kernels, per_device(): call(local_first, [VM] * 3 + [HBM, SM], [VM] * 4, [SUM, SUM, TURNED, TURN...  6.24 us
    pallas_call x1, Pallas kernels, per_device(): call(local_second, [VM] * 3 + [SM], [VM] * 2, [SUM, SUM], [SLABS, SLABS],...  5.17 us
    pallas_call x2, Pallas kernels, per_device(): call(activation(i), [HBM, HBM], VM, ACT, [RAW, GAIN, NATURAL, pltpu.Semap...  5.01 us
    pallas_call x1, Pallas kernels, per_device(): call(last_frame, [VM] * 5 + [SM], [VM, ANY], [SUM, whole], [NATURAL, SLAB...  4.83 us
    pallas_call x1, Pallas kernels, per_device(): call(other_frame, [VM] * 4 + [SM, ANY], ANY, whole, [NATURAL, SLABS, FRAM...  3.35 us
    pallas_call x1, Pallas kernels, per_device(): call(halo_first, [VM] * 3 + [SM, SM], [VM, VM], [ACT, SLAB_ARRAY], [GAINS...  3.05 us
    ppermute x4, waiting for transfers between devices, shifted(): return lax.ppermute(value, axis, [(i, i + 1) for i in range(count - 1)])  3.01 us
  transfers between devices with their start and end apart: 4, of which 2 were waited for; matrix products, arithmetic and copies ran while one was open for 0% of the time, Pallas kernels for 58%

profile of v2, /device:TPU:8, one launch (start us, length us, event | category | flops | bytes accessed | tf_op | source)
XLA Modules:
  0.0 46.0 jit_solution(16191579679138060642)
XLA Ops:
  0.0 2.6 %activation_1.1.a1_ref = bf16[8,192,256]{2,1,0:T(8,128)(2,1)S(1)} custom-call(bf16[2,192,8,256]{3,2,1,0:T(8,128)(2,1)} %f_ref.7, f32[192]{0:T(256)} %gain_any.3), custom_call_target="tpu_custom_call" | custom-call | tf_op jit(solution)/shard_map/activation_1/pallas_call | solution.py:333
  2.6 0.0 copy-start.2
  2.6 1.9 %collective-permute-start.1 = (bf16[8,192,256]{2,1,0:T(8,128)(2,1)S(1)}, bf16[8,192,256]{2,1,0:T(8,128)(2,1)S(1)}, u32[]{:S(2)}, u32[]{:S(2)}) collective-permute-start(bf16[8,192,256]{2,1,0:T(8,128)(2,1)S(1)} %activation_1.1.a1_ref), channel_id=1, source_target_pairs={{0,1},{1,2},{2,3},{3,4},{4,5},{5,6},{6,7},{7,8},{8,9},{9,10},{10,1... | collective-permute-start | bytes 2359304 | tf_op jit(solution)/shard_map/ppermute | solution.py:25
  4.5 2.4 %activation_0.1.a0_ref = bf16[8,192,256]{2,1,0:T(8,128)(2,1)S(1)} custom-call(bf16[2,192,8,256]{3,2,1,0:T(8,128)(2,1)} %f_ref.7, f32[192]{0:T(256)} %gain_any.3), custom_call_target="tpu_custom_call" | custom-call | tf_op jit(solution)/shard_map/activation_0/pallas_call | solution.py:333
  7.0 3.5 %collective-permute-start = (bf16[8,192,256]{2,1,0:T(8,128)(2,1)S(1)}, bf16[8,192,256]{2,1,0:T(8,128)(2,1)S(1)}, u32[]{:S(2)}, u32[]{:S(2)}) collective-permute-start(bf16[8,192,256]{2,1,0:T(8,128)(2,1)S(1)} %activation_0.1.a0_ref), channel_id=1, source_target_pairs={{0,1},{1,2},{2,3},{3,4},{4,5},{5,6},{6,7},{7,8},{8,9},{9,10},{10,1... | collective-permute-start | bytes 2359304 | tf_op jit(solution)/shard_map/ppermute | solution.py:25
  10.5 0.0 copy-done.1
  10.5 0.0 copy-done.2
  10.5 0.0 copy-start.3
  10.5 6.2 %local_first.1 = (f32[8,192,256]{2,1,0:T(8,128)S(1)}, f32[8,192,256]{2,1,0:T(8,128)S(1)}, bf16[576,1728]{1,0:T(8,128)(2,1)S(1)}, bf16[576,1728]{1,0:T(8,128)(2,1)S(1)}) custom-call(bf16[8,192,256]{2,1,0:T(8,128)(2,1)S(1)} %activation_0.1.a0_ref, bf16[8,192,256]{2,1,0:T(8,128)(2,1)S(1)} %activation_1.1.a1_ref, bf16[5184,192]{1,0:T(8,128)(2,1)S(1)} %bitcast.2, ...), custom_call_target="tpu_custom_call" | custom-call | tf_op jit(solution)/shard_map/local_first/pallas_call | solution.py:341
  16.8 0.0 collective-permute-done.1.h_ref
  16.8 0.0 copy-done.3
  16.8 3.0 %halo_first.1 = (bf16[8,192,256]{2,1,0:T(8,128)(2,1)S(1)}, bf16[5760,256]{1,0:T(8,128)(2,1)S(1)}) custom-call(bf16[8,192,256]{2,1,0:T(8,128)(2,1)S(1)} %collective-permute-done.1.h_ref, f32[8,192,256]{2,1,0:T(8,128)S(1)} %get-tuple-element.16.o1_ref, bf16[576,1728]{1,0:T(8,128)(2,1)S(1)} %get-tuple-element.17.wt_ref, f32[192]{0:T(256)S(1)} %copy-done.3, ...), custom_call_target="tpu_custom_call" | custom-call | tf_op jit(solution)/shard_map/halo_first/pallas_call | solution.py:345
  19.9 1.9 %collective-permute-start.3 = (bf16[8,192,256]{2,1,0:T(8,128)(2,1)S(1)}, bf16[8,192,256]{2,1,0:T(8,128)(2,1)S(1)}, u32[]{:S(2)}, u32[]{:S(2)}) collective-permute-start(bf16[8,192,256]{2,1,0:T(8,128)(2,1)S(1)} %get-tuple-element.19.a1_ref), channel_id=1, source_target_pairs={{0,1},{1,2},{2,3},{3,4},{4,5},{5,6},{6,7},{7,8},{8,9},{9,10},{10,1... | collective-permute-start | bytes 2359304 | tf_op jit(solution)/shard_map/ppermute | solution.py:25
  21.8 2.2 %halo_middle.1.p_ref = f32[8,192,256]{2,1,0:T(8,128)S(1)} custom-call(f32[8,192,256]{2,1,0:T(8,128)S(1)} %get-tuple-element.15.o0_ref, bf16[5760,256]{1,0:T(8,128)(2,1)S(1)} %get-tuple-element.18.x_ref, bf16[576,1728]{1,0:T(8,128)(2,1)S(1)} %get-tuple-element.17.wt_ref, s32[8]{0:T(128)S(1)} %copy-done.2), custom_call_target="tpu_custom_call" | custom-call | tf_op jit(solution)/shard_map/halo_middle/pallas_call | solution.py:349
  24.0 1.2 %collective-permute-done.h_ref = bf16[8,192,256]{2,1,0:T(8,128)(2,1)S(1)} collective-permute-done((bf16[8,192,256]{2,1,0:T(8,128)(2,1)S(1)}, bf16[8,192,256]{2,1,0:T(8,128)(2,1)S(1)}, u32[]{:S(2)}, u32[]{:S(2)}) %collective-permute-start) | collective-permute-done | bytes 786464 | tf_op jit(solution)/shard_map/ppermute | solution.py:25
  25.2 2.9 %halo_second.1.a0_ref = bf16[8,192,256]{2,1,0:T(8,128)(2,1)S(1)} custom-call(bf16[8,192,256]{2,1,0:T(8,128)(2,1)S(1)} %collective-permute-done.h_ref, f32[8,192,256]{2,1,0:T(8,128)S(1)} %halo_middle.1.p_ref, bf16[576,1728]{1,0:T(8,128)(2,1)S(1)} %get-tuple-element.17.wt_ref, f32[192]{0:T(256)S(1)} %copy-done.3, s32[8]{0:T(128)S(1)} %copy-done.2), custom_call_target="tpu_custom_call" | custom-call | tf_op jit(solution)/shard_map/halo_second/pallas_call | solution.py:352
  28.2 2.5 %collective-permute-start.2 = (bf16[8,192,256]{2,1,0:T(8,128)(2,1)S(1)}, bf16[8,192,256]{2,1,0:T(8,128)(2,1)S(1)}, u32[]{:S(2)}, u32[]{:S(2)}) collective-permute-start(bf16[8,192,256]{2,1,0:T(8,128)(2,1)S(1)} %halo_second.1.a0_ref), channel_id=1, source_target_pairs={{0,1},{1,2},{2,3},{3,4},{4,5},{5,6},{6,7},{7,8},{8,9},{9,10},{10,1... | collective-permute-start | bytes 2359304 | tf_op jit(solution)/shard_map/ppermute | solution.py:25
  30.7 0.0 copy-start
  30.7 5.2 %local_second.1 = (f32[8,192,256]{2,1,0:T(8,128)S(1)}, f32[8,192,256]{2,1,0:T(8,128)S(1)}) custom-call(bf16[8,192,256]{2,1,0:T(8,128)(2,1)S(1)} %halo_second.1.a0_ref, bf16[8,192,256]{2,1,0:T(8,128)(2,1)S(1)} %get-tuple-element.19.a1_ref, bf16[576,1728]{1,0:T(8,128)(2,1)S(1)} %get-tuple-element.20.wt_ref, s32[8]{0:T(128)S(1)} %copy-done.2), custom_call_target="tpu_custom_call" | custom-call | tf_op jit(solution)/shard_map/local_second/pallas_call | solution.py:356
  35.9 0.0 collective-permute-done.3.h_ref
  35.9 0.0 copy-done
  35.9 4.8 %last_frame.1 = (f32[8,192,256]{2,1,0:T(8,128)S(1)}, bf16[2,192,8,256]{3,2,1,0:T(8,128)(2,1)}) custom-call(bf16[8,192,256]{2,1,0:T(8,128)(2,1)S(1)} %collective-permute-done.3.h_ref, f32[8,192,256]{2,1,0:T(8,128)S(1)} %get-tuple-element.21.o0_ref, f32[8,192,256]{2,1,0:T(8,128)S(1)} %get-tuple-element.22.o1_ref, ...), custom_call_target="tpu_custom_call" | custom-call | tf_op jit(solution)/shard_map/last_frame/pallas_call | solution.py:359
  40.8 1.7 %collective-permute-done.2.h_ref = bf16[8,192,256]{2,1,0:T(8,128)(2,1)S(1)} collective-permute-done((bf16[8,192,256]{2,1,0:T(8,128)(2,1)S(1)}, bf16[8,192,256]{2,1,0:T(8,128)(2,1)S(1)}, u32[]{:S(2)}, u32[]{:S(2)}) %collective-permute-start.2) | collective-permute-done | bytes 786464 | tf_op jit(solution)/shard_map/ppermute | solution.py:25
  42.5 3.4 %other_frame.1 = bf16[2,192,8,256]{3,2,1,0:T(8,128)(2,1)} custom-call(bf16[8,192,256]{2,1,0:T(8,128)(2,1)S(1)} %collective-permute-done.2.h_ref, f32[8,192,256]{2,1,0:T(8,128)S(1)} %get-tuple-element.23.p_ref, bf16[576,1728]{1,0:T(8,128)(2,1)S(1)} %get-tuple-element.20.wt_ref, bf16[2,192,8,256]{3,2,1,0:T(8,128)(2,1)S(1)} %copy-done, ...), custom_call_target="tpu_custom_call", output_to_operand_aliasing={{}: (5, {})} | custom-call | tf_op jit(solution)/shard_map/other_frame/pallas_call | solution.py:363
  (1 shorter events, 0.0 us)
Async XLA Ops:
  0.0 10.5 %copy-start.1 = (bf16[3,3,3,192,192]{4,3,2,1,0:T(8,128)(2,1)S(1)}, bf16[3,3,3,192,192]{4,3,2,1,0:T(8,128)(2,1)}, u32[]{:S(2)}) copy-start(bf16[3,3,3,192,192]{4,3,2,1,0:T(8,128)(2,1)} %param.9) | copy-start | bytes 5971972
  2.6 7.9 %copy-start.2 = (s32[8]{0:T(128)S(1)}, s32[8]{0:T(128)}, u32[]{:S(2)}) copy-start(s32[8]{0:T(128)} %frames_ref.13) | copy-start | bytes 100
  2.6 14.2 %collective-permute-start.1 = (bf16[8,192,256]{2,1,0:T(8,128)(2,1)S(1)}, bf16[8,192,256]{2,1,0:T(8,128)(2,1)S(1)}, u32[]{:S(2)}, u32[]{:S(2)}) collective-permute-start(bf16[8,192,256]{2,1,0:T(8,128)(2,1)S(1)} %activation_1.1.a1_ref), channel_id=1, source_target_pairs={{0,1},{1,2},{2,3},{3,4},{4,5},{5,6},{6,7},{7,8},{8,9},{9,10},{10,1... | collective-permute-start | bytes 2359304 | tf_op jit(solution)/shard_map/ppermute | solution.py:25
  7.0 18.3 %collective-permute-start = (bf16[8,192,256]{2,1,0:T(8,128)(2,1)S(1)}, bf16[8,192,256]{2,1,0:T(8,128)(2,1)S(1)}, u32[]{:S(2)}, u32[]{:S(2)}) collective-permute-start(bf16[8,192,256]{2,1,0:T(8,128)(2,1)S(1)} %activation_0.1.a0_ref), channel_id=1, source_target_pairs={{0,1},{1,2},{2,3},{3,4},{4,5},{5,6},{6,7},{7,8},{8,9},{9,10},{10,1... | collective-permute-start | bytes 2359304 | tf_op jit(solution)/shard_map/ppermute | solution.py:25
  10.5 6.3 %copy-start.3 = (f32[192]{0:T(256)S(1)}, f32[192]{0:T(256)}, u32[]{:S(2)}) copy-start(f32[192]{0:T(256)} %gain_ref.3) | copy-start | bytes 2308
  19.9 16.0 %collective-permute-start.3 = (bf16[8,192,256]{2,1,0:T(8,128)(2,1)S(1)}, bf16[8,192,256]{2,1,0:T(8,128)(2,1)S(1)}, u32[]{:S(2)}, u32[]{:S(2)}) collective-permute-start(bf16[8,192,256]{2,1,0:T(8,128)(2,1)S(1)} %get-tuple-element.19.a1_ref), channel_id=1, source_target_pairs={{0,1},{1,2},{2,3},{3,4},{4,5},{5,6},{6,7},{7,8},{8,9},{9,10},{10,1... | collective-permute-start | bytes 2359304 | tf_op jit(solution)/shard_map/ppermute | solution.py:25
  28.2 14.3 %collective-permute-start.2 = (bf16[8,192,256]{2,1,0:T(8,128)(2,1)S(1)}, bf16[8,192,256]{2,1,0:T(8,128)(2,1)S(1)}, u32[]{:S(2)}, u32[]{:S(2)}) collective-permute-start(bf16[8,192,256]{2,1,0:T(8,128)(2,1)S(1)} %halo_second.1.a0_ref), channel_id=1, source_target_pairs={{0,1},{1,2},{2,3},{3,4},{4,5},{5,6},{6,7},{7,8},{8,9},{9,10},{10,1... | collective-permute-start | bytes 2359304 | tf_op jit(solution)/shard_map/ppermute | solution.py:25
  30.7 5.2 %copy-start = (bf16[2,192,8,256]{3,2,1,0:T(8,128)(2,1)S(1)}, bf16[2,192,8,256]{3,2,1,0:T(8,128)(2,1)}, u32[]{:S(2)}) copy-start(bf16[2,192,8,256]{3,2,1,0:T(8,128)(2,1)} %f_ref.7) | copy-start | bytes 4718596

commit v3 on v1

v3 whole, which is shorter than its diff:
```python
import jax
import jax.numpy as jnp
from jax import lax
from jax.experimental import pallas as pl
from jax.experimental.pallas import tpu as pltpu
from jax.sharding import PartitionSpec as P

C = 192
ROWS = 8
COLS = 256
HALF = 128
TAPS = 3
SLAB = 3 * C
DEPTH = 9 * C
PIECE = 384
PARTS = 4
EPS = 1e-06
VMEM_LIMIT = 16 * 1024 * 1024
F32 = jnp.float32
BF16 = jnp.bfloat16


def shifted(value, axis):
    count = lax.axis_size(axis)
    return lax.ppermute(value, axis, [(i, i + 1) for i in range(count - 1)])


def tap_masks(frames_ref):
    first = 2 * lax.axis_index("tm")

    def step(v, carry):
        begin, start0, start1 = carry
        start0 = jnp.where(begin <= first, begin, start0)
        start1 = jnp.where(begin <= first + 1, begin, start1)
        return begin + frames_ref[v], start0, start1

    zero = jnp.int32(0)
    _, start0, start1 = lax.fori_loop(0, frames_ref.shape[0], step, (zero, zero, zero))
    return tuple(
        jnp.where(test, 1.0, 0.0).astype(F32)
        for test in (
            first - 1 >= start0,
            first - 2 >= start0,
            first >= start1,
            first - 1 >= start1,
        )
    )


def mask(m_ref, i):
    return m_ref[i : i + 1, :]


def turn_pieces(w_ref, wt_ref, taps):
    def turn(k, lo, hi):
        wt_ref[k * C : (k + 1) * C, lo:hi] = w_ref[k * DEPTH + lo : k * DEPTH + hi, :].T

    return [
        (lambda k=k, lo=lo: turn(k, lo, min(lo + PIECE, DEPTH)))
        for k in taps
        for lo in range(0, DEPTH, PIECE)
    ]


def put_row(x_ref, row, values):
    base = (row + 1) * SLAB
    cols = lax.broadcasted_iota(jnp.int32, (C, COLS), 1)
    left = jnp.where(cols == 0, 0.0, pltpu.roll(values, 1, 1))
    right = jnp.where(cols == COLS - 1, 0.0, pltpu.roll(values, COLS - 1, 1))
    x_ref[base : base + C, :] = left.astype(BF16)
    x_ref[base + C : base + 2 * C, :] = values.astype(BF16)
    x_ref[base + 2 * C : base + 3 * C, :] = right.astype(BF16)


def clear_edges(x_ref):
    zeros = jnp.zeros((SLAB, COLS), BF16)
    x_ref[0:SLAB, :] = zeros
    x_ref[(ROWS + 1) * SLAB : (ROWS + 2) * SLAB, :] = zeros


def put(x_ref, a_ref, row):
    if row < ROWS:
        put_row(x_ref, row, a_ref[row].astype(F32))


def product(wt_ref, lo, hi, x_ref, row):
    return jnp.dot(
        wt_ref[lo * C : hi * C, :],
        x_ref[row * SLAB : row * SLAB + DEPTH, :],
        preferred_element_type=F32,
    )


def inverse_rms(raw_ref, h):
    def squares(b, total):
        v = raw_ref[h, pl.ds(b * 16, 16)].astype(F32)
        return total + jnp.sum(v * v, axis=0)

    total = lax.fori_loop(0, C // 16, squares, jnp.zeros((ROWS, HALF), F32))
    return lax.rsqrt(total * (1.0 / C) + EPS)


def activate(raw_ref, h, c, inverse, gain_ref, t_ref):
    u = raw_ref[h, c].astype(F32) * inverse * gain_ref[c]
    at = c * ROWS if isinstance(c, int) else pl.multiple_of(c * ROWS, ROWS)
    t_ref[h, pl.ds(at, ROWS), :] = u * jax.nn.sigmoid(u)


def to_rows(t_ref, h, a_ref):
    for row in range(ROWS):
        a_ref[row, :, h * HALF : (h + 1) * HALF] = t_ref[
            h, pl.ds(row, C, stride=ROWS), :
        ].astype(BF16)


def frame_copies(f_ref, index, raw_ref, sems):
    return [
        [
            pltpu.make_async_copy(
                f_ref.at[index, pl.ds(q * C // 2, C // 2), :, pl.ds(h * HALF, HALF)],
                raw_ref.at[h, pl.ds(q * C // 2, C // 2)],
                sems.at[2 * h + q],
            )
            for q in range(2)
        ]
        for h in range(2)
    ]


def activate_last(f_ref, gain_any, a_ref, raw0_ref, raw1_ref, gain_ref, t_ref, sems, sems0):
    copies = frame_copies(f_ref, 1, raw1_ref, sems)
    others = frame_copies(f_ref, 0, raw0_ref, sems0)
    gains = pltpu.make_async_copy(gain_any, gain_ref, sems.at[4])
    for copy in copies[0] + [gains] + copies[1] + others[0] + others[1]:
        copy.start()
    for h in range(2):
        for copy in copies[h]:
            copy.wait()
        inverse = inverse_rms(raw1_ref, h)
        if h == 0:
            gains.wait()

        def act(b, _):
            for j in range(16):
                activate(raw1_ref, h, b * 16 + j, inverse, gain_ref, t_ref)
            return 0

        lax.fori_loop(0, C // 16, act, 0)
        to_rows(t_ref, h, a_ref)
    for copy in others[0] + others[1]:
        copy.wait()


def second_activation(values, g_ref):
    mean_square = jnp.sum(values * values, axis=0, keepdims=True) * (1.0 / C)
    u = values * lax.rsqrt(mean_square + EPS) * g_ref[...]
    return (u * jax.nn.sigmoid(u)).astype(BF16)


def put_transposed(t_ref, row, values):
    t_ref[0, pl.ds(row, C, stride=ROWS), :] = values[:, :HALF]
    t_ref[1, pl.ds(row, C, stride=ROWS), :] = values[:, HALF:]


def finish(t_ref, f_ref, index, c, buf_ref):
    at = c * ROWS if isinstance(c, int) else pl.multiple_of(c * ROWS, ROWS)
    v = jnp.concatenate([t_ref[h, pl.ds(at, ROWS), :] for h in range(2)], axis=1)
    buf_ref[c] = (f_ref[index, c].astype(F32) + v).astype(BF16)


def out_copy(buf_ref, out_ref, index, part, sems):
    span = pl.ds(part * (C // PARTS), C // PARTS)
    return pltpu.make_async_copy(buf_ref.at[span], out_ref.at[index, span], sems.at[part])


def own_last(
    a1_ref, raw0_ref, w1_ref, w2_any, gain_any, gain2_any, frames_any,
    a0_ref, o1_ref, wt1_ref, w2_ref, m_ref, g2_ref,
    gain_ref, gain2_ref, frames_ref, t_ref, x_ref, sems,
):
    small = [
        pltpu.make_async_copy(src, dst, sems.at[i])
        for i, (src, dst) in enumerate(
            ((gain_any, gain_ref), (frames_any, frames_ref), (gain2_any, gain2_ref))
        )
    ]
    third = DEPTH
    loads = [
        pltpu.make_async_copy(
            w2_any.at[pl.ds(k * third, third)], w2_ref.at[pl.ds(k * third, third)], sems.at[3 + k]
        )
        for k in range(TAPS)
    ]
    for copy in small + loads:
        copy.start()
    for step in turn_pieces(w1_ref, wt1_ref, (0,)):
        step()
    clear_edges(x_ref)
    put(x_ref, a1_ref, 0)
    put(x_ref, a1_ref, 1)
    inverse = [inverse_rms(raw0_ref, h) for h in range(2)]
    for copy in small:
        copy.wait()
    masks = tap_masks(frames_ref)
    for i in range(8):
        m_ref[i : i + 1, :] = jnp.full((1, COLS), masks[i % 4], F32)
    later = turn_pieces(w1_ref, wt1_ref, (1, 2))
    share = C // ROWS
    for row in range(ROWS):
        d = product(wt1_ref, 0, 1, x_ref, row)
        put(x_ref, a1_ref, row + 2)
        for c in range(row * share, (row + 1) * share):
            for h in range(2):
                activate(raw0_ref, h, c, inverse[h], gain_ref, t_ref)
            g2_ref[c : c + 1, :] = jnp.full((1, COLS), gain2_ref[c], F32)
        for step in later[row * len(later) // ROWS : (row + 1) * len(later) // ROWS]:
            step()
        o1_ref[row] = d
    for h in range(2):
        to_rows(t_ref, h, a0_ref)
    for load in loads:
        load.wait()


def own_first(a0_ref, o1_ref, wt1_ref, w2_ref, m_ref, p0_ref, p1_ref, wt2_ref, x_ref):
    clear_edges(x_ref)
    put(x_ref, a0_ref, 0)
    put(x_ref, a0_ref, 1)
    later = turn_pieces(w2_ref, wt2_ref, (0, 1, 2))
    for row in range(ROWS):
        d = product(wt1_ref, 0, 2, x_ref, row)
        put(x_ref, a0_ref, row + 2)
        for step in later[row * len(later) // ROWS : (row + 1) * len(later) // ROWS]:
            step()
        p0_ref[row] = d[:C]
        p1_ref[row] = o1_ref[row] + mask(m_ref, 2) * d[C:]


def halo_first(h_ref, o1_ref, wt_ref, g_ref, m_ref, s_ref, x_ref):
    clear_edges(x_ref)
    put(x_ref, h_ref, 0)
    put(x_ref, h_ref, 1)
    for row in range(ROWS):
        d = product(wt_ref, 2, 3, x_ref, row)
        put(x_ref, h_ref, row + 2)
        s_ref[row] = second_activation(o1_ref[row] + mask(m_ref, 3) * d, g_ref)


def halo_middle(o0_ref, x_ref, wt_ref, m_ref, p_ref):
    for row in range(ROWS):
        p_ref[row] = o0_ref[row] + mask(m_ref, 0) * product(wt_ref, 1, 2, x_ref, row)


def halo_second(h_ref, p_ref, wt_ref, g_ref, m_ref, s_ref, x_ref):
    clear_edges(x_ref)
    put(x_ref, h_ref, 0)
    put(x_ref, h_ref, 1)
    for row in range(ROWS):
        d = product(wt_ref, 2, 3, x_ref, row)
        put(x_ref, h_ref, row + 2)
        s_ref[row] = second_activation(p_ref[row] + mask(m_ref, 1) * d, g_ref)


def local_second(s0_ref, s1_ref, wt_ref, m_ref, o0_ref, o1_ref, x0_ref, x1_ref):
    clear_edges(x0_ref)
    put(x0_ref, s0_ref, 0)
    put(x0_ref, s0_ref, 1)
    for row in range(ROWS):
        d = product(wt_ref, 0, 2, x0_ref, row)
        put(x0_ref, s0_ref, row + 2)
        put(x1_ref, s1_ref, row)
        o0_ref[row] = d[:C]
        o1_ref[row] = mask(m_ref, 2) * d[C:]
    clear_edges(x1_ref)
    for row in range(ROWS):
        o1_ref[row] += product(wt_ref, 0, 1, x1_ref, row)


def last_frame(h_ref, o0_ref, o1_ref, wt_ref, m_ref, p_ref, t_ref, x_ref):
    clear_edges(x_ref)
    put(x_ref, h_ref, 0)
    put(x_ref, h_ref, 1)
    for row in range(ROWS):
        d = product(wt_ref, 1, 3, x_ref, row)
        put(x_ref, h_ref, row + 2)
        p_ref[row] = o0_ref[row] + mask(m_ref, 0) * d[:C]
        put_transposed(t_ref, row, o1_ref[row] + mask(m_ref, 3) * d[C:])


def other_frame(
    h_ref, p_ref, wt_ref, m_ref, t1_ref, f_ref, out_ref, t_ref, x_ref, buf0_ref, buf1_ref, sems0, sems1
):
    clear_edges(x_ref)
    put(x_ref, h_ref, 0)
    put(x_ref, h_ref, 1)
    share = C // ROWS
    for row in range(ROWS):
        d = product(wt_ref, 2, 3, x_ref, row)
        put(x_ref, h_ref, row + 2)
        for c in range(row * share, (row + 1) * share):
            finish(t1_ref, f_ref, 1, c, buf1_ref)
        put_transposed(t_ref, row, p_ref[row] + mask(m_ref, 1) * d)
        if (row + 1) % (ROWS // PARTS) == 0:
            out_copy(buf1_ref, out_ref, 1, row // (ROWS // PARTS), sems1).start()
    for part in range(PARTS):

        def step(b, _):
            for j in range(16):
                finish(t_ref, f_ref, 0, part * (C // PARTS) + b * 16 + j, buf0_ref)
            return 0

        lax.fori_loop(0, C // PARTS // 16, step, 0)
        out_copy(buf0_ref, out_ref, 0, part, sems0).start()
    for part in range(PARTS):
        out_copy(buf1_ref, out_ref, 1, part, sems1).wait()
        out_copy(buf0_ref, out_ref, 0, part, sems0).wait()


VM = pl.BlockSpec(memory_space=pltpu.VMEM)
ANY = pl.BlockSpec(memory_space=pl.ANY)
HBM = pl.BlockSpec(memory_space=pltpu.HBM)
NATURAL = pltpu.VMEM((2, C * ROWS, HALF), F32)
RAW = pltpu.VMEM((2, C, ROWS, HALF), BF16)
SLABS = pltpu.VMEM(((ROWS + 2) * SLAB, COLS), BF16)
FRAME = pltpu.VMEM((C, ROWS, COLS), BF16)
GAIN = pltpu.SMEM((C,), F32)
SEMS = pltpu.SemaphoreType.DMA((PARTS,))
A_SUM = jax.ShapeDtypeStruct((ROWS, C, COLS), F32)
A_ACT = jax.ShapeDtypeStruct((ROWS, C, COLS), BF16)
A_RAW = jax.ShapeDtypeStruct((2, C, ROWS, HALF), BF16)
A_SLABS = jax.ShapeDtypeStruct(((ROWS + 2) * SLAB, COLS), BF16)
A_NATURAL = jax.ShapeDtypeStruct((2, C * ROWS, HALF), F32)
A_WEIGHTS = jax.ShapeDtypeStruct((TAPS * DEPTH, C), BF16)
A_TURNED = jax.ShapeDtypeStruct((TAPS * C, DEPTH), BF16)
A_MASKS = jax.ShapeDtypeStruct((8, COLS), F32)
A_GAINS = jax.ShapeDtypeStruct((C, COLS), F32)


def stay(value):
    return pltpu.with_memory_space_constraint(value, pltpu.HBM)


def call(kernel, in_specs, out_shape, scratch=(), out_specs=None):
    return pl.pallas_call(
        kernel,
        in_specs=in_specs,
        out_specs=out_specs or jax.tree.map(lambda _: VM, out_shape),
        out_shape=out_shape,
        scratch_shapes=scratch,
        compiler_params=pltpu.CompilerParams(vmem_limit_bytes=VMEM_LIMIT),
        name=kernel.__name__,
    )


def per_device(features, video_frames, gain_first, conv_first, gain_second, conv_second):
    w1 = conv_first.reshape(TAPS * DEPTH, C)
    w2 = conv_second.reshape(TAPS * DEPTH, C)

    a1, raw0 = call(
        activate_last, [HBM, HBM], [A_ACT, A_RAW],
        [RAW, GAIN, NATURAL, pltpu.SemaphoreType.DMA((5,)), pltpu.SemaphoreType.DMA((4,))],
    )(stay(features), stay(gain_first))
    a_before = shifted(a1, "tm")
    a0, o1, wt1, w2, m, g2 = call(
        own_last, [VM] * 3 + [HBM] * 4, [A_ACT, A_SUM, A_TURNED, A_WEIGHTS, A_MASKS, A_GAINS],
        [
            GAIN, GAIN, pltpu.SMEM(video_frames.shape, jnp.int32), NATURAL, SLABS,
            pltpu.SemaphoreType.DMA((6,)),
        ],
    )(a1, raw0, w1, stay(w2), stay(gain_first), stay(gain_second), stay(video_frames))
    a_earlier = shifted(a0, "tm")
    p0, p1, wt2 = call(own_first, [VM] * 5, [A_SUM, A_SUM, A_TURNED], [SLABS])(a0, o1, wt1, w2, m)
    s1, x = call(halo_first, [VM] * 5, [A_ACT, A_SLABS])(a_before, p1, wt1, g2, m)
    s_before = shifted(s1, "tm")
    part = call(halo_middle, [VM] * 4, A_SUM)(p0, x, wt1, m)
    s0 = call(halo_second, [VM] * 5, A_ACT, [SLABS])(a_earlier, part, wt1, g2, m)
    s_earlier = shifted(s0, "tm")
    q0, q1 = call(local_second, [VM] * 4, [A_SUM, A_SUM], [SLABS, SLABS])(s0, s1, wt2, m)
    part2, t1 = call(last_frame, [VM] * 5, [A_SUM, A_NATURAL], [SLABS])(s_before, q0, q1, wt2, m)
    return call(
        other_frame, [VM] * 6, jax.ShapeDtypeStruct(features.shape, BF16),
        [NATURAL, SLABS, FRAME, FRAME, SEMS, SEMS], out_specs=ANY,
    )(s_earlier, part2, wt2, m, t1, features)


def solution(mesh):
    in_specs = (P(("group", "tm"), None, None, None), P("group"), P(), P(), P(), P())
    out_specs = P(("group", "tm"), None, None, None)
    return jax.shard_map(
        per_device, mesh=mesh, in_specs=in_specs, out_specs=out_specs, check_vma=False
    )
```

time: 48.6 us -> 45.4 us (0.934)
  Pallas kernels: 29.1 us -> 25.1 us
  waiting for transfers between devices: 5.7 us -> 8.54 us
  local copies, waits for them, and re-layouts: 3.85 us -> 1.75 us
    pallas_call x8 -> x9, Pallas kernels: 29.1 us -> 25.1 us  [the longest x1 4.62 us: per_device(): call(local_second, [VM] * 4, [A_SUM, A_SUM], [SLABS, SLABS])(s0, s1, wt2, m)]
    ppermute x4, waiting for transfers between devices: 5.7 us -> 8.54 us  [shifted(): return lax.ppermute(value, axis, [(i, i + 1) for i in range(count - 1)])]
    unnamed x14 -> x4, local copies, waits for them, and re-layouts: 3.85 us -> 1.75 us
  transfers between devices with their start and end apart: 4 -> 4, of which waited for: 3 -> 3; matrix products, arithmetic and copies ran while one was open for 0% -> 0% of each run, Pallas kernels for 50% -> 44%
where the time goes in v3:
time: 45.4 us; the launch traced here: 45.1 us
  Pallas kernels  25.1 us (55%)
  starting transfers between devices  9.44 us (21%)
  waiting for transfers between devices  8.54 us (19%)
  local copies, waits for them, and re-layouts  1.75 us (4%)
    ppermute x4, starting transfers between devices, shifted(): return lax.ppermute(value, axis, [(i, i + 1) for i in range(count - 1)])  9.44 us
    ppermute x4, waiting for transfers between devices, shifted(): return lax.ppermute(value, axis, [(i, i + 1) for i in range(count - 1)])  8.54 us
    pallas_call x1, Pallas kernels, per_device(): call(local_second, [VM] * 4, [A_SUM, A_SUM], [SLABS, SLABS])(s0, s1, wt2, m)  4.62 us
    pallas_call x1, Pallas kernels, per_device(): call(last_frame, [VM] * 5, [A_SUM, A_NATURAL], [SLABS])  3.28 us
    pallas_call x1, Pallas kernels, per_device(): call(own_first, [VM] * 5, [A_SUM, A_SUM, A_TURNED], [SLABS])  3.18 us
    pallas_call x1, Pallas kernels, per_device(): call(own_last, [VM] * 3 + [HBM] * 4, [A_ACT, A_SUM, A_TURNED, A_WEIGHTS,...  3.09 us
    pallas_call x1, Pallas kernels, per_device(): call(other_frame, [VM] * 6, jax.ShapeDtypeStruct(features.shape, BF16), [...  2.99 us
    pallas_call x1, Pallas kernels, per_device(): call(activate_last, [HBM, HBM], [A_ACT, A_RAW], [RAW, GAIN, NATURAL, pltp...  2.47 us
  transfers between devices with their start and end apart: 4, of which 3 were waited for; matrix products, arithmetic and copies ran while one was open for 0% of the time, Pallas kernels for 44%

profile of v3, /device:TPU:8, one launch (start us, length us, event | category | flops | bytes accessed | tf_op | source)
XLA Modules:
  0.0 45.1 jit_solution(15694643764586462386)
XLA Ops:
  0.0 2.5 %activate_last.1 = (bf16[8,192,256]{2,1,0:T(8,128)(2,1)S(1)}, bf16[2,192,8,128]{3,2,1,0:T(8,128)(2,1)S(1)}) custom-call(bf16[2,192,8,256]{3,2,1,0:T(8,128)(2,1)} %f_ref.3, f32[192]{0:T(256)} %gain_any.3), custom_call_target="tpu_custom_call" | custom-call | tf_op jit(solution)/shard_map/activate_last/pallas_call | solution.py:359
  2.5 1.9 %collective-permute-start.1 = (bf16[8,192,256]{2,1,0:T(8,128)(2,1)S(1)}, bf16[8,192,256]{2,1,0:T(8,128)(2,1)S(1)}, u32[]{:S(2)}, u32[]{:S(2)}) collective-permute-start(bf16[8,192,256]{2,1,0:T(8,128)(2,1)S(1)} %get-tuple-element.22.a1_ref), channel_id=1, source_target_pairs={{0,1},{1,2},{2,3},{3,4},{4,5},{5,6},{6,7},{7,8},{8,9},{9,10},{10,1... | collective-permute-start | bytes 2359304 | tf_op jit(solution)/shard_map/ppermute | solution.py:25
  4.4 0.0 copy-start.1
  4.4 1.7 %copy-done.1 = bf16[3,3,3,192,192]{4,3,2,1,0:T(8,128)(2,1)S(1)} copy-done((bf16[3,3,3,192,192]{4,3,2,1,0:T(8,128)(2,1)S(1)}, bf16[3,3,3,192,192]{4,3,2,1,0:T(8,128)(2,1)}, u32[]{:S(2)}) %copy-start.1) | copy-done | bytes 1990680
  6.2 3.1 %own_last.1 = (bf16[8,192,256]{2,1,0:T(8,128)(2,1)S(1)}, f32[8,192,256]{2,1,0:T(8,128)S(1)}, bf16[576,1728]{1,0:T(8,128)(2,1)S(1)}, bf16[5184,192]{1,0:T(8,128)(...) custom-call(bf16[8,192,256]{2,1,0:T(8,128)(2,1)S(1)} %get-tuple-element.22.a1_ref, ...), custom_call_target="tpu_custom_call" | custom-call | tf_op jit(solution)/shard_map/own_last/pallas_call | solution.py:364
  9.3 3.5 %collective-permute-start = (bf16[8,192,256]{2,1,0:T(8,128)(2,1)S(1)}, bf16[8,192,256]{2,1,0:T(8,128)(2,1)S(1)}, u32[]{:S(2)}, u32[]{:S(2)}) collective-permute-start(bf16[8,192,256]{2,1,0:T(8,128)(2,1)S(1)} %get-tuple-element.24.a0_ref), channel_id=1, source_target_pairs={{0,1},{1,2},{2,3},{3,4},{4,5},{5,6},{6,7},{7,8},{8,9},{9,10},{10,1... | collective-permute-start | bytes 2359304 | tf_op jit(solution)/shard_map/ppermute | solution.py:25
  12.8 3.2 %own_first.1 = (f32[8,192,256]{2,1,0:T(8,128)S(1)}, f32[8,192,256]{2,1,0:T(8,128)S(1)}, bf16[576,1728]{1,0:T(8,128)(2,1)S(1)}) custom-call(bf16[8,192,256]{2,1,0:T(8,128)(2,1)S(1)} %get-tuple-element.24.a0_ref, f32[8,192,256]{2,1,0:T(8,128)S(1)} %get-tuple-element.25.o1_ref, bf16[576,1728]{1,0:T(8,128)(2,1)S(1)} %get-tuple-element.26.wt1_ref.wt_ref, ...), custom_call_target="tpu_custom_call" | custom-call | tf_op jit(solution)/shard_map/own_first/pallas_call | solution.py:372
  15.9 0.7 %collective-permute-done.1.h_ref = bf16[8,192,256]{2,1,0:T(8,128)(2,1)S(1)} collective-permute-done((bf16[8,192,256]{2,1,0:T(8,128)(2,1)S(1)}, bf16[8,192,256]{2,1,0:T(8,128)(2,1)S(1)}, u32[]{:S(2)}, u32[]{:S(2)}) %collective-permute-start.1) | collective-permute-done | bytes 786464 | tf_op jit(solution)/shard_map/ppermute | solution.py:25
  16.7 2.0 %halo_first.1 = (bf16[8,192,256]{2,1,0:T(8,128)(2,1)S(1)}, bf16[5760,256]{1,0:T(8,128)(2,1)S(1)}) custom-call(bf16[8,192,256]{2,1,0:T(8,128)(2,1)S(1)} %collective-permute-done.1.h_ref, f32[8,192,256]{2,1,0:T(8,128)S(1)} %get-tuple-element.30.o1_ref, bf16[576,1728]{1,0:T(8,128)(2,1)S(1)} %get-tuple-element.26.wt1_ref.wt_ref, ...), custom_call_target="tpu_custom_call" | custom-call | tf_op jit(solution)/shard_map/halo_first/pallas_call | solution.py:373
  18.6 1.9 %collective-permute-start.3 = (bf16[8,192,256]{2,1,0:T(8,128)(2,1)S(1)}, bf16[8,192,256]{2,1,0:T(8,128)(2,1)S(1)}, u32[]{:S(2)}, u32[]{:S(2)}) collective-permute-start(bf16[8,192,256]{2,1,0:T(8,128)(2,1)S(1)} %get-tuple-element.33.s1_ref), channel_id=1, source_target_pairs={{0,1},{1,2},{2,3},{3,4},{4,5},{5,6},{6,7},{7,8},{8,9},{9,10},{10,1... | collective-permute-start | bytes 2359304 | tf_op jit(solution)/shard_map/ppermute | solution.py:25
  20.6 1.6 %halo_middle.1.p_ref = f32[8,192,256]{2,1,0:T(8,128)S(1)} custom-call(f32[8,192,256]{2,1,0:T(8,128)S(1)} %get-tuple-element.29.o0_ref, bf16[5760,256]{1,0:T(8,128)(2,1)S(1)} %get-tuple-element.32.x_ref, bf16[576,1728]{1,0:T(8,128)(2,1)S(1)} %get-tuple-element.26.wt1_ref.wt_ref, f32[8,256]{1,0:T(8,128)S(1)} %get-tuple-element.28.m_ref), custom_call_target="tpu_custom_call" | custom-call | tf_op jit(solution)/shard_map/halo_middle/pallas_call | solution.py:375
  22.2 2.9 %collective-permute-done.h_ref = bf16[8,192,256]{2,1,0:T(8,128)(2,1)S(1)} collective-permute-done((bf16[8,192,256]{2,1,0:T(8,128)(2,1)S(1)}, bf16[8,192,256]{2,1,0:T(8,128)(2,1)S(1)}, u32[]{:S(2)}, u32[]{:S(2)}) %collective-permute-start) | collective-permute-done | bytes 786464 | tf_op jit(solution)/shard_map/ppermute | solution.py:25
  25.1 1.9 %halo_second.1.s0_ref = bf16[8,192,256]{2,1,0:T(8,128)(2,1)S(1)} custom-call(bf16[8,192,256]{2,1,0:T(8,128)(2,1)S(1)} %collective-permute-done.h_ref, f32[8,192,256]{2,1,0:T(8,128)S(1)} %halo_middle.1.p_ref, bf16[576,1728]{1,0:T(8,128)(2,1)S(1)} %get-tuple-element.26.wt1_ref.wt_ref, f32[192,256]{1,0:T(8,128)S(1)} %get-tuple-element.31.g_ref, ...), custom_call_target="tpu_custom_call" | custom-call | tf_op jit(solution)/shard_map/halo_second/pallas_call | solution.py:376
  27.1 2.1 %collective-permute-start.2 = (bf16[8,192,256]{2,1,0:T(8,128)(2,1)S(1)}, bf16[8,192,256]{2,1,0:T(8,128)(2,1)S(1)}, u32[]{:S(2)}, u32[]{:S(2)}) collective-permute-start(bf16[8,192,256]{2,1,0:T(8,128)(2,1)S(1)} %halo_second.1.s0_ref), channel_id=1, source_target_pairs={{0,1},{1,2},{2,3},{3,4},{4,5},{5,6},{6,7},{7,8},{8,9},{9,10},{10,1... | collective-permute-start | bytes 2359304 | tf_op jit(solution)/shard_map/ppermute | solution.py:25
  29.2 4.6 %local_second.1 = (f32[8,192,256]{2,1,0:T(8,128)S(1)}, f32[8,192,256]{2,1,0:T(8,128)S(1)}) custom-call(bf16[8,192,256]{2,1,0:T(8,128)(2,1)S(1)} %halo_second.1.s0_ref, bf16[8,192,256]{2,1,0:T(8,128)(2,1)S(1)} %get-tuple-element.33.s1_ref, bf16[576,1728]{1,0:T(8,128)(2,1)S(1)} %get-tuple-element.34.wt_ref, f32[8,256]{1,0:T(8,128)S(1)} %get-tuple-element.28.m_ref), custom_call_target="tpu_custom_call" | custom-call | tf_op jit(solution)/shard_map/local_second/pallas_call | solution.py:378
  33.8 0.0 collective-permute-done.3.h_ref
  33.8 0.0 copy-start
  33.8 3.3 %last_frame.1 = (f32[8,192,256]{2,1,0:T(8,128)S(1)}, f32[2,1536,128]{2,1,0:T(8,128)S(1)}) custom-call(bf16[8,192,256]{2,1,0:T(8,128)(2,1)S(1)} %collective-permute-done.3.h_ref, f32[8,192,256]{2,1,0:T(8,128)S(1)} %get-tuple-element.35.o0_ref, f32[8,192,256]{2,1,0:T(8,128)S(1)} %get-tuple-element.36.o1_ref, bf16[576,1728]{1,0:T(8,128)(2,1)S(1)} %get-tuple-element.34.wt_ref, ...), custom_call_target="tpu_custom_call" | custom-call | tf_op jit(solution)/shard_map/last_frame/pallas_call | solution.py:379
  37.1 4.9 %collective-permute-done.2.h_ref = bf16[8,192,256]{2,1,0:T(8,128)(2,1)S(1)} collective-permute-done((bf16[8,192,256]{2,1,0:T(8,128)(2,1)S(1)}, bf16[8,192,256]{2,1,0:T(8,128)(2,1)S(1)}, u32[]{:S(2)}, u32[]{:S(2)}) %collective-permute-start.2) | collective-permute-done | bytes 786464 | tf_op jit(solution)/shard_map/ppermute | solution.py:25
  42.0 0.0 copy-done
  42.0 3.0 %other_frame.1 = bf16[2,192,8,256]{3,2,1,0:T(8,128)(2,1)} custom-call(bf16[8,192,256]{2,1,0:T(8,128)(2,1)S(1)} %collective-permute-done.2.h_ref, f32[8,192,256]{2,1,0:T(8,128)S(1)} %get-tuple-element.37.p_ref, bf16[576,1728]{1,0:T(8,128)(2,1)S(1)} %get-tuple-element.34.wt_ref, f32[8,256]{1,0:T(8,128)S(1)} %get-tuple-element.28.m_ref, ...), custom_call_target="tpu_custom_call" | custom-call | tf_op jit(solution)/shard_map/other_frame/pallas_call | solution.py:380
Async XLA Ops:
  2.5 14.2 %collective-permute-start.1 = (bf16[8,192,256]{2,1,0:T(8,128)(2,1)S(1)}, bf16[8,192,256]{2,1,0:T(8,128)(2,1)S(1)}, u32[]{:S(2)}, u32[]{:S(2)}) collective-permute-start(bf16[8,192,256]{2,1,0:T(8,128)(2,1)S(1)} %get-tuple-element.22.a1_ref), channel_id=1, source_target_pairs={{0,1},{1,2},{2,3},{3,4},{4,5},{5,6},{6,7},{7,8},{8,9},{9,10},{10,1... | collective-permute-start | bytes 2359304 | tf_op jit(solution)/shard_map/ppermute | solution.py:25
  4.4 1.8 %copy-start.1 = (bf16[3,3,3,192,192]{4,3,2,1,0:T(8,128)(2,1)S(1)}, bf16[3,3,3,192,192]{4,3,2,1,0:T(8,128)(2,1)}, u32[]{:S(2)}) copy-start(bf16[3,3,3,192,192]{4,3,2,1,0:T(8,128)(2,1)} %param.9) | copy-start | bytes 5971972
  9.3 15.9 %collective-permute-start = (bf16[8,192,256]{2,1,0:T(8,128)(2,1)S(1)}, bf16[8,192,256]{2,1,0:T(8,128)(2,1)S(1)}, u32[]{:S(2)}, u32[]{:S(2)}) collective-permute-start(bf16[8,192,256]{2,1,0:T(8,128)(2,1)S(1)} %get-tuple-element.24.a0_ref), channel_id=1, source_target_pairs={{0,1},{1,2},{2,3},{3,4},{4,5},{5,6},{6,7},{7,8},{8,9},{9,10},{10,1... | collective-permute-start | bytes 2359304 | tf_op jit(solution)/shard_map/ppermute | solution.py:25
  18.6 15.1 %collective-permute-start.3 = (bf16[8,192,256]{2,1,0:T(8,128)(2,1)S(1)}, bf16[8,192,256]{2,1,0:T(8,128)(2,1)S(1)}, u32[]{:S(2)}, u32[]{:S(2)}) collective-permute-start(bf16[8,192,256]{2,1,0:T(8,128)(2,1)S(1)} %get-tuple-element.33.s1_ref), channel_id=1, source_target_pairs={{0,1},{1,2},{2,3},{3,4},{4,5},{5,6},{6,7},{7,8},{8,9},{9,10},{10,1... | collective-permute-start | bytes 2359304 | tf_op jit(solution)/shard_map/ppermute | solution.py:25
  27.1 14.9 %collective-permute-start.2 = (bf16[8,192,256]{2,1,0:T(8,128)(2,1)S(1)}, bf16[8,192,256]{2,1,0:T(8,128)(2,1)S(1)}, u32[]{:S(2)}, u32[]{:S(2)}) collective-permute-start(bf16[8,192,256]{2,1,0:T(8,128)(2,1)S(1)} %halo_second.1.s0_ref), channel_id=1, source_target_pairs={{0,1},{1,2},{2,3},{3,4},{4,5},{5,6},{6,7},{7,8},{8,9},{9,10},{10,1... | collective-permute-start | bytes 2359304 | tf_op jit(solution)/shard_map/ppermute | solution.py:25
  33.8 8.2 %copy-start = (bf16[2,192,8,256]{3,2,1,0:T(8,128)(2,1)S(1)}, bf16[2,192,8,256]{3,2,1,0:T(8,128)(2,1)}, u32[]{:S(2)}) copy-start(bf16[2,192,8,256]{3,2,1,0:T(8,128)(2,1)} %f_ref.3) | copy-start | bytes 4718596

commit v4 on v3

--- a/solution.py
+++ b/solution.py
@@ -14,6 +14,7 @@
 DEPTH = 9 * C
 PIECE = 384
 PARTS = 4
+EARLY = 6
 EPS = 1e-06
 VMEM_LIMIT = 16 * 1024 * 1024
 F32 = jnp.float32
@@ -51,9 +52,10 @@
     return m_ref[i : i + 1, :]
 
 
-def turn_pieces(w_ref, wt_ref, taps):
+def turn_pieces(w_ref, wt_ref, taps, start=0):
     def turn(k, lo, hi):
-        wt_ref[k * C : (k + 1) * C, lo:hi] = w_ref[k * DEPTH + lo : k * DEPTH + hi, :].T
+        base = (k - start) * DEPTH
+        wt_ref[k * C : (k + 1) * C, lo:hi] = w_ref[base + lo : base + hi, :].T
 
     return [
         (lambda k=k, lo=lo: turn(k, lo, min(lo + PIECE, DEPTH)))
@@ -78,9 +80,9 @@
     x_ref[(ROWS + 1) * SLAB : (ROWS + 2) * SLAB, :] = zeros
 
 
-def put(x_ref, a_ref, row):
-    if row < ROWS:
-        put_row(x_ref, row, a_ref[row].astype(F32))
+def put(x_ref, a_ref, row, start=0):
+    if row - start < a_ref.shape[0]:
+        put_row(x_ref, row, a_ref[row - start].astype(F32))
 
 
 def product(wt_ref, lo, hi, x_ref, row):
@@ -127,11 +129,14 @@
     ]
 
 
-def activate_last(f_ref, gain_any, a_ref, raw0_ref, raw1_ref, gain_ref, t_ref, sems, sems0):
+def activate_last(
+    f_ref, w1_any, gain_any, a_ref, raw0_ref, w_ref, raw1_ref, gain_ref, t_ref, sems, sems0
+):
     copies = frame_copies(f_ref, 1, raw1_ref, sems)
     others = frame_copies(f_ref, 0, raw0_ref, sems0)
     gains = pltpu.make_async_copy(gain_any, gain_ref, sems.at[4])
-    for copy in copies[0] + [gains] + copies[1] + others[0] + others[1]:
+    later = [pltpu.make_async_copy(w1_any.at[pl.ds(0, DEPTH)], w_ref, sems.at[5])] + others[0] + others[1]
+    for copy in copies[0] + [gains] + copies[1] + later:
         copy.start()
     for h in range(2):
         for copy in copies[h]:
@@ -140,14 +145,10 @@
         if h == 0:
             gains.wait()
 
-        def act(b, _):
-            for j in range(16):
-                activate(raw1_ref, h, b * 16 + j, inverse, gain_ref, t_ref)
-            return 0
-
-        lax.fori_loop(0, C // 16, act, 0)
+        for c in range(C):
+            activate(raw1_ref, h, c, inverse, gain_ref, t_ref)
         to_rows(t_ref, h, a_ref)
-    for copy in others[0] + others[1]:
+    for copy in later:
         copy.wait()
 
 
@@ -174,9 +175,9 @@
 
 
 def own_last(
-    a1_ref, raw0_ref, w1_ref, w2_any, gain_any, gain2_any, frames_any,
+    a1_ref, raw0_ref, first_ref, w1_any, w2_any, gain_any, gain2_any, frames_any,
     a0_ref, o1_ref, wt1_ref, w2_ref, m_ref, g2_ref,
-    gain_ref, gain2_ref, frames_ref, t_ref, x_ref, sems,
+    gain_ref, gain2_ref, frames_ref, t_ref, x_ref, w1_ref, sems,
 ):
     small = [
         pltpu.make_async_copy(src, dst, sems.at[i])
@@ -184,16 +185,11 @@
             ((gain_any, gain_ref), (frames_any, frames_ref), (gain2_any, gain2_ref))
         )
     ]
-    third = DEPTH
-    loads = [
-        pltpu.make_async_copy(
-            w2_any.at[pl.ds(k * third, third)], w2_ref.at[pl.ds(k * third, third)], sems.at[3 + k]
-        )
-        for k in range(TAPS)
-    ]
-    for copy in small + loads:
+    others = pltpu.make_async_copy(w1_any.at[pl.ds(DEPTH, 2 * DEPTH)], w1_ref, sems.at[3])
+    load = pltpu.make_async_copy(w2_any, w2_ref, sems.at[4])
+    for copy in small + [others, load]:
         copy.start()
-    for step in turn_pieces(w1_ref, wt1_ref, (0,)):
+    for step in turn_pieces(first_ref, wt1_ref, (0,)):
         step()
     clear_edges(x_ref)
     put(x_ref, a1_ref, 0)
@@ -204,7 +200,7 @@
     masks = tap_masks(frames_ref)
     for i in range(8):
         m_ref[i : i + 1, :] = jnp.full((1, COLS), masks[i % 4], F32)
-    later = turn_pieces(w1_ref, wt1_ref, (1, 2))
+    later = turn_pieces(w1_ref, wt1_ref, (1, 2), 1)
     share = C // ROWS
     for row in range(ROWS):
         d = product(wt1_ref, 0, 1, x_ref, row)
@@ -213,13 +209,15 @@
             for h in range(2):
                 activate(raw0_ref, h, c, inverse[h], gain_ref, t_ref)
             g2_ref[c : c + 1, :] = jnp.full((1, COLS), gain2_ref[c], F32)
-        for step in later[row * len(later) // ROWS : (row + 1) * len(later) // ROWS]:
-            step()
+        if row == 2:
+            others.wait()
+        if row >= 2:
+            for step in later[(row - 2) * len(later) // 6 : (row - 1) * len(later) // 6]:
+                step()
         o1_ref[row] = d
     for h in range(2):
         to_rows(t_ref, h, a0_ref)
-    for load in loads:
-        load.wait()
+    load.wait()
 
 
 def own_first(a0_ref, o1_ref, wt1_ref, w2_ref, m_ref, p0_ref, p1_ref, wt2_ref, x_ref):
@@ -246,34 +244,41 @@
         s_ref[row] = second_activation(o1_ref[row] + mask(m_ref, 3) * d, g_ref)
 
 
-def halo_middle(o0_ref, x_ref, wt_ref, m_ref, p_ref):
-    for row in range(ROWS):
-        p_ref[row] = o0_ref[row] + mask(m_ref, 0) * product(wt_ref, 1, 2, x_ref, row)
-
-
-def halo_second(h_ref, p_ref, wt_ref, g_ref, m_ref, s_ref, x_ref):
+def halo_middle(o0_ref, x_ref, wt1_ref, m_ref, s1_ref, wt2_ref, p_ref, q_ref, x1_ref):
+    clear_edges(x1_ref)
+    for row in range(ROWS):
+        p_ref[row] = o0_ref[row] + mask(m_ref, 0) * product(wt1_ref, 1, 2, x_ref, row)
+        put(x1_ref, s1_ref, row)
+    for row in range(ROWS):
+        q_ref[row] = product(wt2_ref, 0, 1, x1_ref, row)
+
+
+def halo_second(h_ref, p_ref, wt_ref, g_ref, m_ref, s_ref, end_ref, x_ref):
     clear_edges(x_ref)
     put(x_ref, h_ref, 0)
     put(x_ref, h_ref, 1)
     for row in range(ROWS):
         d = product(wt_ref, 2, 3, x_ref, row)
         put(x_ref, h_ref, row + 2)
-        s_ref[row] = second_activation(p_ref[row] + mask(m_ref, 1) * d, g_ref)
-
-
-def local_second(s0_ref, s1_ref, wt_ref, m_ref, o0_ref, o1_ref, x0_ref, x1_ref):
-    clear_edges(x0_ref)
-    put(x0_ref, s0_ref, 0)
-    put(x0_ref, s0_ref, 1)
-    for row in range(ROWS):
-        d = product(wt_ref, 0, 2, x0_ref, row)
-        put(x0_ref, s0_ref, row + 2)
-        put(x1_ref, s1_ref, row)
+        act = second_activation(p_ref[row] + mask(m_ref, 1) * d, g_ref)
+        if row < EARLY:
+            s_ref[row] = act
+        else:
+            end_ref[row - EARLY] = act
+
+
+def local_second(s0_ref, end_ref, p_ref, wt_ref, m_ref, o0_ref, o1_ref, x_ref):
+    clear_edges(x_ref)
+    put(x_ref, s0_ref, 0)
+    put(x_ref, s0_ref, 1)
+    for row in range(ROWS):
+        d = product(wt_ref, 0, 2, x_ref, row)
+        if row + 2 < EARLY:
+            put(x_ref, s0_ref, row + 2)
+        else:
+            put(x_ref, end_ref, row + 2, EARLY)
         o0_ref[row] = d[:C]
-        o1_ref[row] = mask(m_ref, 2) * d[C:]
-    clear_edges(x1_ref)
-    for row in range(ROWS):
-        o1_ref[row] += product(wt_ref, 0, 1, x1_ref, row)
+        o1_ref[row] = p_ref[row] + mask(m_ref, 2) * d[C:]
 
 
 def last_frame(h_ref, o0_ref, o1_ref, wt_ref, m_ref, p_ref, t_ref, x_ref):
@@ -287,33 +292,43 @@
         put_transposed(t_ref, row, o1_ref[row] + mask(m_ref, 3) * d[C:])
 
 
-def other_frame(
-    h_ref, p_ref, wt_ref, m_ref, t1_ref, f_ref, out_ref, t_ref, x_ref, buf0_ref, buf1_ref, sems0, sems1
-):
+def early_rows(h_ref, p_ref, wt_ref, m_ref, t1_ref, f_ref, t_ref, x_ref, out_ref, buf_ref, sems):
     clear_edges(x_ref)
     put(x_ref, h_ref, 0)
     put(x_ref, h_ref, 1)
-    share = C // ROWS
-    for row in range(ROWS):
+    rows = EARLY - 1
+    for row in range(rows):
         d = product(wt_ref, 2, 3, x_ref, row)
         put(x_ref, h_ref, row + 2)
-        for c in range(row * share, (row + 1) * share):
-            finish(t1_ref, f_ref, 1, c, buf1_ref)
+        for c in range(row * C // rows, (row + 1) * C // rows):
+            finish(t1_ref, f_ref, 1, c, buf_ref)
         put_transposed(t_ref, row, p_ref[row] + mask(m_ref, 1) * d)
-        if (row + 1) % (ROWS // PARTS) == 0:
-            out_copy(buf1_ref, out_ref, 1, row // (ROWS // PARTS), sems1).start()
+        for part in range(PARTS):
+            if row * C // rows < (part + 1) * C // PARTS <= (row + 1) * C // rows:
+                out_copy(buf_ref, out_ref, 1, part, sems).start()
+    for part in range(PARTS):
+        out_copy(buf_ref, out_ref, 1, part, sems).wait()
+
+
+def late_rows(
+    end_ref, p_ref, wt_ref, m_ref, f_ref, _, __, ___, t_ref, x_ref, out_ref, buf_ref, sems
+):
+    for row in range(EARLY, ROWS):
+        put(x_ref, end_ref, row, EARLY)
+    for row in range(EARLY - 1, ROWS):
+        d = product(wt_ref, 2, 3, x_ref, row)
+        put_transposed(t_ref, row, p_ref[row] + mask(m_ref, 1) * d)
     for part in range(PARTS):
 
         def step(b, _):
             for j in range(16):
-                finish(t_ref, f_ref, 0, part * (C // PARTS) + b * 16 + j, buf0_ref)
+                finish(t_ref, f_ref, 0, part * (C // PARTS) + b * 16 + j, buf_ref)
             return 0
 
         lax.fori_loop(0, C // PARTS // 16, step, 0)
-        out_copy(buf0_ref, out_ref, 0, part, sems0).start()
+        out_copy(buf_ref, out_ref, 0, part, sems).start()
     for part in range(PARTS):
-        out_copy(buf1_ref, out_ref, 1, part, sems1).wait()
-        out_copy(buf0_ref, out_ref, 0, part, sems0).wait()
+        out_copy(buf_ref, out_ref, 0, part, sems).wait()
 
 
 VM = pl.BlockSpec(memory_space=pltpu.VMEM)
@@ -327,6 +342,9 @@
 SEMS = pltpu.SemaphoreType.DMA((PARTS,))
 A_SUM = jax.ShapeDtypeStruct((ROWS, C, COLS), F32)
 A_ACT = jax.ShapeDtypeStruct((ROWS, C, COLS), BF16)
+A_EARLY = jax.ShapeDtypeStruct((EARLY, C, COLS), BF16)
+A_LATE = jax.ShapeDtypeStruct((ROWS - EARLY, C, COLS), BF16)
+A_FIRST = jax.ShapeDtypeStruct((DEPTH, C), BF16)
 A_RAW = jax.ShapeDtypeStruct((2, C, ROWS, HALF), BF16)
 A_SLABS = jax.ShapeDtypeStruct(((ROWS + 2) * SLAB, COLS), BF16)
 A_NATURAL = jax.ShapeDtypeStruct((2, C * ROWS, HALF), F32)
@@ -340,13 +358,14 @@
     return pltpu.with_memory_space_constraint(value, pltpu.HBM)
 
 
-def call(kernel, in_specs, out_shape, scratch=(), out_specs=None):
+def call(kernel, in_specs, out_shape, scratch=(), out_specs=None, aliases=None):
     return pl.pallas_call(
         kernel,
         in_specs=in_specs,
         out_specs=out_specs or jax.tree.map(lambda _: VM, out_shape),
         out_shape=out_shape,
         scratch_shapes=scratch,
+        input_output_aliases=aliases or {},
         compiler_params=pltpu.CompilerParams(vmem_limit_bytes=VMEM_LIMIT),
         name=kernel.__name__,
     )
@@ -356,31 +375,36 @@
     w1 = conv_first.reshape(TAPS * DEPTH, C)
     w2 = conv_second.reshape(TAPS * DEPTH, C)
 
-    a1, raw0 = call(
-        activate_last, [HBM, HBM], [A_ACT, A_RAW],
-        [RAW, GAIN, NATURAL, pltpu.SemaphoreType.DMA((5,)), pltpu.SemaphoreType.DMA((4,))],
-    )(stay(features), stay(gain_first))
+    a1, raw0, first = call(
+        activate_last, [HBM] * 3, [A_ACT, A_RAW, A_FIRST],
+        [RAW, GAIN, NATURAL, pltpu.SemaphoreType.DMA((6,)), pltpu.SemaphoreType.DMA((4,))],
+    )(stay(features), stay(w1), stay(gain_first))
     a_before = shifted(a1, "tm")
     a0, o1, wt1, w2, m, g2 = call(
-        own_last, [VM] * 3 + [HBM] * 4, [A_ACT, A_SUM, A_TURNED, A_WEIGHTS, A_MASKS, A_GAINS],
+        own_last, [VM] * 3 + [HBM] * 5, [A_ACT, A_SUM, A_TURNED, A_WEIGHTS, A_MASKS, A_GAINS],
         [
             GAIN, GAIN, pltpu.SMEM(video_frames.shape, jnp.int32), NATURAL, SLABS,
-            pltpu.SemaphoreType.DMA((6,)),
+            pltpu.VMEM((2 * DEPTH, C), BF16), pltpu.SemaphoreType.DMA((5,)),
         ],
-    )(a1, raw0, w1, stay(w2), stay(gain_first), stay(gain_second), stay(video_frames))
+    )(a1, raw0, first, stay(w1), stay(w2), stay(gain_first), stay(gain_second), stay(video_frames))
     a_earlier = shifted(a0, "tm")
     p0, p1, wt2 = call(own_first, [VM] * 5, [A_SUM, A_SUM, A_TURNED], [SLABS])(a0, o1, wt1, w2, m)
     s1, x = call(halo_first, [VM] * 5, [A_ACT, A_SLABS])(a_before, p1, wt1, g2, m)
     s_before = shifted(s1, "tm")
-    part = call(halo_middle, [VM] * 4, A_SUM)(p0, x, wt1, m)
-    s0 = call(halo_second, [VM] * 5, A_ACT, [SLABS])(a_earlier, part, wt1, g2, m)
+    part, q = call(halo_middle, [VM] * 6, [A_SUM, A_SUM], [SLABS])(p0, x, wt1, m, s1, wt2)
+    s0, end = call(halo_second, [VM] * 5, [A_EARLY, A_LATE], [SLABS])(a_earlier, part, wt1, g2, m)
     s_earlier = shifted(s0, "tm")
-    q0, q1 = call(local_second, [VM] * 4, [A_SUM, A_SUM], [SLABS, SLABS])(s0, s1, wt2, m)
+    s_end = shifted(end, "tm")
+    q0, q1 = call(local_second, [VM] * 5, [A_SUM, A_SUM], [SLABS])(s0, end, q, wt2, m)
     part2, t1 = call(last_frame, [VM] * 5, [A_SUM, A_NATURAL], [SLABS])(s_before, q0, q1, wt2, m)
+    whole = jax.ShapeDtypeStruct(features.shape, BF16)
+    t0, x0, out = call(
+        early_rows, [VM] * 6, [A_NATURAL, A_SLABS, whole], [FRAME, SEMS], [VM, VM, ANY]
+    )(s_earlier, part2, wt2, m, t1, features)
     return call(
-        other_frame, [VM] * 6, jax.ShapeDtypeStruct(features.shape, BF16),
-        [NATURAL, SLABS, FRAME, FRAME, SEMS, SEMS], out_specs=ANY,
-    )(s_earlier, part2, wt2, m, t1, features)
+        late_rows, [VM] * 7 + [ANY], [A_NATURAL, A_SLABS, whole], [FRAME, SEMS], [VM, VM, ANY],
+        {5: 0, 6: 1, 7: 2},
+    )(s_end, part2, wt2, m, features, t0, x0, out)[2]
 
 
 def solution(mesh):

time: 45.4 us -> 44.5 us (0.980)
  waiting for transfers between devices: 8.54 us -> 5.09 us
  starting transfers between devices: 9.44 us -> 12 us
  local copies, waits for them, and re-layouts: 1.75 us -> 0.01 us
  Pallas kernels: 25.1 us -> 26.3 us
    ppermute x4 -> x5, waiting for transfers between devices: 8.54 us -> 5.09 us  [shifted(): return lax.ppermute(value, axis, [(i, i + 1) for i in range(count - 1)])]
    ppermute x4 -> x5, starting transfers between devices: 9.44 us -> 12 us  [shifted(): return lax.ppermute(value, axis, [(i, i + 1) for i in range(count - 1)])]
    unnamed x4 -> x2, local copies, waits for them, and re-layouts: 1.75 us -> 0.01 us
    pallas_call x6 -> x7, Pallas kernels: 16.7 us -> 17.9 us  [the longest x1 3.56 us: per_device(): call(own_last, [VM] * 3 + [HBM] * 5, [A_ACT, A_SUM, A_TURNED, A_WEIGHTS,...]
  transfers between devices with their start and end apart: 4 -> 5, of which waited for: 3 -> 3; matrix products, arithmetic and copies ran while one was open for 0% -> 0% of each run, Pallas kernels for 44% -> 51%
where the time goes in v4:
time: 44.5 us; the launch traced here: 43.8 us
  Pallas kernels  26.3 us (59%)
  starting transfers between devices  12 us (27%)
  waiting for transfers between devices  5.09 us (11%)
    ppermute x5, starting transfers between devices, shifted(): return lax.ppermute(value, axis, [(i, i + 1) for i in range(count - 1)])  12 us
    ppermute x5, waiting for transfers between devices, shifted(): return lax.ppermute(value, axis, [(i, i + 1) for i in range(count - 1)])  5.09 us
    pallas_call x1, Pallas kernels, per_device(): call(own_last, [VM] * 3 + [HBM] * 5, [A_ACT, A_SUM, A_TURNED, A_WEIGHTS,...  3.56 us
    pallas_call x1, Pallas kernels, per_device(): call(last_frame, [VM] * 5, [A_SUM, A_NATURAL], [SLABS])  3.28 us
    pallas_call x1, Pallas kernels, per_device(): call(own_first, [VM] * 5, [A_SUM, A_SUM, A_TURNED], [SLABS])  3.18 us
    pallas_call x1, Pallas kernels, per_device(): call(local_second, [VM] * 5, [A_SUM, A_SUM], [SLABS])(s0, end, q, wt2, m)  3.15 us
    pallas_call x1, Pallas kernels, per_device(): call(halo_middle, [VM] * 6, [A_SUM, A_SUM], [SLABS])(p0, x, wt1, m, s1, wt2)  3.05 us
    pallas_call x1, Pallas kernels, per_device(): call(activate_last, [HBM] * 3, [A_ACT, A_RAW, A_FIRST], [RAW, GAIN, NATUR...  2.27 us
  transfers between devices with their start and end apart: 5, of which 3 were waited for; matrix products, arithmetic and copies ran while one was open for 0% of the time, Pallas kernels for 51%

profile of v4, /device:TPU:8, one launch (start us, length us, event | category | flops | bytes accessed | tf_op | source)
XLA Modules:
  0.0 43.8 jit_solution(9491762714972517732)
XLA Ops:
  0.0 2.3 %activate_last.1 = (bf16[8,192,256]{2,1,0:T(8,128)(2,1)S(1)}, bf16[2,192,8,128]{3,2,1,0:T(8,128)(2,1)S(1)}, bf16[1728,192]{1,0:T(8,128)(2,1)S(1)}) custom-call(bf16[2,192,8,256]{3,2,1,0:T(8,128)(2,1)} %f_ref.5, bf16[5184,192]{1,0:T(8,128)(2,1)} %bitcast.2, f32[192]{0:T(256)} %gain_any.3), custom_call_target="tpu_custom_call" | custom-call | tf_op jit(solution)/shard_map/activate_last/pallas_call | solution.py:378
  2.3 1.9 %collective-permute-start.1 = (bf16[8,192,256]{2,1,0:T(8,128)(2,1)S(1)}, bf16[8,192,256]{2,1,0:T(8,128)(2,1)S(1)}, u32[]{:S(2)}, u32[]{:S(2)}) collective-permute-start(bf16[8,192,256]{2,1,0:T(8,128)(2,1)S(1)} %get-tuple-element.31.a1_ref), channel_id=1, source_target_pairs={{0,1},{1,2},{2,3},{3,4},{4,5},{5,6},{6,7},{7,8},{8,9},{9,10},{10,1... | collective-permute-start | bytes 2359304 | tf_op jit(solution)/shard_map/ppermute | solution.py:26
  4.2 3.6 %own_last.1 = (bf16[8,192,256]{2,1,0:T(8,128)(2,1)S(1)}, f32[8,192,256]{2,1,0:T(8,128)S(1)}, bf16[576,1728]{1,0:T(8,128)(2,1)S(1)}, bf16[5184,192]{1,0:T(8,128)(...) custom-call(bf16[8,192,256]{2,1,0:T(8,128)(2,1)S(1)} %get-tuple-element.31.a1_ref, ...), custom_call_target="tpu_custom_call" | custom-call | tf_op jit(solution)/shard_map/own_last/pallas_call | solution.py:383
  7.8 3.5 %collective-permute-start = (bf16[8,192,256]{2,1,0:T(8,128)(2,1)S(1)}, bf16[8,192,256]{2,1,0:T(8,128)(2,1)S(1)}, u32[]{:S(2)}, u32[]{:S(2)}) collective-permute-start(bf16[8,192,256]{2,1,0:T(8,128)(2,1)S(1)} %get-tuple-element.34.a0_ref), channel_id=1, source_target_pairs={{0,1},{1,2},{2,3},{3,4},{4,5},{5,6},{6,7},{7,8},{8,9},{9,10},{10,1... | collective-permute-start | bytes 2359304 | tf_op jit(solution)/shard_map/ppermute | solution.py:26
  11.3 3.2 %own_first.1 = (f32[8,192,256]{2,1,0:T(8,128)S(1)}, f32[8,192,256]{2,1,0:T(8,128)S(1)}, bf16[576,1728]{1,0:T(8,128)(2,1)S(1)}) custom-call(bf16[8,192,256]{2,1,0:T(8,128)(2,1)S(1)} %get-tuple-element.34.a0_ref, f32[8,192,256]{2,1,0:T(8,128)S(1)} %get-tuple-element.35.o1_ref, bf16[576,1728]{1,0:T(8,128)(2,1)S(1)} %get-tuple-element.36.wt1_ref.wt_ref, ...), custom_call_target="tpu_custom_call" | custom-call | tf_op jit(solution)/shard_map/own_first/pallas_call | solution.py:391
  14.5 2.0 %collective-permute-done.1.h_ref = bf16[8,192,256]{2,1,0:T(8,128)(2,1)S(1)} collective-permute-done((bf16[8,192,256]{2,1,0:T(8,128)(2,1)S(1)}, bf16[8,192,256]{2,1,0:T(8,128)(2,1)S(1)}, u32[]{:S(2)}, u32[]{:S(2)}) %collective-permute-start.1) | collective-permute-done | bytes 786464 | tf_op jit(solution)/shard_map/ppermute | solution.py:26
  16.5 2.0 %halo_first.1 = (bf16[8,192,256]{2,1,0:T(8,128)(2,1)S(1)}, bf16[5760,256]{1,0:T(8,128)(2,1)S(1)}) custom-call(bf16[8,192,256]{2,1,0:T(8,128)(2,1)S(1)} %collective-permute-done.1.h_ref, f32[8,192,256]{2,1,0:T(8,128)S(1)} %get-tuple-element.40.o1_ref, bf16[576,1728]{1,0:T(8,128)(2,1)S(1)} %get-tuple-element.36.wt1_ref.wt_ref, ...), custom_call_target="tpu_custom_call" | custom-call | tf_op jit(solution)/shard_map/halo_first/pallas_call | solution.py:392
  18.5 2.1 %collective-permute-start.3 = (bf16[8,192,256]{2,1,0:T(8,128)(2,1)S(1)}, bf16[8,192,256]{2,1,0:T(8,128)(2,1)S(1)}, u32[]{:S(2)}, u32[]{:S(2)}) collective-permute-start(bf16[8,192,256]{2,1,0:T(8,128)(2,1)S(1)} %get-tuple-element.43.s1_ref), channel_id=1, source_target_pairs={{0,1},{1,2},{2,3},{3,4},{4,5},{5,6},{6,7},{7,8},{8,9},{9,10},{10,1... | collective-permute-start | bytes 2359304 | tf_op jit(solution)/shard_map/ppermute | solution.py:26
  20.6 3.1 %halo_middle.1 = (f32[8,192,256]{2,1,0:T(8,128)S(1)}, f32[8,192,256]{2,1,0:T(8,128)S(1)}) custom-call(f32[8,192,256]{2,1,0:T(8,128)S(1)} %get-tuple-element.39.o0_ref, bf16[5760,256]{1,0:T(8,128)(2,1)S(1)} %get-tuple-element.42.x_ref, bf16[576,1728]{1,0:T(8,128)(2,1)S(1)} %get-tuple-element.36.wt1_ref.wt_ref, f32[8,256]{1,0:T(8,128)S(1)} %get-tuple-element.38.m_ref, ...), custom_call_target="tpu_custom_call" | custom-call | tf_op jit(solution)/shard_map/halo_middle/pallas_call | solution.py:394
  23.6 1.3 %collective-permute-done.h_ref = bf16[8,192,256]{2,1,0:T(8,128)(2,1)S(1)} collective-permute-done((bf16[8,192,256]{2,1,0:T(8,128)(2,1)S(1)}, bf16[8,192,256]{2,1,0:T(8,128)(2,1)S(1)}, u32[]{:S(2)}, u32[]{:S(2)}) %collective-permute-start) | collective-permute-done | bytes 786464 | tf_op jit(solution)/shard_map/ppermute | solution.py:26
  24.9 1.9 %halo_second.1 = (bf16[6,192,256]{2,1,0:T(8,128)(2,1)S(1)}, bf16[2,192,256]{2,1,0:T(8,128)(2,1)S(1)}) custom-call(bf16[8,192,256]{2,1,0:T(8,128)(2,1)S(1)} %collective-permute-done.h_ref, f32[8,192,256]{2,1,0:T(8,128)S(1)} %get-tuple-element.45.p_ref, bf16[576,1728]{1,0:T(8,128)(2,1)S(1)} %get-tuple-element.36.wt1_ref.wt_ref, ...), custom_call_target="tpu_custom_call" | custom-call | tf_op jit(solution)/shard_map/halo_second/pallas_call | solution.py:395
  26.9 1.9 %collective-permute-start.4 = (bf16[6,192,256]{2,1,0:T(8,128)(2,1)S(1)}, bf16[6,192,256]{2,1,0:T(8,128)(2,1)S(1)}, u32[]{:S(2)}, u32[]{:S(2)}) collective-permute-start(bf16[6,192,256]{2,1,0:T(8,128)(2,1)S(1)} %get-tuple-element.47.s0_ref), channel_id=1, source_target_pairs={{0,1},{1,2},{2,3},{3,4},{4,5},{5,6},{6,7},{7,8},{8,9},{9,10},{10,1... | collective-permute-start | bytes 1769480 | tf_op jit(solution)/shard_map/ppermute | solution.py:26
  28.8 2.6 %collective-permute-start.2 = (bf16[2,192,256]{2,1,0:T(8,128)(2,1)S(1)}, bf16[2,192,256]{2,1,0:T(8,128)(2,1)S(1)}, u32[]{:S(2)}, u32[]{:S(2)}) collective-permute-start(bf16[2,192,256]{2,1,0:T(8,128)(2,1)S(1)} %get-tuple-element.46.end_ref), channel_id=1, source_target_pairs={{0,1},{1,2},{2,3},{3,4},{4,5},{5,6},{6,7},{7,8},{8,9},{9,10},{10,1... | collective-permute-start | bytes 589832 | tf_op jit(solution)/shard_map/ppermute | solution.py:26
  31.4 3.2 %local_second.1 = (f32[8,192,256]{2,1,0:T(8,128)S(1)}, f32[8,192,256]{2,1,0:T(8,128)S(1)}) custom-call(bf16[6,192,256]{2,1,0:T(8,128)(2,1)S(1)} %get-tuple-element.47.s0_ref, bf16[2,192,256]{2,1,0:T(8,128)(2,1)S(1)} %get-tuple-element.46.end_ref, f32[8,192,256]{2,1,0:T(8,128)S(1)} %get-tuple-element.48.p_ref, ...), custom_call_target="tpu_custom_call" | custom-call | tf_op jit(solution)/shard_map/local_second/pallas_call | solution.py:398
  34.6 0.0 collective-permute-done.3.h_ref
  34.6 0.0 copy-start
  34.6 3.3 %last_frame.1 = (f32[8,192,256]{2,1,0:T(8,128)S(1)}, f32[2,1536,128]{2,1,0:T(8,128)S(1)}) custom-call(bf16[8,192,256]{2,1,0:T(8,128)(2,1)S(1)} %collective-permute-done.3.h_ref, f32[8,192,256]{2,1,0:T(8,128)S(1)} %get-tuple-element.49.o0_ref, f32[8,192,256]{2,1,0:T(8,128)S(1)} %get-tuple-element.50.o1_ref, ...), custom_call_target="tpu_custom_call" | custom-call | tf_op jit(solution)/shard_map/last_frame/pallas_call | solution.py:399
  37.9 1.8 %collective-permute-done.4.h_ref = bf16[6,192,256]{2,1,0:T(8,128)(2,1)S(1)} collective-permute-done((bf16[6,192,256]{2,1,0:T(8,128)(2,1)S(1)}, bf16[6,192,256]{2,1,0:T(8,128)(2,1)S(1)}, u32[]{:S(2)}, u32[]{:S(2)}) %collective-permute-start.4) | collective-permute-done | bytes 589856 | tf_op jit(solution)/shard_map/ppermute | solution.py:26
  39.7 0.0 copy-done
  39.7 2.2 %early_rows.1 = (f32[2,1536,128]{2,1,0:T(8,128)S(1)}, bf16[5760,256]{1,0:T(8,128)(2,1)S(1)}, bf16[2,192,8,256]{3,2,1,0:T(8,128)(2,1)}) custom-call(bf16[6,192,256]{2,1,0:T(8,128)(2,1)S(1)} %collective-permute-done.4.h_ref, f32[8,192,256]{2,1,0:T(8,128)S(1)} %get-tuple-element.51.p_ref, bf16[576,1728]{1,0:T(8,128)(2,1)S(1)} %get-tuple-element.44.wt2_ref.wt_ref, ...), custom_call_target="tpu_custom_call" | custom-call | tf_op jit(solution)/shard_map/early_rows/pallas_call | solution.py:401
  41.9 0.0 collective-permute-done.2.end_ref
  41.9 1.7 %late_rows.1 = (f32[2,1536,128]{2,1,0:T(8,128)S(1)}, bf16[5760,256]{1,0:T(8,128)(2,1)S(1)}, bf16[2,192,8,256]{3,2,1,0:T(8,128)(2,1)}) custom-call(bf16[2,192,256]{2,1,0:T(8,128)(2,1)S(1)} %collective-permute-done.2.end_ref, f32[8,192,256]{2,1,0:T(8,128)S(1)} %get-tuple-element.51.p_ref, ...), custom_call_target="tpu_custom_call", output_to_operand_aliasing={{0}: (5, {}), {1}: (6, {}), {2}: (7, {})} | custom-call | tf_op jit(solution)/shard_map/late_rows/pallas_call | solution.py:404
Async XLA Ops:
  2.3 14.2 %collective-permute-start.1 = (bf16[8,192,256]{2,1,0:T(8,128)(2,1)S(1)}, bf16[8,192,256]{2,1,0:T(8,128)(2,1)S(1)}, u32[]{:S(2)}, u32[]{:S(2)}) collective-permute-start(bf16[8,192,256]{2,1,0:T(8,128)(2,1)S(1)} %get-tuple-element.31.a1_ref), channel_id=1, source_target_pairs={{0,1},{1,2},{2,3},{3,4},{4,5},{5,6},{6,7},{7,8},{8,9},{9,10},{10,1... | collective-permute-start | bytes 2359304 | tf_op jit(solution)/shard_map/ppermute | solution.py:26
  7.8 17.1 %collective-permute-start = (bf16[8,192,256]{2,1,0:T(8,128)(2,1)S(1)}, bf16[8,192,256]{2,1,0:T(8,128)(2,1)S(1)}, u32[]{:S(2)}, u32[]{:S(2)}) collective-permute-start(bf16[8,192,256]{2,1,0:T(8,128)(2,1)S(1)} %get-tuple-element.34.a0_ref), channel_id=1, source_target_pairs={{0,1},{1,2},{2,3},{3,4},{4,5},{5,6},{6,7},{7,8},{8,9},{9,10},{10,1... | collective-permute-start | bytes 2359304 | tf_op jit(solution)/shard_map/ppermute | solution.py:26
  18.5 16.1 %collective-permute-start.3 = (bf16[8,192,256]{2,1,0:T(8,128)(2,1)S(1)}, bf16[8,192,256]{2,1,0:T(8,128)(2,1)S(1)}, u32[]{:S(2)}, u32[]{:S(2)}) collective-permute-start(bf16[8,192,256]{2,1,0:T(8,128)(2,1)S(1)} %get-tuple-element.43.s1_ref), channel_id=1, source_target_pairs={{0,1},{1,2},{2,3},{3,4},{4,5},{5,6},{6,7},{7,8},{8,9},{9,10},{10,1... | collective-permute-start | bytes 2359304 | tf_op jit(solution)/shard_map/ppermute | solution.py:26
  26.9 12.8 %collective-permute-start.4 = (bf16[6,192,256]{2,1,0:T(8,128)(2,1)S(1)}, bf16[6,192,256]{2,1,0:T(8,128)(2,1)S(1)}, u32[]{:S(2)}, u32[]{:S(2)}) collective-permute-start(bf16[6,192,256]{2,1,0:T(8,128)(2,1)S(1)} %get-tuple-element.47.s0_ref), channel_id=1, source_target_pairs={{0,1},{1,2},{2,3},{3,4},{4,5},{5,6},{6,7},{7,8},{8,9},{9,10},{10,1... | collective-permute-start | bytes 1769480 | tf_op jit(solution)/shard_map/ppermute | solution.py:26
  28.8 13.1 %collective-permute-start.2 = (bf16[2,192,256]{2,1,0:T(8,128)(2,1)S(1)}, bf16[2,192,256]{2,1,0:T(8,128)(2,1)S(1)}, u32[]{:S(2)}, u32[]{:S(2)}) collective-permute-start(bf16[2,192,256]{2,1,0:T(8,128)(2,1)S(1)} %get-tuple-element.46.end_ref), channel_id=1, source_target_pairs={{0,1},{1,2},{2,3},{3,4},{4,5},{5,6},{6,7},{7,8},{8,9},{9,10},{10,1... | collective-permute-start | bytes 589832 | tf_op jit(solution)/shard_map/ppermute | solution.py:26
  34.6 5.1 %copy-start = (bf16[2,192,8,256]{3,2,1,0:T(8,128)(2,1)S(1)}, bf16[2,192,8,256]{3,2,1,0:T(8,128)(2,1)}, u32[]{:S(2)}) copy-start(bf16[2,192,8,256]{3,2,1,0:T(8,128)(2,1)} %f_ref.5) | copy-start | bytes 4718596

commit v5 on v3

v5 whole, which is shorter than its diff:
```python
import jax
import jax.numpy as jnp
from jax import lax
from jax.experimental import pallas as pl
from jax.experimental.pallas import tpu as pltpu
from jax.sharding import PartitionSpec as P

C = 192
ROWS = 8
COLS = 256
HALF = 128
TAPS = 3
SLAB = 3 * C
DEPTH = 9 * C
PIECE = 384
PARTS = 4
EPS = 1e-06
VMEM_LIMIT = 18 * 1024 * 1024
F32 = jnp.float32
BF16 = jnp.bfloat16


def shifted(value):
    return lax.ppermute(value, "tm", [(i, i + 1) for i in range(lax.axis_size("tm") - 1)])


def to_next_pair(value):
    return lax.ppermute(value, "tm", [(i, i + 1) for i in range(1, lax.axis_size("tm") - 1, 2)])


def within_pair(value):
    return lax.ppermute(value, "tm", [(i, i + 1) for i in range(0, lax.axis_size("tm"), 2)])


def tap_masks(frames_ref):
    first = 2 * lax.axis_index("tm")

    def step(v, carry):
        begin, start0, start1 = carry
        start0 = jnp.where(begin <= first, begin, start0)
        start1 = jnp.where(begin <= first + 1, begin, start1)
        return begin + frames_ref[v], start0, start1

    zero = jnp.int32(0)
    _, start0, start1 = lax.fori_loop(0, frames_ref.shape[0], step, (zero, zero, zero))
    return tuple(
        jnp.where(test, 1.0, 0.0).astype(F32)
        for test in (
            first - 1 >= start0,
            first - 2 >= start0,
            first >= start1,
            first - 1 >= start1,
        )
    )


def mask(m_ref, i):
    return m_ref[i : i + 1, :]


def turn_pieces(w_ref, wt_ref, taps, start=0):
    def turn(k, lo, hi):
        base = (k - start) * DEPTH
        wt_ref[k * C : (k + 1) * C, lo:hi] = w_ref[base + lo : base + hi, :].T

    return [
        (lambda k=k, lo=lo: turn(k, lo, min(lo + PIECE, DEPTH)))
        for k in taps
        for lo in range(0, DEPTH, PIECE)
    ]


def put_row(x_ref, row, values):
    base = (row + 1) * SLAB
    cols = lax.broadcasted_iota(jnp.int32, (C, COLS), 1)
    left = jnp.where(cols == 0, 0.0, pltpu.roll(values, 1, 1))
    right = jnp.where(cols == COLS - 1, 0.0, pltpu.roll(values, COLS - 1, 1))
    x_ref[base : base + C, :] = left.astype(BF16)
    x_ref[base + C : base + 2 * C, :] = values.astype(BF16)
    x_ref[base + 2 * C : base + 3 * C, :] = right.astype(BF16)


def clear_edges(x_ref):
    zeros = jnp.zeros((SLAB, COLS), BF16)
    x_ref[0:SLAB, :] = zeros
    x_ref[(ROWS + 1) * SLAB : (ROWS + 2) * SLAB, :] = zeros


def put(x_ref, a_ref, row):
    if row < ROWS:
        put_row(x_ref, row, a_ref[row].astype(F32))


def put_either(x_ref, far_ref, near_ref, row):
    if row < ROWS:
        put_row(x_ref, row, far_ref[row].astype(F32) + near_ref[row].astype(F32))


def product(wt_ref, lo, hi, x_ref, row):
    return jnp.dot(
        wt_ref[lo * C : hi * C, :],
        x_ref[row * SLAB : row * SLAB + DEPTH, :],
        preferred_element_type=F32,
    )


def sends_far():
    return lax.rem(lax.axis_index("tm"), 2) == 1


def inverse_rms(raw_ref, h):
    cols = slice(h * HALF, (h + 1) * HALF)

    def squares(b, total):
        v = raw_ref[pl.ds(b * 16, 16), :, cols].astype(F32)
        return total + jnp.sum(v * v, axis=0)

    total = lax.fori_loop(0, C // 16, squares, jnp.zeros((ROWS, HALF), F32))
    return lax.rsqrt(total * (1.0 / C) + EPS)


def activate(raw_ref, h, c, inverse, gain, t_ref):
    u = raw_ref[c, :, h * HALF : (h + 1) * HALF].astype(F32) * inverse * gain
    t_ref[h, c * ROWS : (c + 1) * ROWS, :] = u * jax.nn.sigmoid(u)


def row_of(t_ref, h, row):
    return t_ref[h, pl.ds(row, C, stride=ROWS), :]


def to_rows(t_ref, h, a_ref):
    for row in range(ROWS):
        a_ref[row, :, h * HALF : (h + 1) * HALF] = row_of(t_ref, h, row).astype(BF16)


def frame_copies(f_ref, index, raw_ref, sems):
    return [
        [
            pltpu.make_async_copy(
                f_ref.at[index, pl.ds(q * C // 2, C // 2), :, pl.ds(h * HALF, HALF)],
                raw_ref.at[pl.ds(q * C // 2, C // 2), :, pl.ds(h * HALF, HALF)],
                sems.at[2 * h + q],
            )
            for q in range(2)
        ]
        for h in range(2)
    ]


def first_tap(w1_any, w_ref, sem):
    return pltpu.make_async_copy(w1_any.at[pl.ds(0, DEPTH)], w_ref, sem)


def flat(copies):
    return copies[0] + copies[1]


def activate_frame(raw_ref, gain, t_ref, a_ref, before=None, extra=None):
    for h in range(2):
        if before:
            before(h)
        inverse = inverse_rms(raw_ref, h)
        for c in range(C):
            activate(raw_ref, h, c, inverse, gain(c), t_ref)
            if extra and h == 0:
                extra(c)
        to_rows(t_ref, h, a_ref)


def waits(copies):
    def wait(h):
        for copy in copies[h]:
            copy.wait()

    return wait


def first_sent(
    f_ref, w1_any, gain_any, a_ref, raw0_ref, w_ref, g1_ref, raw1_ref, gain_ref, t_ref, sems, sems0
):
    @pl.when(sends_far())
    def _():
        copies = frame_copies(f_ref, 1, raw1_ref, sems)
        gains = pltpu.make_async_copy(gain_any, gain_ref, sems.at[4])
        later = [first_tap(w1_any, w_ref, sems.at[5])] + flat(frame_copies(f_ref, 0, raw0_ref, sems0))
        for copy in copies[0] + [gains] + copies[1] + later:
            copy.start()

        def before(h):
            waits(copies)(h)
            if h == 0:
                gains.wait()

        def spread(c):
            g1_ref[c : c + 1, :] = jnp.full((1, HALF), gain_ref[c], F32)

        activate_frame(raw1_ref, lambda c: gain_ref[c], t_ref, a_ref, before, spread)
        for copy in later:
            copy.wait()


def rest_sent(
    a_ref, raw0_ref, g1_ref, _, f_ref, w1_any, gain_any,
    first_ref, a0_ref, a1_ref, gain_ref, raw_ref, last_ref, t_ref, sems, sems0, sems1,
):
    far = sends_far()

    @pl.when(far)
    def _():
        a1_ref[...] = a_ref[...]
        activate_frame(raw0_ref, lambda c: g1_ref[c : c + 1, :], t_ref, a0_ref)

    @pl.when(jnp.logical_not(far))
    def _():
        gains = pltpu.make_async_copy(gain_any, gain_ref, sems.at[0])
        first = first_tap(w1_any, first_ref, sems.at[1])
        last = frame_copies(f_ref, 1, last_ref, sems1)
        other = frame_copies(f_ref, 0, raw_ref, sems0)
        for copy in last[0] + [gains] + last[1] + flat(other) + [first]:
            copy.start()
        gains.wait()
        activate_frame(last_ref, lambda c: gain_ref[c], t_ref, a1_ref, waits(last))
        activate_frame(raw_ref, lambda c: gain_ref[c], t_ref, a0_ref, waits(other))
        first.wait()


def second_activation(values, g_ref):
    mean_square = jnp.sum(values * values, axis=0, keepdims=True) * (1.0 / C)
    u = values * lax.rsqrt(mean_square + EPS) * g_ref[...]
    return (u * jax.nn.sigmoid(u)).astype(BF16)


def put_transposed(t_ref, row, values):
    t_ref[0, pl.ds(row, C, stride=ROWS), :] = values[:, :HALF]
    t_ref[1, pl.ds(row, C, stride=ROWS), :] = values[:, HALF:]


def finish(t_ref, f_ref, index, c, buf_ref):
    at = c * ROWS if isinstance(c, int) else pl.multiple_of(c * ROWS, ROWS)
    v = jnp.concatenate([t_ref[h, pl.ds(at, ROWS), :] for h in range(2)], axis=1)
    buf_ref[c] = (f_ref[index, c].astype(F32) + v).astype(BF16)


def out_copy(buf_ref, out_ref, index, part, sems):
    span = pl.ds(part * (C // PARTS), C // PARTS)
    return pltpu.make_async_copy(buf_ref.at[span], out_ref.at[index, span], sems.at[part])


def own_frames(
    a0_ref, a1_ref, first_ref, w1_any, w2_any, gain2_any, frames_any,
    p1_ref, wt1_ref, wt2_ref, m_ref, g2_ref, x0_ref,
    gain2_ref, frames_ref, x1_ref, w1_ref, w2_ref, sems,
):
    small = [
        pltpu.make_async_copy(frames_any, frames_ref, sems.at[0]),
        pltpu.make_async_copy(gain2_any, gain2_ref, sems.at[1]),
    ]
    others = pltpu.make_async_copy(w1_any.at[pl.ds(DEPTH, 2 * DEPTH)], w1_ref, sems.at[2])
    load = pltpu.make_async_copy(w2_any, w2_ref, sems.at[3])
    for copy in small + [others, load]:
        copy.start()
    for step in turn_pieces(first_ref, wt1_ref, (0,)):
        step()
    clear_edges(x1_ref)
    clear_edges(x0_ref)
    put(x1_ref, a1_ref, 0)
    put(x1_ref, a1_ref, 1)
    turn1 = turn_pieces(w1_ref, wt1_ref, (1, 2), 1)
    share = C // ROWS
    for row in range(ROWS):
        d = product(wt1_ref, 0, 1, x1_ref, row)
        put(x1_ref, a1_ref, row + 2)
        put(x0_ref, a0_ref, row)
        if row == 2:
            others.wait()
            for copy in small:
                copy.wait()
            masks = tap_masks(frames_ref)
            for i in range(8):
                m_ref[i : i + 1, :] = jnp.full((1, COLS), masks[i % 4], F32)
        if row >= 2:
            for step in turn1[(row - 2) * len(turn1) // 6 : (row - 1) * len(turn1) // 6]:
                step()
        p1_ref[row] = d
    load.wait()
    turn2 = turn_pieces(w2_ref, wt2_ref, (0, 1, 2))
    for row in range(ROWS):
        d = product(wt1_ref, 1, 2, x0_ref, row)
        for c in range(row * share, (row + 1) * share):
            g2_ref[c : c + 1, :] = jnp.full((1, COLS), gain2_ref[c], F32)
        for step in turn2[row * len(turn2) // ROWS : (row + 1) * len(turn2) // ROWS]:
            step()
        p1_ref[row] += mask(m_ref, 2) * d


def halo_first(far_ref, near_ref, o1_ref, wt_ref, g_ref, m_ref, s_ref, x_ref):
    clear_edges(x_ref)
    put_either(x_ref, far_ref, near_ref, 0)
    put_either(x_ref, far_ref, near_ref, 1)
    for row in range(ROWS):
        d = product(wt_ref, 2, 3, x_ref, row)
        put_either(x_ref, far_ref, near_ref, row + 2)
        s_ref[row] = second_activation(o1_ref[row] + mask(m_ref, 3) * d, g_ref)


def halo_middle(x0_ref, x_ref, wt1_ref, m_ref, s1_ref, wt2_ref, p_ref, q_ref, x1_ref):
    clear_edges(x1_ref)
    for row in range(ROWS):
        d = mask(m_ref, 0) * product(wt1_ref, 1, 2, x_ref, row)
        put(x1_ref, s1_ref, row)
        p_ref[row] = d + product(wt1_ref, 0, 1, x0_ref, row)
    for row in range(ROWS):
        q_ref[row] = product(wt2_ref, 0, 1, x1_ref, row)


def halo_second(h_ref, p_ref, wt_ref, g_ref, m_ref, s_ref, x_ref):
    clear_edges(x_ref)
    put(x_ref, h_ref, 0)
    put(x_ref, h_ref, 1)
    for row in range(ROWS):
        d = product(wt_ref, 2, 3, x_ref, row)
        put(x_ref, h_ref, row + 2)
        s_ref[row] = second_activation(p_ref[row] + mask(m_ref, 1) * d, g_ref)


def local_second(s0_ref, p_ref, wt_ref, m_ref, o0_ref, o1_ref, x_ref):
    clear_edges(x_ref)
    put(x_ref, s0_ref, 0)
    put(x_ref, s0_ref, 1)
    for row in range(ROWS):
        d = product(wt_ref, 0, 2, x_ref, row)
        put(x_ref, s0_ref, row + 2)
        o0_ref[row] = d[:C]
        o1_ref[row] = p_ref[row] + mask(m_ref, 2) * d[C:]


def last_frame(h_ref, o0_ref, o1_ref, wt_ref, m_ref, p_ref, t_ref, x_ref):
    clear_edges(x_ref)
    put(x_ref, h_ref, 0)
    put(x_ref, h_ref, 1)
    for row in range(ROWS):
        d = product(wt_ref, 1, 3, x_ref, row)
        put(x_ref, h_ref, row + 2)
        p_ref[row] = o0_ref[row] + mask(m_ref, 0) * d[:C]
        put_transposed(t_ref, row, o1_ref[row] + mask(m_ref, 3) * d[C:])


def other_frame(
    h_ref, p_ref, wt_ref, m_ref, t1_ref, f_ref, out_ref, t_ref, x_ref, buf0_ref, buf1_ref, sems0, sems1
):
    clear_edges(x_ref)
    put(x_ref, h_ref, 0)
    put(x_ref, h_ref, 1)
    share = C // ROWS
    for row in range(ROWS):
        d = product(wt_ref, 2, 3, x_ref, row)
        put(x_ref, h_ref, row + 2)
        for c in range(row * share, (row + 1) * share):
            finish(t1_ref, f_ref, 1, c, buf1_ref)
        put_transposed(t_ref, row, p_ref[row] + mask(m_ref, 1) * d)
        if (row + 1) % (ROWS // PARTS) == 0:
            out_copy(buf1_ref, out_ref, 1, row // (ROWS // PARTS), sems1).start()
    for part in range(PARTS):

        def step(b, _):
            for j in range(16):
                finish(t_ref, f_ref, 0, part * (C // PARTS) + b * 16 + j, buf0_ref)
            return 0

        lax.fori_loop(0, C // PARTS // 16, step, 0)
        out_copy(buf0_ref, out_ref, 0, part, sems0).start()
    for part in range(PARTS):
        out_copy(buf1_ref, out_ref, 1, part, sems1).wait()
        out_copy(buf0_ref, out_ref, 0, part, sems0).wait()


VM = pl.BlockSpec(memory_space=pltpu.VMEM)
ANY = pl.BlockSpec(memory_space=pl.ANY)
HBM = pl.BlockSpec(memory_space=pltpu.HBM)
NATURAL = pltpu.VMEM((2, C * ROWS, HALF), F32)
RAW = pltpu.VMEM((C, ROWS, COLS), BF16)
SLABS = pltpu.VMEM(((ROWS + 2) * SLAB, COLS), BF16)
FRAME = pltpu.VMEM((C, ROWS, COLS), BF16)
GAIN = pltpu.SMEM((C,), F32)
SEMS = pltpu.SemaphoreType.DMA((PARTS,))
A_SUM = jax.ShapeDtypeStruct((ROWS, C, COLS), F32)
A_ACT = jax.ShapeDtypeStruct((ROWS, C, COLS), BF16)
A_FIRST = jax.ShapeDtypeStruct((DEPTH, C), BF16)
A_RAW = jax.ShapeDtypeStruct((C, ROWS, COLS), BF16)
A_SLABS = jax.ShapeDtypeStruct(((ROWS + 2) * SLAB, COLS), BF16)
A_NATURAL = jax.ShapeDtypeStruct((2, C * ROWS, HALF), F32)
A_TURNED = jax.ShapeDtypeStruct((TAPS * C, DEPTH), BF16)
A_MASKS = jax.ShapeDtypeStruct((8, COLS), F32)
A_GAINS = jax.ShapeDtypeStruct((C, COLS), F32)
A_HALF_GAINS = jax.ShapeDtypeStruct((C, HALF), F32)


def stay(value):
    return pltpu.with_memory_space_constraint(value, pltpu.HBM)


def call(kernel, in_specs, out_shape, scratch=(), out_specs=None, aliases=None):
    return pl.pallas_call(
        kernel,
        in_specs=in_specs,
        out_specs=out_specs or jax.tree.map(lambda _: VM, out_shape),
        out_shape=out_shape,
        scratch_shapes=scratch,
        input_output_aliases=aliases or {},
        compiler_params=pltpu.CompilerParams(vmem_limit_bytes=VMEM_LIMIT),
        cost_estimate=pl.CostEstimate(flops=3 * 10**10, bytes_accessed=10**7, transcendentals=0),
        name=kernel.__name__,
    )


def per_device(features, video_frames, gain_first, conv_first, gain_second, conv_second):
    w1 = conv_first.reshape(TAPS * DEPTH, C)
    w2 = conv_second.reshape(TAPS * DEPTH, C)

    a1, raw0, first, g1 = call(
        first_sent, [HBM] * 3, [A_ACT, A_RAW, A_FIRST, A_HALF_GAINS],
        [RAW, GAIN, NATURAL, pltpu.SemaphoreType.DMA((6,)), pltpu.SemaphoreType.DMA((4,))],
    )(stay(features), stay(w1), stay(gain_first))
    a_far = to_next_pair(a1)
    first, a0, a1 = call(
        rest_sent, [VM] * 4 + [HBM] * 3, [A_FIRST, A_ACT, A_ACT],
        [
            GAIN, RAW, RAW, NATURAL, pltpu.SemaphoreType.DMA((2,)),
            pltpu.SemaphoreType.DMA((4,)), pltpu.SemaphoreType.DMA((4,)),
        ],
        aliases={3: 0},
    )(a1, raw0, g1, first, stay(features), stay(w1), stay(gain_first))
    a_earlier = shifted(a0)
    a_near = within_pair(a1)
    p1, wt1, wt2, m, g2, x0 = call(
        own_frames, [VM] * 3 + [HBM] * 4, [A_SUM, A_TURNED, A_TURNED, A_MASKS, A_GAINS, A_SLABS],
        [
            GAIN, pltpu.SMEM(video_frames.shape, jnp.int32), SLABS,
            pltpu.VMEM((2 * DEPTH, C), BF16), pltpu.VMEM((TAPS * DEPTH, C), BF16),
            pltpu.SemaphoreType.DMA((4,)),
        ],
    )(a0, a1, first, stay(w1), stay(w2), stay(gain_second), stay(video_frames))
    s1, x = call(halo_first, [VM] * 6, [A_ACT, A_SLABS])(a_far, a_near, p1, wt1, g2, m)
    s_before = shifted(s1)
    part, q = call(halo_middle, [VM] * 6, [A_SUM, A_SUM], [SLABS])(x0, x, wt1, m, s1, wt2)
    s0 = call(halo_second, [VM] * 5, A_ACT, [SLABS])(a_earlier, part, wt1, g2, m)
    s_earlier = shifted(s0)
    q0, q1 = call(local_second, [VM] * 4, [A_SUM, A_SUM], [SLABS])(s0, q, wt2, m)
    part2, t1 = call(last_frame, [VM] * 5, [A_SUM, A_NATURAL], [SLABS])(s_before, q0, q1, wt2, m)
    return call(
        other_frame, [VM] * 6, jax.ShapeDtypeStruct(features.shape, BF16),
        [NATURAL, SLABS, FRAME, FRAME, SEMS, SEMS], out_specs=ANY,
    )(s_earlier, part2, wt2, m, t1, features)


def solution(mesh):
    in_specs = (P(("group", "tm"), None, None, None), P("group"), P(), P(), P(), P())
    out_specs = P(("group", "tm"), None, None, None)
    return jax.shard_map(
        per_device, mesh=mesh, in_specs=in_specs, out_specs=out_specs, check_vma=False
    )
```

time: 45.4 us -> 43.3 us (0.954)
  waiting for transfers between devices: 8.54 us -> 3.96 us
  starting transfers between devices: 9.44 us -> 12.6 us
  local copies, waits for them, and re-layouts: 1.75 us -> 0.01 us
  Pallas kernels: 25.1 us -> 26.2 us
    ppermute x4 -> x5, waiting for transfers between devices: 8.54 us -> 3.96 us  [the longest x3 3.96 us: shifted(): lax.ppermute(value, 'tm', [(i, i + 1) for i in range(lax.axis_size('tm')...]
    ppermute x4 -> x5, starting transfers between devices: 9.44 us -> 12.6 us  [the longest x3 7.8 us: shifted(): lax.ppermute(value, 'tm', [(i, i + 1) for i in range(lax.axis_size('tm')...]
    unnamed x4 -> x2, local copies, waits for them, and re-layouts: 1.75 us -> 0.01 us
    pallas_call x6, Pallas kernels: 16.9 us -> 17.9 us  [the longest x1 4.72 us: per_device(): call(own_frames, [VM] * 3 + [HBM] * 4, [A_SUM, A_TURNED, A_TURNED, A_MASK...]
  transfers between devices with their start and end apart: 4 -> 5, of which waited for: 3 -> 1; matrix products, arithmetic and copies ran while one was open for 0% -> 0% of each run, Pallas kernels for 44% -> 54%
where the time goes in v5:
time: 43.3 us; the launch traced here: 43.1 us
  Pallas kernels  26.2 us (61%)
  starting transfers between devices  12.6 us (29%)
  waiting for transfers between devices  3.96 us (9%)
    ppermute x3, starting transfers between devices, shifted(): lax.ppermute(value, 'tm', [(i, i + 1) for i in range(lax.axis_size('tm')...  7.8 us
    pallas_call x1, Pallas kernels, per_device(): call(own_frames, [VM] * 3 + [HBM] * 4, [A_SUM, A_TURNED, A_TURNED, A_MASK...  4.72 us
    pallas_call x1, Pallas kernels, per_device(): call(halo_middle, [VM] * 6, [A_SUM, A_SUM], [SLABS])(x0, x, wt1, m, s1, wt2)  4.47 us
    ppermute x3, waiting for transfers between devices, shifted(): lax.ppermute(value, 'tm', [(i, i + 1) for i in range(lax.axis_size('tm')...  3.96 us
    ppermute x1, starting transfers between devices, within_pair(): lax.ppermute(value, 'tm', [(i, i + 1) for i in range(0, lax.axis_size('tm...  3.55 us
    pallas_call x1, Pallas kernels, per_device(): call(rest_sent, [VM] * 4 + [HBM] * 3, [A_FIRST, A_ACT, A_ACT], [GAIN, RAW...  3.52 us
    pallas_call x1, Pallas kernels, per_device(): call(last_frame, [VM] * 5, [A_SUM, A_NATURAL], [SLABS])  3.28 us
    pallas_call x1, Pallas kernels, per_device(): call(local_second, [VM] * 4, [A_SUM, A_SUM], [SLABS])(s0, q, wt2, m)  3.15 us
  transfers between devices with their start and end apart: 5, of which 1 were waited for; matrix products, arithmetic and copies ran while one was open for 0% of the time, Pallas kernels for 54%

profile of v5, /device:TPU:8, one launch (start us, length us, event | category | flops | bytes accessed | tf_op | source)
XLA Modules:
  0.0 43.1 jit_solution(10888914991452762333)
XLA Ops:
  0.0 0.1 first_sent.1
  0.1 1.3 %collective-permute-start.1 = (bf16[8,192,256]{2,1,0:T(8,128)(2,1)S(1)}, bf16[8,192,256]{2,1,0:T(8,128)(2,1)S(1)}, u32[]{:S(2)}, u32[]{:S(2)}) collective-permute-start(bf16[8,192,256]{2,1,0:T(8,128)(2,1)S(1)} %get-tuple-element.26.a_ref), channel_id=1, source_target_pairs={{1,2},{3,4},{5,6},{7,8},{9,10},{11,12},{13,14},{17,18},{19,20},{21... | collective-permute-start | bytes 2359304 | tf_op jit(solution)/shard_map/ppermute | solution.py:28
  1.4 3.5 %rest_sent.1 = (bf16[1728,192]{1,0:T(8,128)(2,1)S(1)}, bf16[8,192,256]{2,1,0:T(8,128)(2,1)S(1)}, bf16[8,192,256]{2,1,0:T(8,128)(2,1)S(1)}) custom-call(bf16[8,192,256]{2,1,0:T(8,128)(2,1)S(1)} %get-tuple-element.26.a_ref, bf16[192,8,256]{2,1,0:T(8,128)(2,1)S(1)} %get-tuple-element.27.raw0_ref, ...), custom_call_target="tpu_custom_call", output_to_operand_aliasing={{0}: (3, {})} | custom-call | flops 30000001024 | bytes 10000000 | tf_op jit(solution)/shard_map/rest_sent/pallas_call | solution.py:425
  4.9 1.9 %collective-permute-start = (bf16[8,192,256]{2,1,0:T(8,128)(2,1)S(1)}, bf16[8,192,256]{2,1,0:T(8,128)(2,1)S(1)}, u32[]{:S(2)}, u32[]{:S(2)}) collective-permute-start(bf16[8,192,256]{2,1,0:T(8,128)(2,1)S(1)} %get-tuple-element.30.a0_ref), channel_id=1, source_target_pairs={{0,1},{1,2},{2,3},{3,4},{4,5},{5,6},{6,7},{7,8},{8,9},{9,10},{10,1... | collective-permute-start | bytes 2359304 | tf_op jit(solution)/shard_map/ppermute | solution.py:24
  6.9 3.5 %collective-permute-start.2 = (bf16[8,192,256]{2,1,0:T(8,128)(2,1)S(1)}, bf16[8,192,256]{2,1,0:T(8,128)(2,1)S(1)}, u32[]{:S(2)}, u32[]{:S(2)}) collective-permute-start(bf16[8,192,256]{2,1,0:T(8,128)(2,1)S(1)} %get-tuple-element.31.a1_ref), channel_id=1, source_target_pairs={{0,1},{2,3},{4,5},{6,7},{8,9},{10,11},{12,13},{14,15},{16,17},{18,... | collective-permute-start | bytes 2359304 | tf_op jit(solution)/shard_map/ppermute | solution.py:32
  10.4 4.7 %own_frames.1 = (f32[8,192,256]{2,1,0:T(8,128)S(1)}, bf16[576,1728]{1,0:T(8,128)(2,1)S(1)}, bf16[576,1728]{1,0:T(8,128)(2,1)S(1)}, f32[8,256]{1,0:T(8,128)S(1)},...) custom-call(bf16[8,192,256]{2,1,0:T(8,128)(2,1)S(1)} %get-tuple-element.30.a0_ref, ...), custom_call_target="tpu_custom_call" | custom-call | flops 30000001024 | bytes 10000000 | tf_op jit(solution)/shard_map/own_frames/pallas_call | solution.py:435
  15.1 0.0 collective-permute-done.2.near_ref
  15.1 0.0 collective-permute-done.1.far_ref
  15.2 2.0 %halo_first.1 = (bf16[8,192,256]{2,1,0:T(8,128)(2,1)S(1)}, bf16[5760,256]{1,0:T(8,128)(2,1)S(1)}) custom-call(bf16[8,192,256]{2,1,0:T(8,128)(2,1)S(1)} %collective-permute-done.1.far_ref, bf16[8,192,256]{2,1,0:T(8,128)(2,1)S(1)} %collective-permute-done.2.near_ref, f32[8,192,256]{2,1,0:T(8,128)S(1)} %get-tuple-element.34.o1_ref, ...), custom_call_target="tpu_custom_call" | custom-call | flops 30000001024 | bytes 10000000 | tf_op jit(solution)/shard_map/halo_first/pallas_call | solution.py:443
  17.2 2.1 %collective-permute-start.4 = (bf16[8,192,256]{2,1,0:T(8,128)(2,1)S(1)}, bf16[8,192,256]{2,1,0:T(8,128)(2,1)S(1)}, u32[]{:S(2)}, u32[]{:S(2)}) collective-permute-start(bf16[8,192,256]{2,1,0:T(8,128)(2,1)S(1)} %get-tuple-element.39.s1_ref), channel_id=1, source_target_pairs={{0,1},{1,2},{2,3},{3,4},{4,5},{5,6},{6,7},{7,8},{8,9},{9,10},{10,1... | collective-permute-start | bytes 2359304 | tf_op jit(solution)/shard_map/ppermute | solution.py:24
  19.3 4.5 %halo_middle.1 = (f32[8,192,256]{2,1,0:T(8,128)S(1)}, f32[8,192,256]{2,1,0:T(8,128)S(1)}) custom-call(bf16[5760,256]{1,0:T(8,128)(2,1)S(1)} %get-tuple-element.33.x0_ref, bf16[5760,256]{1,0:T(8,128)(2,1)S(1)} %get-tuple-element.38.x_ref, bf16[576,1728]{1,0:T(8,128)(2,1)S(1)} %get-tuple-element.35.wt_ref.wt1_ref, f32[8,256]{1,0:T(8,128)S(1)} %get-tuple-element.37.m_ref, ...), custom_call_target="tpu_custom_call" | custom-call | flops 30000001024 | bytes 10000000 | tf_op jit(solution)/shard_map/halo_middle/pallas_call | solution.py:445
  23.7 0.0 collective-permute-done.h_ref
  23.8 1.9 %halo_second.1.s0_ref = bf16[8,192,256]{2,1,0:T(8,128)(2,1)S(1)} custom-call(bf16[8,192,256]{2,1,0:T(8,128)(2,1)S(1)} %collective-permute-done.h_ref, f32[8,192,256]{2,1,0:T(8,128)S(1)} %get-tuple-element.41.p_ref, bf16[576,1728]{1,0:T(8,128)(2,1)S(1)} %get-tuple-element.35.wt_ref.wt1_ref, f32[192,256]{1,0:T(8,128)S(1)} %get-tuple-element.36.g_ref, ...), custom_call_target="tpu_custom_call" | custom-call | flops 30000001024 | bytes 10000000 | tf_op jit(solution)/shard_map/halo_second/pallas_call | solution.py:446
  25.7 3.8 %collective-permute-start.3 = (bf16[8,192,256]{2,1,0:T(8,128)(2,1)S(1)}, bf16[8,192,256]{2,1,0:T(8,128)(2,1)S(1)}, u32[]{:S(2)}, u32[]{:S(2)}) collective-permute-start(bf16[8,192,256]{2,1,0:T(8,128)(2,1)S(1)} %halo_second.1.s0_ref), channel_id=1, source_target_pairs={{0,1},{1,2},{2,3},{3,4},{4,5},{5,6},{6,7},{7,8},{8,9},{9,10},{10,1... | collective-permute-start | bytes 2359304 | tf_op jit(solution)/shard_map/ppermute | solution.py:24
  29.5 3.1 %local_second.1 = (f32[8,192,256]{2,1,0:T(8,128)S(1)}, f32[8,192,256]{2,1,0:T(8,128)S(1)}) custom-call(bf16[8,192,256]{2,1,0:T(8,128)(2,1)S(1)} %halo_second.1.s0_ref, f32[8,192,256]{2,1,0:T(8,128)S(1)} %get-tuple-element.42.p_ref, bf16[576,1728]{1,0:T(8,128)(2,1)S(1)} %get-tuple-element.40.wt2_ref.wt_ref, f32[8,256]{1,0:T(8,128)S(1)} %get-tuple-element.37.m_ref), custom_call_target="tpu_custom_call" | custom-call | flops 30000001024 | bytes 10000000 | tf_op jit(solution)/shard_map/local_second/pallas_call | solution.py:448
  32.6 0.0 collective-permute-done.4.h_ref
  32.6 0.0 copy-start
  32.7 3.3 %last_frame.1 = (f32[8,192,256]{2,1,0:T(8,128)S(1)}, f32[2,1536,128]{2,1,0:T(8,128)S(1)}) custom-call(bf16[8,192,256]{2,1,0:T(8,128)(2,1)S(1)} %collective-permute-done.4.h_ref, f32[8,192,256]{2,1,0:T(8,128)S(1)} %get-tuple-element.43.o0_ref, f32[8,192,256]{2,1,0:T(8,128)S(1)} %get-tuple-element.44.o1_ref, ...), custom_call_target="tpu_custom_call" | custom-call | flops 30000001024 | bytes 10000000 | tf_op jit(solution)/shard_map/last_frame/pallas_call | solution.py:449
  35.9 4.0 %collective-permute-done.3.h_ref = bf16[8,192,256]{2,1,0:T(8,128)(2,1)S(1)} collective-permute-done((bf16[8,192,256]{2,1,0:T(8,128)(2,1)S(1)}, bf16[8,192,256]{2,1,0:T(8,128)(2,1)S(1)}, u32[]{:S(2)}, u32[]{:S(2)}) %collective-permute-start.3) | collective-permute-done | bytes 786464 | tf_op jit(solution)/shard_map/ppermute | solution.py:24
  39.9 0.0 copy-done
  39.9 3.0 %other_frame.1 = bf16[2,192,8,256]{3,2,1,0:T(8,128)(2,1)} custom-call(bf16[8,192,256]{2,1,0:T(8,128)(2,1)S(1)} %collective-permute-done.3.h_ref, f32[8,192,256]{2,1,0:T(8,128)S(1)} %get-tuple-element.45.p_ref, bf16[576,1728]{1,0:T(8,128)(2,1)S(1)} %get-tuple-element.40.wt2_ref.wt_ref, f32[8,256]{1,0:T(8,128)S(1)} %get-tuple-element.37.m_ref, ...), custom_call_target="tpu_custom_call" | custom-call | flops 30000001024 | bytes 10000000 | tf_op jit(solution)/shard_map/other_frame/pallas_call | solution.py:450
Async XLA Ops:
  0.1 15.0 %collective-permute-start.1 = (bf16[8,192,256]{2,1,0:T(8,128)(2,1)S(1)}, bf16[8,192,256]{2,1,0:T(8,128)(2,1)S(1)}, u32[]{:S(2)}, u32[]{:S(2)}) collective-permute-start(bf16[8,192,256]{2,1,0:T(8,128)(2,1)S(1)} %get-tuple-element.26.a_ref), channel_id=1, source_target_pairs={{1,2},{3,4},{5,6},{7,8},{9,10},{11,12},{13,14},{17,18},{19,20},{21... | collective-permute-start | bytes 2359304 | tf_op jit(solution)/shard_map/ppermute | solution.py:28
  4.9 18.8 %collective-permute-start = (bf16[8,192,256]{2,1,0:T(8,128)(2,1)S(1)}, bf16[8,192,256]{2,1,0:T(8,128)(2,1)S(1)}, u32[]{:S(2)}, u32[]{:S(2)}) collective-permute-start(bf16[8,192,256]{2,1,0:T(8,128)(2,1)S(1)} %get-tuple-element.30.a0_ref), channel_id=1, source_target_pairs={{0,1},{1,2},{2,3},{3,4},{4,5},{5,6},{6,7},{7,8},{8,9},{9,10},{10,1... | collective-permute-start | bytes 2359304 | tf_op jit(solution)/shard_map/ppermute | solution.py:24
  6.9 8.3 %collective-permute-start.2 = (bf16[8,192,256]{2,1,0:T(8,128)(2,1)S(1)}, bf16[8,192,256]{2,1,0:T(8,128)(2,1)S(1)}, u32[]{:S(2)}, u32[]{:S(2)}) collective-permute-start(bf16[8,192,256]{2,1,0:T(8,128)(2,1)S(1)} %get-tuple-element.31.a1_ref), channel_id=1, source_target_pairs={{0,1},{2,3},{4,5},{6,7},{8,9},{10,11},{12,13},{14,15},{16,17},{18,... | collective-permute-start | bytes 2359304 | tf_op jit(solution)/shard_map/ppermute | solution.py:32
  17.2 15.5 %collective-permute-start.4 = (bf16[8,192,256]{2,1,0:T(8,128)(2,1)S(1)}, bf16[8,192,256]{2,1,0:T(8,128)(2,1)S(1)}, u32[]{:S(2)}, u32[]{:S(2)}) collective-permute-start(bf16[8,192,256]{2,1,0:T(8,128)(2,1)S(1)} %get-tuple-element.39.s1_ref), channel_id=1, source_target_pairs={{0,1},{1,2},{2,3},{3,4},{4,5},{5,6},{6,7},{7,8},{8,9},{9,10},{10,1... | collective-permute-start | bytes 2359304 | tf_op jit(solution)/shard_map/ppermute | solution.py:24
  25.7 14.2 %collective-permute-start.3 = (bf16[8,192,256]{2,1,0:T(8,128)(2,1)S(1)}, bf16[8,192,256]{2,1,0:T(8,128)(2,1)S(1)}, u32[]{:S(2)}, u32[]{:S(2)}) collective-permute-start(bf16[8,192,256]{2,1,0:T(8,128)(2,1)S(1)} %halo_second.1.s0_ref), channel_id=1, source_target_pairs={{0,1},{1,2},{2,3},{3,4},{4,5},{5,6},{6,7},{7,8},{8,9},{9,10},{10,1... | collective-permute-start | bytes 2359304 | tf_op jit(solution)/shard_map/ppermute | solution.py:24
  32.6 7.3 %copy-start = (bf16[2,192,8,256]{3,2,1,0:T(8,128)(2,1)S(1)}, bf16[2,192,8,256]{3,2,1,0:T(8,128)(2,1)}, u32[]{:S(2)}) copy-start(bf16[2,192,8,256]{3,2,1,0:T(8,128)(2,1)} %f_ref.5) | copy-start | bytes 4718596

commit v6 on v5

--- a/solution.py
+++ b/solution.py
@@ -58,9 +58,9 @@
     return m_ref[i : i + 1, :]
 
 
-def turn_pieces(w_ref, wt_ref, taps, start=0):
+def turn_pieces(w_ref, wt_ref, taps):
     def turn(k, lo, hi):
-        base = (k - start) * DEPTH
+        base = k * DEPTH
         wt_ref[k * C : (k + 1) * C, lo:hi] = w_ref[base + lo : base + hi, :].T
 
     return [
@@ -147,8 +147,9 @@
     ]
 
 
-def first_tap(w1_any, w_ref, sem):
-    return pltpu.make_async_copy(w1_any.at[pl.ds(0, DEPTH)], w_ref, sem)
+def taps_copy(w_any, w_ref, lo, hi, sem):
+    span = pl.ds(lo * DEPTH, (hi - lo) * DEPTH)
+    return pltpu.make_async_copy(w_any.at[span], w_ref.at[span], sem)
 
 
 def flat(copies):
@@ -182,7 +183,7 @@
     def _():
         copies = frame_copies(f_ref, 1, raw1_ref, sems)
         gains = pltpu.make_async_copy(gain_any, gain_ref, sems.at[4])
-        later = [first_tap(w1_any, w_ref, sems.at[5])] + flat(frame_copies(f_ref, 0, raw0_ref, sems0))
+        later = [taps_copy(w1_any, w_ref, 0, 1, sems.at[5])] + flat(frame_copies(f_ref, 0, raw0_ref, sems0))
         for copy in copies[0] + [gains] + copies[1] + later:
             copy.start()
 
@@ -201,19 +202,22 @@
 
 def rest_sent(
     a_ref, raw0_ref, g1_ref, _, f_ref, w1_any, gain_any,
-    first_ref, a0_ref, a1_ref, gain_ref, raw_ref, last_ref, t_ref, sems, sems0, sems1,
+    w_ref, a0_ref, a1_ref, gain_ref, raw_ref, last_ref, t_ref, sems, sems0, sems1,
 ):
     far = sends_far()
 
     @pl.when(far)
     def _():
+        others = taps_copy(w1_any, w_ref, 1, TAPS, sems.at[0])
+        others.start()
         a1_ref[...] = a_ref[...]
         activate_frame(raw0_ref, lambda c: g1_ref[c : c + 1, :], t_ref, a0_ref)
+        others.wait()
 
     @pl.when(jnp.logical_not(far))
     def _():
         gains = pltpu.make_async_copy(gain_any, gain_ref, sems.at[0])
-        first = first_tap(w1_any, first_ref, sems.at[1])
+        first = taps_copy(w1_any, w_ref, 0, TAPS, sems.at[1])
         last = frame_copies(f_ref, 1, last_ref, sems1)
         other = frame_copies(f_ref, 0, raw_ref, sems0)
         for copy in last[0] + [gains] + last[1] + flat(other) + [first]:
@@ -247,40 +251,37 @@
 
 
 def own_frames(
-    a0_ref, a1_ref, first_ref, w1_any, w2_any, gain2_any, frames_any,
+    a0_ref, a1_ref, w1_ref, w2_any, gain2_any, frames_any,
     p1_ref, wt1_ref, wt2_ref, m_ref, g2_ref, x0_ref,
-    gain2_ref, frames_ref, x1_ref, w1_ref, w2_ref, sems,
+    gain2_ref, frames_ref, x1_ref, w2_ref, sems,
 ):
     small = [
         pltpu.make_async_copy(frames_any, frames_ref, sems.at[0]),
         pltpu.make_async_copy(gain2_any, gain2_ref, sems.at[1]),
     ]
-    others = pltpu.make_async_copy(w1_any.at[pl.ds(DEPTH, 2 * DEPTH)], w1_ref, sems.at[2])
-    load = pltpu.make_async_copy(w2_any, w2_ref, sems.at[3])
-    for copy in small + [others, load]:
+    load = pltpu.make_async_copy(w2_any, w2_ref, sems.at[2])
+    for copy in small + [load]:
         copy.start()
-    for step in turn_pieces(first_ref, wt1_ref, (0,)):
+    for step in turn_pieces(w1_ref, wt1_ref, (0,)):
         step()
     clear_edges(x1_ref)
     clear_edges(x0_ref)
     put(x1_ref, a1_ref, 0)
     put(x1_ref, a1_ref, 1)
-    turn1 = turn_pieces(w1_ref, wt1_ref, (1, 2), 1)
+    turn1 = turn_pieces(w1_ref, wt1_ref, (1, 2))
     share = C // ROWS
     for row in range(ROWS):
         d = product(wt1_ref, 0, 1, x1_ref, row)
         put(x1_ref, a1_ref, row + 2)
         put(x0_ref, a0_ref, row)
         if row == 2:
-            others.wait()
             for copy in small:
                 copy.wait()
             masks = tap_masks(frames_ref)
             for i in range(8):
                 m_ref[i : i + 1, :] = jnp.full((1, COLS), masks[i % 4], F32)
-        if row >= 2:
-            for step in turn1[(row - 2) * len(turn1) // 6 : (row - 1) * len(turn1) // 6]:
-                step()
+        for step in turn1[row * len(turn1) // ROWS : (row + 1) * len(turn1) // ROWS]:
+            step()
         p1_ref[row] = d
     load.wait()
     turn2 = turn_pieces(w2_ref, wt2_ref, (0, 1, 2))
@@ -303,38 +304,57 @@
         s_ref[row] = second_activation(o1_ref[row] + mask(m_ref, 3) * d, g_ref)
 
 
-def halo_middle(x0_ref, x_ref, wt1_ref, m_ref, s1_ref, wt2_ref, p_ref, q_ref, x1_ref):
-    clear_edges(x1_ref)
-    for row in range(ROWS):
-        d = mask(m_ref, 0) * product(wt1_ref, 1, 2, x_ref, row)
-        put(x1_ref, s1_ref, row)
-        p_ref[row] = d + product(wt1_ref, 0, 1, x0_ref, row)
-    for row in range(ROWS):
-        q_ref[row] = product(wt2_ref, 0, 1, x1_ref, row)
-
-
-def halo_second(h_ref, p_ref, wt_ref, g_ref, m_ref, s_ref, x_ref):
+def halo_middle(x0_ref, x_ref, wt_ref, m_ref, p_ref):
+    for row in range(ROWS):
+        d = mask(m_ref, 0) * product(wt_ref, 1, 2, x_ref, row)
+        p_ref[row] = d + product(wt_ref, 0, 1, x0_ref, row)
+
+
+def halo_second(h_ref, p_ref, wt1_ref, wt2_ref, g_ref, m_ref, sent_ref, x0_ref, x_ref):
     clear_edges(x_ref)
+    clear_edges(x0_ref)
     put(x_ref, h_ref, 0)
     put(x_ref, h_ref, 1)
-    for row in range(ROWS):
-        d = product(wt_ref, 2, 3, x_ref, row)
-        put(x_ref, h_ref, row + 2)
-        s_ref[row] = second_activation(p_ref[row] + mask(m_ref, 1) * d, g_ref)
-
-
-def local_second(s0_ref, p_ref, wt_ref, m_ref, o0_ref, o1_ref, x_ref):
-    clear_edges(x_ref)
-    put(x_ref, s0_ref, 0)
-    put(x_ref, s0_ref, 1)
-    for row in range(ROWS):
-        d = product(wt_ref, 0, 2, x_ref, row)
-        put(x_ref, s0_ref, row + 2)
+    for row in range(ROWS + 1):
+        if row < ROWS:
+            d = product(wt1_ref, 2, 3, x_ref, row)
+            put(x_ref, h_ref, row + 2)
+            act = second_activation(p_ref[row] + mask(m_ref, 1) * d, g_ref)
+            put_row(x0_ref, row, act.astype(F32))
+        if row > 0:
+            sent_ref[row - 1] = product(wt2_ref, 2, 3, x0_ref, row - 1).astype(BF16)
+
+
+def local_second(x0_ref, s1_ref, wt_ref, m_ref, o0_ref, o1_ref, x1_ref):
+    clear_edges(x1_ref)
+    for row in range(ROWS):
+        d = product(wt_ref, 0, 2, x0_ref, row)
+        put(x1_ref, s1_ref, row)
         o0_ref[row] = d[:C]
-        o1_ref[row] = p_ref[row] + mask(m_ref, 2) * d[C:]
-
-
-def last_frame(h_ref, o0_ref, o1_ref, wt_ref, m_ref, p_ref, t_ref, x_ref):
+        o1_ref[row] = mask(m_ref, 2) * d[C:]
+    for row in range(ROWS):
+        o1_ref[row] += product(wt_ref, 0, 1, x1_ref, row)
+
+
+def finish(t_ref, f_ref, index, c, buf_ref):
+    v = jnp.concatenate([t_ref[h, c * ROWS : (c + 1) * ROWS, :] for h in range(2)], axis=1)
+    buf_ref[c] = (f_ref[index, c].astype(F32) + v).astype(BF16)
+
+
+def write_frame(t_ref, f_ref, index, buf_ref, out_ref, sems):
+    step = C // PARTS
+    copies = []
+    for part in range(PARTS):
+        for c in range(part * step, (part + 1) * step):
+            finish(t_ref, f_ref, index, c, buf_ref)
+        span = pl.ds(part * step, step)
+        copies.append(pltpu.make_async_copy(buf_ref.at[span], out_ref.at[index, span], sems.at[part]))
+        copies[-1].start()
+    for copy in copies:
+        copy.wait()
+
+
+def last_frame(h_ref, o0_ref, o1_ref, wt_ref, m_ref, f_ref, p_ref, out_ref, t_ref, x_ref, buf_ref, sems):
     clear_edges(x_ref)
     put(x_ref, h_ref, 0)
     put(x_ref, h_ref, 1)
@@ -343,35 +363,13 @@
         put(x_ref, h_ref, row + 2)
         p_ref[row] = o0_ref[row] + mask(m_ref, 0) * d[:C]
         put_transposed(t_ref, row, o1_ref[row] + mask(m_ref, 3) * d[C:])
-
-
-def other_frame(
-    h_ref, p_ref, wt_ref, m_ref, t1_ref, f_ref, out_ref, t_ref, x_ref, buf0_ref, buf1_ref, sems0, sems1
-):
-    clear_edges(x_ref)
-    put(x_ref, h_ref, 0)
-    put(x_ref, h_ref, 1)
-    share = C // ROWS
-    for row in range(ROWS):
-        d = product(wt_ref, 2, 3, x_ref, row)
-        put(x_ref, h_ref, row + 2)
-        for c in range(row * share, (row + 1) * share):
-            finish(t1_ref, f_ref, 1, c, buf1_ref)
-        put_transposed(t_ref, row, p_ref[row] + mask(m_ref, 1) * d)
-        if (row + 1) % (ROWS // PARTS) == 0:
-            out_copy(buf1_ref, out_ref, 1, row // (ROWS // PARTS), sems1).start()
-    for part in range(PARTS):
-
-        def step(b, _):
-            for j in range(16):
-                finish(t_ref, f_ref, 0, part * (C // PARTS) + b * 16 + j, buf0_ref)
-            return 0
-
-        lax.fori_loop(0, C // PARTS // 16, step, 0)
-        out_copy(buf0_ref, out_ref, 0, part, sems0).start()
-    for part in range(PARTS):
-        out_copy(buf1_ref, out_ref, 1, part, sems1).wait()
-        out_copy(buf0_ref, out_ref, 0, part, sems0).wait()
+    write_frame(t_ref, f_ref, 1, buf_ref, out_ref, sems)
+
+
+def first_frame(d_ref, p_ref, m_ref, f_ref, _, out_ref, t_ref, buf_ref, sems):
+    for row in range(ROWS):
+        put_transposed(t_ref, row, p_ref[row] + mask(m_ref, 1) * d_ref[row].astype(F32))
+    write_frame(t_ref, f_ref, 0, buf_ref, out_ref, sems)
 
 
 VM = pl.BlockSpec(memory_space=pltpu.VMEM)
@@ -385,7 +383,7 @@
 SEMS = pltpu.SemaphoreType.DMA((PARTS,))
 A_SUM = jax.ShapeDtypeStruct((ROWS, C, COLS), F32)
 A_ACT = jax.ShapeDtypeStruct((ROWS, C, COLS), BF16)
-A_FIRST = jax.ShapeDtypeStruct((DEPTH, C), BF16)
+A_WEIGHTS = jax.ShapeDtypeStruct((TAPS * DEPTH, C), BF16)
 A_RAW = jax.ShapeDtypeStruct((C, ROWS, COLS), BF16)
 A_SLABS = jax.ShapeDtypeStruct(((ROWS + 2) * SLAB, COLS), BF16)
 A_NATURAL = jax.ShapeDtypeStruct((2, C * ROWS, HALF), F32)
@@ -399,7 +397,7 @@
     return pltpu.with_memory_space_constraint(value, pltpu.HBM)
 
 
-def call(kernel, in_specs, out_shape, scratch=(), out_specs=None, aliases=None):
+def call(kernel, in_specs, out_shape, scratch=(), out_specs=None, aliases=None, flops=3 * 10**10):
     return pl.pallas_call(
         kernel,
         in_specs=in_specs,
@@ -408,7 +406,7 @@
         scratch_shapes=scratch,
         input_output_aliases=aliases or {},
         compiler_params=pltpu.CompilerParams(vmem_limit_bytes=VMEM_LIMIT),
-        cost_estimate=pl.CostEstimate(flops=3 * 10**10, bytes_accessed=10**7, transcendentals=0),
+        cost_estimate=pl.CostEstimate(flops=flops, bytes_accessed=10**7, transcendentals=0),
         name=kernel.__name__,
     )
 
@@ -417,40 +415,41 @@
     w1 = conv_first.reshape(TAPS * DEPTH, C)
     w2 = conv_second.reshape(TAPS * DEPTH, C)
 
-    a1, raw0, first, g1 = call(
-        first_sent, [HBM] * 3, [A_ACT, A_RAW, A_FIRST, A_HALF_GAINS],
+    a1, raw0, held, g1 = call(
+        first_sent, [HBM] * 3, [A_ACT, A_RAW, A_WEIGHTS, A_HALF_GAINS],
         [RAW, GAIN, NATURAL, pltpu.SemaphoreType.DMA((6,)), pltpu.SemaphoreType.DMA((4,))],
     )(stay(features), stay(w1), stay(gain_first))
     a_far = to_next_pair(a1)
-    first, a0, a1 = call(
-        rest_sent, [VM] * 4 + [HBM] * 3, [A_FIRST, A_ACT, A_ACT],
+    w1, a0, a1 = call(
+        rest_sent, [VM] * 4 + [HBM] * 3, [A_WEIGHTS, A_ACT, A_ACT],
         [
             GAIN, RAW, RAW, NATURAL, pltpu.SemaphoreType.DMA((2,)),
             pltpu.SemaphoreType.DMA((4,)), pltpu.SemaphoreType.DMA((4,)),
         ],
         aliases={3: 0},
-    )(a1, raw0, g1, first, stay(features), stay(w1), stay(gain_first))
+    )(a1, raw0, g1, held, stay(features), stay(w1), stay(gain_first))
     a_earlier = shifted(a0)
     a_near = within_pair(a1)
     p1, wt1, wt2, m, g2, x0 = call(
-        own_frames, [VM] * 3 + [HBM] * 4, [A_SUM, A_TURNED, A_TURNED, A_MASKS, A_GAINS, A_SLABS],
+        own_frames, [VM] * 3 + [HBM] * 3, [A_SUM, A_TURNED, A_TURNED, A_MASKS, A_GAINS, A_SLABS],
         [
             GAIN, pltpu.SMEM(video_frames.shape, jnp.int32), SLABS,
-            pltpu.VMEM((2 * DEPTH, C), BF16), pltpu.VMEM((TAPS * DEPTH, C), BF16),
-            pltpu.SemaphoreType.DMA((4,)),
+            pltpu.VMEM((TAPS * DEPTH, C), BF16), pltpu.SemaphoreType.DMA((3,)),
         ],
-    )(a0, a1, first, stay(w1), stay(w2), stay(gain_second), stay(video_frames))
+    )(a0, a1, w1, stay(w2), stay(gain_second), stay(video_frames))
     s1, x = call(halo_first, [VM] * 6, [A_ACT, A_SLABS])(a_far, a_near, p1, wt1, g2, m)
     s_before = shifted(s1)
-    part, q = call(halo_middle, [VM] * 6, [A_SUM, A_SUM], [SLABS])(x0, x, wt1, m, s1, wt2)
-    s0 = call(halo_second, [VM] * 5, A_ACT, [SLABS])(a_earlier, part, wt1, g2, m)
-    s_earlier = shifted(s0)
-    q0, q1 = call(local_second, [VM] * 4, [A_SUM, A_SUM], [SLABS])(s0, q, wt2, m)
-    part2, t1 = call(last_frame, [VM] * 5, [A_SUM, A_NATURAL], [SLABS])(s_before, q0, q1, wt2, m)
+    part = call(halo_middle, [VM] * 4, A_SUM)(x0, x, wt1, m)
+    sent, x0 = call(halo_second, [VM] * 6, [A_ACT, A_SLABS], [SLABS])(a_earlier, part, wt1, wt2, g2, m)
+    d_earlier = shifted(sent)
+    q0, q1 = call(local_second, [VM] * 4, [A_SUM, A_SUM], [SLABS], flops=10**10)(x0, s1, wt2, m)
+    whole = jax.ShapeDtypeStruct(features.shape, BF16)
+    part, out = call(
+        last_frame, [VM] * 6, [A_SUM, whole], [NATURAL, SLABS, FRAME, SEMS], [VM, ANY], flops=10**10,
+    )(s_before, q0, q1, wt2, m, features)
     return call(
-        other_frame, [VM] * 6, jax.ShapeDtypeStruct(features.shape, BF16),
-        [NATURAL, SLABS, FRAME, FRAME, SEMS, SEMS], out_specs=ANY,
-    )(s_earlier, part2, wt2, m, t1, features)
+        first_frame, [VM] * 4 + [ANY], whole, [NATURAL, FRAME, SEMS], ANY, {4: 0}
+    )(d_earlier, part, m, features, out)
 
 
 def solution(mesh):

time: 43.3 us -> 42.3 us (0.977)
  starting transfers between devices: 12.6 us -> 10.6 us
  waiting for transfers between devices: 3.96 us -> 4.53 us
    ppermute x1, starting transfers between devices: 3.55 us -> 2.28 us  [within_pair(): lax.ppermute(value, 'tm', [(i, i + 1) for i in range(0, lax.axis_size('tm...]
    ppermute x1, waiting for transfers between devices: 0.01 us -> 0.77 us  [to_next_pair(): lax.ppermute(value, 'tm', [(i, i + 1) for i in range(1, lax.axis_size('tm...]
    ppermute x3, starting transfers between devices: 7.8 us -> 7.05 us  [shifted(): lax.ppermute(value, 'tm', [(i, i + 1) for i in range(lax.axis_size('tm')...]
    pallas_call x8, Pallas kernels: 24.2 us -> 24.7 us  [the longest x1 4.49 us: per_device(): call(local_second, [VM] * 4, [A_SUM, A_SUM], [SLABS], flops=10 ** 10)]
  transfers between devices with their start and end apart: 5 -> 5, of which waited for: 1 -> 3; matrix products, arithmetic and copies ran while one was open for 0% -> 0% of each run, Pallas kernels for 54% -> 59%
where the time goes in v6:
time: 42.3 us; the launch traced here: 42.1 us
  Pallas kernels  26.6 us (63%)
  starting transfers between devices  10.6 us (25%)
  waiting for transfers between devices  4.53 us (11%)
    ppermute x3, starting transfers between devices, shifted(): lax.ppermute(value, 'tm', [(i, i + 1) for i in range(lax.axis_size('tm')...  7.05 us
    pallas_call x1, Pallas kernels, per_device(): call(local_second, [VM] * 4, [A_SUM, A_SUM], [SLABS], flops=10 ** 10)  4.49 us
    pallas_call x1, Pallas kernels, per_device(): call(own_frames, [VM] * 3 + [HBM] * 3, [A_SUM, A_TURNED, A_TURNED, A_MASK...  4.38 us
    pallas_call x1, Pallas kernels, per_device(): call(last_frame, [VM] * 6, [A_SUM, whole], [NATURAL, SLABS, FRAME, SEMS],...  4.22 us
    ppermute x3, waiting for transfers between devices, shifted(): lax.ppermute(value, 'tm', [(i, i + 1) for i in range(lax.axis_size('tm')...  3.76 us
    pallas_call x1, Pallas kernels, per_device(): call(rest_sent, [VM] * 4 + [HBM] * 3, [A_WEIGHTS, A_ACT, A_ACT], [GAIN, R...  3.52 us
    pallas_call x1, Pallas kernels, per_device(): call(halo_second, [VM] * 6, [A_ACT, A_SLABS], [SLABS])  3.47 us
    pallas_call x1, Pallas kernels, per_device(): part = call(halo_middle, [VM] * 4, A_SUM)(x0, x, wt1, m)  3.02 us
  transfers between devices with their start and end apart: 5, of which 3 were waited for; matrix products, arithmetic and copies ran while one was open for 0% of the time, Pallas kernels for 59%

profile of v6, /device:TPU:8, one launch (start us, length us, event | category | flops | bytes accessed | tf_op | source)
XLA Modules:
  0.0 42.1 jit_solution(7139819964499194473)
XLA Ops:
  0.0 0.1 first_sent.1
  0.1 1.3 %collective-permute-start.1 = (bf16[8,192,256]{2,1,0:T(8,128)(2,1)S(1)}, bf16[8,192,256]{2,1,0:T(8,128)(2,1)S(1)}, u32[]{:S(2)}, u32[]{:S(2)}) collective-permute-start(bf16[8,192,256]{2,1,0:T(8,128)(2,1)S(1)} %get-tuple-element.26.a_ref), channel_id=1, source_target_pairs={{1,2},{3,4},{5,6},{7,8},{9,10},{11,12},{13,14},{17,18},{19,20},{21... | collective-permute-start | bytes 2359304 | tf_op jit(solution)/shard_map/ppermute | solution.py:28
  1.4 3.5 %rest_sent.1 = (bf16[5184,192]{1,0:T(8,128)(2,1)S(1)}, bf16[8,192,256]{2,1,0:T(8,128)(2,1)S(1)}, bf16[8,192,256]{2,1,0:T(8,128)(2,1)S(1)}) custom-call(bf16[8,192,256]{2,1,0:T(8,128)(2,1)S(1)} %get-tuple-element.26.a_ref, bf16[192,8,256]{2,1,0:T(8,128)(2,1)S(1)} %get-tuple-element.27.raw0_ref, ...), custom_call_target="tpu_custom_call", output_to_operand_aliasing={{0}: (3, {})} | custom-call | flops 30000001024 | bytes 10000000 | tf_op jit(solution)/shard_map/rest_sent/pallas_call | solution.py:423
  4.9 2.3 %collective-permute-start.2 = (bf16[8,192,256]{2,1,0:T(8,128)(2,1)S(1)}, bf16[8,192,256]{2,1,0:T(8,128)(2,1)S(1)}, u32[]{:S(2)}, u32[]{:S(2)}) collective-permute-start(bf16[8,192,256]{2,1,0:T(8,128)(2,1)S(1)} %get-tuple-element.31.a1_ref), channel_id=1, source_target_pairs={{0,1},{2,3},{4,5},{6,7},{8,9},{10,11},{12,13},{14,15},{16,17},{18,... | collective-permute-start | bytes 2359304 | tf_op jit(solution)/shard_map/ppermute | solution.py:32
  7.2 1.9 %collective-permute-start = (bf16[8,192,256]{2,1,0:T(8,128)(2,1)S(1)}, bf16[8,192,256]{2,1,0:T(8,128)(2,1)S(1)}, u32[]{:S(2)}, u32[]{:S(2)}) collective-permute-start(bf16[8,192,256]{2,1,0:T(8,128)(2,1)S(1)} %get-tuple-element.30.a0_ref), channel_id=1, source_target_pairs={{0,1},{1,2},{2,3},{3,4},{4,5},{5,6},{6,7},{7,8},{8,9},{9,10},{10,1... | collective-permute-start | bytes 2359304 | tf_op jit(solution)/shard_map/ppermute | solution.py:24
  9.1 4.4 %own_frames.1 = (f32[8,192,256]{2,1,0:T(8,128)S(1)}, bf16[576,1728]{1,0:T(8,128)(2,1)S(1)}, bf16[576,1728]{1,0:T(8,128)(2,1)S(1)}, f32[8,256]{1,0:T(8,128)S(1)},...) custom-call(bf16[8,192,256]{2,1,0:T(8,128)(2,1)S(1)} %get-tuple-element.30.a0_ref, ...), custom_call_target="tpu_custom_call" | custom-call | flops 30000001024 | bytes 10000000 | tf_op jit(solution)/shard_map/own_frames/pallas_call | solution.py:433
  13.5 0.0 collective-permute-done.2.near_ref
  13.5 0.8 %collective-permute-done.1.far_ref = bf16[8,192,256]{2,1,0:T(8,128)(2,1)S(1)} collective-permute-done((bf16[8,192,256]{2,1,0:T(8,128)(2,1)S(1)}, bf16[8,192,256]{2,1,0:T(8,128)(2,1)S(1)}, u32[]{:S(2)}, u32[]{:S(2)}) %collective-permute-start.1) | collective-permute-done | bytes 786464 | tf_op jit(solution)/shard_map/ppermute | solution.py:28
  14.3 1.9 %halo_first.1 = (bf16[8,192,256]{2,1,0:T(8,128)(2,1)S(1)}, bf16[5760,256]{1,0:T(8,128)(2,1)S(1)}) custom-call(bf16[8,192,256]{2,1,0:T(8,128)(2,1)S(1)} %collective-permute-done.1.far_ref, bf16[8,192,256]{2,1,0:T(8,128)(2,1)S(1)} %collective-permute-done.2.near_ref, f32[8,192,256]{2,1,0:T(8,128)S(1)} %get-tuple-element.34.o1_ref, ...), custom_call_target="tpu_custom_call" | custom-call | flops 30000001024 | bytes 10000000 | tf_op jit(solution)/shard_map/halo_first/pallas_call | solution.py:440
  16.3 3.0 %collective-permute-start.4 = (bf16[8,192,256]{2,1,0:T(8,128)(2,1)S(1)}, bf16[8,192,256]{2,1,0:T(8,128)(2,1)S(1)}, u32[]{:S(2)}, u32[]{:S(2)}) collective-permute-start(bf16[8,192,256]{2,1,0:T(8,128)(2,1)S(1)} %get-tuple-element.41.s1_ref), channel_id=1, source_target_pairs={{0,1},{1,2},{2,3},{3,4},{4,5},{5,6},{6,7},{7,8},{8,9},{9,10},{10,1... | collective-permute-start | bytes 2359304 | tf_op jit(solution)/shard_map/ppermute | solution.py:24
  19.3 3.0 %halo_middle.1.p_ref = f32[8,192,256]{2,1,0:T(8,128)S(1)} custom-call(bf16[5760,256]{1,0:T(8,128)(2,1)S(1)} %get-tuple-element.33.x0_ref, bf16[5760,256]{1,0:T(8,128)(2,1)S(1)} %get-tuple-element.38.x_ref, bf16[576,1728]{1,0:T(8,128)(2,1)S(1)} %get-tuple-element.35.wt_ref.wt1_ref, f32[8,256]{1,0:T(8,128)S(1)} %get-tuple-element.37.m_ref), custom_call_target="tpu_custom_call" | custom-call | flops 30000001024 | bytes 10000000 | tf_op jit(solution)/shard_map/halo_middle/pallas_call | solution.py:442
  22.3 0.5 %collective-permute-done.h_ref = bf16[8,192,256]{2,1,0:T(8,128)(2,1)S(1)} collective-permute-done((bf16[8,192,256]{2,1,0:T(8,128)(2,1)S(1)}, bf16[8,192,256]{2,1,0:T(8,128)(2,1)S(1)}, u32[]{:S(2)}, u32[]{:S(2)}) %collective-permute-start) | collective-permute-done | bytes 786464 | tf_op jit(solution)/shard_map/ppermute | solution.py:24
  22.7 3.5 %halo_second.1 = (bf16[8,192,256]{2,1,0:T(8,128)(2,1)S(1)}, bf16[5760,256]{1,0:T(8,128)(2,1)S(1)}) custom-call(bf16[8,192,256]{2,1,0:T(8,128)(2,1)S(1)} %collective-permute-done.h_ref, f32[8,192,256]{2,1,0:T(8,128)S(1)} %halo_middle.1.p_ref, bf16[576,1728]{1,0:T(8,128)(2,1)S(1)} %get-tuple-element.35.wt_ref.wt1_ref, ...), custom_call_target="tpu_custom_call" | custom-call | flops 30000001024 | bytes 10000000 | tf_op jit(solution)/shard_map/halo_second/pallas_call | solution.py:443
  26.2 2.1 %collective-permute-start.3 = (bf16[8,192,256]{2,1,0:T(8,128)(2,1)S(1)}, bf16[8,192,256]{2,1,0:T(8,128)(2,1)S(1)}, u32[]{:S(2)}, u32[]{:S(2)}) collective-permute-start(bf16[8,192,256]{2,1,0:T(8,128)(2,1)S(1)} %get-tuple-element.40), channel_id=1, source_target_pairs={{0,1},{1,2},{2,3},{3,4},{4,5},{5,6},{6,7},{7,8},{8,9},{9,10},{10,1... | collective-permute-start | bytes 2359304 | tf_op jit(solution)/shard_map/ppermute | solution.py:24
  28.4 0.0 copy-start
  28.4 4.5 %local_second.1 = (f32[8,192,256]{2,1,0:T(8,128)S(1)}, f32[8,192,256]{2,1,0:T(8,128)S(1)}) custom-call(bf16[5760,256]{1,0:T(8,128)(2,1)S(1)} %get-tuple-element.42.x0_ref, bf16[8,192,256]{2,1,0:T(8,128)(2,1)S(1)} %get-tuple-element.41.s1_ref, bf16[576,1728]{1,0:T(8,128)(2,1)S(1)} %get-tuple-element.39.wt2_ref.wt_ref, f32[8,256]{1,0:T(8,128)S(1)} %get-tuple-element.37.m_ref), custom_call_target="tpu_custom_call" | custom-call | flops 10000000000 | bytes 10000000 | tf_op jit(solution)/shard_map/local_second/pallas_call | solution.py:445
  32.9 0.0 collective-permute-done.4.h_ref
  32.9 0.0 copy-done
  32.9 4.2 %last_frame.1 = (f32[8,192,256]{2,1,0:T(8,128)S(1)}, bf16[2,192,8,256]{3,2,1,0:T(8,128)(2,1)}) custom-call(bf16[8,192,256]{2,1,0:T(8,128)(2,1)S(1)} %collective-permute-done.4.h_ref, f32[8,192,256]{2,1,0:T(8,128)S(1)} %get-tuple-element.43.o0_ref, f32[8,192,256]{2,1,0:T(8,128)S(1)} %get-tuple-element.44.o1_ref, ...), custom_call_target="tpu_custom_call" | custom-call | flops 10000000000 | bytes 10000000 | tf_op jit(solution)/shard_map/last_frame/pallas_call | solution.py:447
  37.1 3.3 %collective-permute-done.3.d_ref = bf16[8,192,256]{2,1,0:T(8,128)(2,1)S(1)} collective-permute-done((bf16[8,192,256]{2,1,0:T(8,128)(2,1)S(1)}, bf16[8,192,256]{2,1,0:T(8,128)(2,1)S(1)}, u32[]{:S(2)}, u32[]{:S(2)}) %collective-permute-start.3) | collective-permute-done | bytes 786464 | tf_op jit(solution)/shard_map/ppermute | solution.py:24
  40.4 1.5 %first_frame.1 = bf16[2,192,8,256]{3,2,1,0:T(8,128)(2,1)} custom-call(bf16[8,192,256]{2,1,0:T(8,128)(2,1)S(1)} %collective-permute-done.3.d_ref, f32[8,192,256]{2,1,0:T(8,128)S(1)} %get-tuple-element.45.p_ref, f32[8,256]{1,0:T(8,128)S(1)} %get-tuple-element.37.m_ref, bf16[2,192,8,256]{3,2,1,0:T(8,128)(2,1)S(1)} %copy-done, ...), custom_call_target="tpu_custom_call", output_to_operand_aliasing={{}: (4, {})} | custom-call | flops 30000001024 | bytes 10000000 | tf_op jit(solution)/shard_map/first_frame/pallas_call | solution.py:450
Async XLA Ops:
  0.1 14.2 %collective-permute-start.1 = (bf16[8,192,256]{2,1,0:T(8,128)(2,1)S(1)}, bf16[8,192,256]{2,1,0:T(8,128)(2,1)S(1)}, u32[]{:S(2)}, u32[]{:S(2)}) collective-permute-start(bf16[8,192,256]{2,1,0:T(8,128)(2,1)S(1)} %get-tuple-element.26.a_ref), channel_id=1, source_target_pairs={{1,2},{3,4},{5,6},{7,8},{9,10},{11,12},{13,14},{17,18},{19,20},{21... | collective-permute-start | bytes 2359304 | tf_op jit(solution)/shard_map/ppermute | solution.py:28
  4.9 8.6 %collective-permute-start.2 = (bf16[8,192,256]{2,1,0:T(8,128)(2,1)S(1)}, bf16[8,192,256]{2,1,0:T(8,128)(2,1)S(1)}, u32[]{:S(2)}, u32[]{:S(2)}) collective-permute-start(bf16[8,192,256]{2,1,0:T(8,128)(2,1)S(1)} %get-tuple-element.31.a1_ref), channel_id=1, source_target_pairs={{0,1},{2,3},{4,5},{6,7},{8,9},{10,11},{12,13},{14,15},{16,17},{18,... | collective-permute-start | bytes 2359304 | tf_op jit(solution)/shard_map/ppermute | solution.py:32
  7.2 15.5 %collective-permute-start = (bf16[8,192,256]{2,1,0:T(8,128)(2,1)S(1)}, bf16[8,192,256]{2,1,0:T(8,128)(2,1)S(1)}, u32[]{:S(2)}, u32[]{:S(2)}) collective-permute-start(bf16[8,192,256]{2,1,0:T(8,128)(2,1)S(1)} %get-tuple-element.30.a0_ref), channel_id=1, source_target_pairs={{0,1},{1,2},{2,3},{3,4},{4,5},{5,6},{6,7},{7,8},{8,9},{9,10},{10,1... | collective-permute-start | bytes 2359304 | tf_op jit(solution)/shard_map/ppermute | solution.py:24
  16.3 16.6 %collective-permute-start.4 = (bf16[8,192,256]{2,1,0:T(8,128)(2,1)S(1)}, bf16[8,192,256]{2,1,0:T(8,128)(2,1)S(1)}, u32[]{:S(2)}, u32[]{:S(2)}) collective-permute-start(bf16[8,192,256]{2,1,0:T(8,128)(2,1)S(1)} %get-tuple-element.41.s1_ref), channel_id=1, source_target_pairs={{0,1},{1,2},{2,3},{3,4},{4,5},{5,6},{6,7},{7,8},{8,9},{9,10},{10,1... | collective-permute-start | bytes 2359304 | tf_op jit(solution)/shard_map/ppermute | solution.py:24
  26.2 14.2 %collective-permute-start.3 = (bf16[8,192,256]{2,1,0:T(8,128)(2,1)S(1)}, bf16[8,192,256]{2,1,0:T(8,128)(2,1)S(1)}, u32[]{:S(2)}, u32[]{:S(2)}) collective-permute-start(bf16[8,192,256]{2,1,0:T(8,128)(2,1)S(1)} %get-tuple-element.40), channel_id=1, source_target_pairs={{0,1},{1,2},{2,3},{3,4},{4,5},{5,6},{6,7},{7,8},{8,9},{9,10},{10,1... | collective-permute-start | bytes 2359304 | tf_op jit(solution)/shard_map/ppermute | solution.py:24
  28.4 4.5 %copy-start = (bf16[2,192,8,256]{3,2,1,0:T(8,128)(2,1)S(1)}, bf16[2,192,8,256]{3,2,1,0:T(8,128)(2,1)}, u32[]{:S(2)}) copy-start(bf16[2,192,8,256]{3,2,1,0:T(8,128)(2,1)} %f_ref.7) | copy-start | bytes 4718596

commit v7 on v6

--- a/solution.py
+++ b/solution.py
@@ -237,17 +237,6 @@
 def put_transposed(t_ref, row, values):
     t_ref[0, pl.ds(row, C, stride=ROWS), :] = values[:, :HALF]
     t_ref[1, pl.ds(row, C, stride=ROWS), :] = values[:, HALF:]
-
-
-def finish(t_ref, f_ref, index, c, buf_ref):
-    at = c * ROWS if isinstance(c, int) else pl.multiple_of(c * ROWS, ROWS)
-    v = jnp.concatenate([t_ref[h, pl.ds(at, ROWS), :] for h in range(2)], axis=1)
-    buf_ref[c] = (f_ref[index, c].astype(F32) + v).astype(BF16)
-
-
-def out_copy(buf_ref, out_ref, index, part, sems):
-    span = pl.ds(part * (C // PARTS), C // PARTS)
-    return pltpu.make_async_copy(buf_ref.at[span], out_ref.at[index, span], sems.at[part])
 
 
 def own_frames(
@@ -310,28 +299,49 @@
         p_ref[row] = d + product(wt_ref, 0, 1, x0_ref, row)
 
 
+def next_product(wt_ref, x_ref, sent_ref):
+    for row in range(ROWS):
+        sent_ref[row] = product(wt_ref, 2, 3, x_ref, row).astype(BF16)
+
+
 def halo_second(h_ref, p_ref, wt1_ref, wt2_ref, g_ref, m_ref, sent_ref, x0_ref, x_ref):
     clear_edges(x_ref)
     clear_edges(x0_ref)
     put(x_ref, h_ref, 0)
     put(x_ref, h_ref, 1)
-    for row in range(ROWS + 1):
-        if row < ROWS:
-            d = product(wt1_ref, 2, 3, x_ref, row)
-            put(x_ref, h_ref, row + 2)
-            act = second_activation(p_ref[row] + mask(m_ref, 1) * d, g_ref)
-            put_row(x0_ref, row, act.astype(F32))
-        if row > 0:
-            sent_ref[row - 1] = product(wt2_ref, 2, 3, x0_ref, row - 1).astype(BF16)
-
-
-def local_second(x0_ref, s1_ref, wt_ref, m_ref, o0_ref, o1_ref, x1_ref):
-    clear_edges(x1_ref)
+    for row in range(ROWS):
+        d = product(wt1_ref, 2, 3, x_ref, row)
+        put(x_ref, h_ref, row + 2)
+        act = second_activation(p_ref[row] + mask(m_ref, 1) * d, g_ref)
+        put_row(x0_ref, row, act.astype(F32))
+
+    @pl.when(sends_far())
+    def _():
+        next_product(wt2_ref, x0_ref, sent_ref)
+
+
+def first_part(x0_ref, wt_ref, m_ref, o0_ref, o1_ref):
     for row in range(ROWS):
         d = product(wt_ref, 0, 2, x0_ref, row)
-        put(x1_ref, s1_ref, row)
         o0_ref[row] = d[:C]
         o1_ref[row] = mask(m_ref, 2) * d[C:]
+
+
+def near_second(x0_ref, wt_ref, m_ref, o0_ref, o1_ref, sent_ref):
+    @pl.when(jnp.logical_not(sends_far()))
+    def _():
+        next_product(wt_ref, x0_ref, sent_ref)
+        first_part(x0_ref, wt_ref, m_ref, o0_ref, o1_ref)
+
+
+def local_second(x0_ref, s1_ref, wt_ref, m_ref, _, __, o0_ref, o1_ref, x1_ref):
+    @pl.when(sends_far())
+    def _():
+        first_part(x0_ref, wt_ref, m_ref, o0_ref, o1_ref)
+
+    clear_edges(x1_ref)
+    for row in range(ROWS):
+        put(x1_ref, s1_ref, row)
     for row in range(ROWS):
         o1_ref[row] += product(wt_ref, 0, 1, x1_ref, row)
 
@@ -366,10 +376,22 @@
     write_frame(t_ref, f_ref, 1, buf_ref, out_ref, sems)
 
 
-def first_frame(d_ref, p_ref, m_ref, f_ref, _, out_ref, t_ref, buf_ref, sems):
+def first_frame(d_ref, p_ref, m_ref, f_ref, out_ref, t_ref, buf_ref, sems):
     for row in range(ROWS):
         put_transposed(t_ref, row, p_ref[row] + mask(m_ref, 1) * d_ref[row].astype(F32))
     write_frame(t_ref, f_ref, 0, buf_ref, out_ref, sems)
+
+
+def from_far(d_ref, p_ref, m_ref, f_ref, _, out_ref, *scratch):
+    @pl.when(jnp.logical_not(sends_far()))
+    def _():
+        first_frame(d_ref, p_ref, m_ref, f_ref, out_ref, *scratch)
+
+
+def from_near(d_ref, p_ref, m_ref, f_ref, _, out_ref, *scratch):
+    @pl.when(sends_far())
+    def _():
+        first_frame(d_ref, p_ref, m_ref, f_ref, out_ref, *scratch)
 
 
 VM = pl.BlockSpec(memory_space=pltpu.VMEM)
@@ -441,15 +463,21 @@
     s_before = shifted(s1)
     part = call(halo_middle, [VM] * 4, A_SUM)(x0, x, wt1, m)
     sent, x0 = call(halo_second, [VM] * 6, [A_ACT, A_SLABS], [SLABS])(a_earlier, part, wt1, wt2, g2, m)
-    d_earlier = shifted(sent)
-    q0, q1 = call(local_second, [VM] * 4, [A_SUM, A_SUM], [SLABS], flops=10**10)(x0, s1, wt2, m)
+    d_far = to_next_pair(sent)
+    q0, q1, sent = call(near_second, [VM] * 3, [A_SUM, A_SUM, A_ACT], flops=10**10)(x0, wt2, m)
+    d_near = within_pair(sent)
+    q0, q1 = call(
+        local_second, [VM] * 6, [A_SUM, A_SUM], [SLABS], aliases={4: 0, 5: 1}, flops=10**9
+    )(x0, s1, wt2, m, q0, q1)
     whole = jax.ShapeDtypeStruct(features.shape, BF16)
     part, out = call(
-        last_frame, [VM] * 6, [A_SUM, whole], [NATURAL, SLABS, FRAME, SEMS], [VM, ANY], flops=10**10,
+        last_frame, [VM] * 6, [A_SUM, whole], [NATURAL, SLABS, FRAME, SEMS], [VM, ANY], flops=10**9,
     )(s_before, q0, q1, wt2, m, features)
-    return call(
-        first_frame, [VM] * 4 + [ANY], whole, [NATURAL, FRAME, SEMS], ANY, {4: 0}
-    )(d_earlier, part, m, features, out)
+    for kernel, d in ((from_far, d_far), (from_near, d_near)):
+        out = call(
+            kernel, [VM] * 4 + [ANY], whole, [NATURAL, FRAME, SEMS], ANY, {4: 0}
+        )(d, part, m, features, out)
+    return out
 
 
 def solution(mesh):

time: 42.3 us -> 41.7 us (0.986)
  waiting for transfers between devices: 4.53 us -> 2.58 us
  Pallas kernels: 26.6 us -> 27.4 us
    ppermute x3 -> x2, waiting for transfers between devices: 3.76 us -> 0.47 us  [shifted(): lax.ppermute(value, 'tm', [(i, i + 1) for i in range(lax.axis_size('tm')...]
    ppermute x3 -> x2, starting transfers between devices: 7.05 us -> 4.83 us  [shifted(): lax.ppermute(value, 'tm', [(i, i + 1) for i in range(lax.axis_size('tm')...]
    pallas_call x2 -> x4, Pallas kernels: 5.99 us -> 7.93 us  [the longest x1 4.44 us: per_device(): call(near_second, [VM] * 3, [A_SUM, A_SUM, A_ACT], flops=10 ** 10)]
    ppermute x1 -> x2, waiting for transfers between devices: 0.77 us -> 2.11 us  [to_next_pair(): lax.ppermute(value, 'tm', [(i, i + 1) for i in range(1, lax.axis_size('tm...]
    ppermute x1 -> x2, starting transfers between devices: 2.28 us -> 3.62 us  [within_pair(): lax.ppermute(value, 'tm', [(i, i + 1) for i in range(0, lax.axis_size('tm...]
    ppermute x1 -> x2, starting transfers between devices: 1.29 us -> 2.58 us  [to_next_pair(): lax.ppermute(value, 'tm', [(i, i + 1) for i in range(1, lax.axis_size('tm...]
    pallas_call x1, Pallas kernels: 3.47 us -> 2.29 us  [per_device(): call(halo_second, [VM] * 6, [A_ACT, A_SLABS], [SLABS])]
  transfers between devices with their start and end apart: 5 -> 6, of which waited for: 3 -> 3; matrix products, arithmetic and copies ran while one was open for 0% -> 0% of each run, Pallas kernels for 59% -> 66%
where the time goes in v7:
time: 41.7 us; the launch traced here: 41.3 us
  Pallas kernels  27.4 us (66%)
  starting transfers between devices  11 us (26%)
  waiting for transfers between devices  2.58 us (6%)
    ppermute x2, starting transfers between devices, shifted(): lax.ppermute(value, 'tm', [(i, i + 1) for i in range(lax.axis_size('tm')...  4.83 us
    pallas_call x1, Pallas kernels, per_device(): call(near_second, [VM] * 3, [A_SUM, A_SUM, A_ACT], flops=10 ** 10)  4.44 us
    pallas_call x1, Pallas kernels, per_device(): call(own_frames, [VM] * 3 + [HBM] * 3, [A_SUM, A_TURNED, A_TURNED, A_MASK...  4.3 us
    pallas_call x1, Pallas kernels, per_device(): call(last_frame, [VM] * 6, [A_SUM, whole], [NATURAL, SLABS, FRAME, SEMS],...  4.22 us
    ppermute x2, starting transfers between devices, within_pair(): lax.ppermute(value, 'tm', [(i, i + 1) for i in range(0, lax.axis_size('tm...  3.62 us
    pallas_call x1, Pallas kernels, per_device(): call(rest_sent, [VM] * 4 + [HBM] * 3, [A_WEIGHTS, A_ACT, A_ACT], [GAIN, R...  3.52 us
    pallas_call x1, Pallas kernels, per_device(): part = call(halo_middle, [VM] * 4, A_SUM)(x0, x, wt1, m)  3.04 us
    ppermute x2, starting transfers between devices, to_next_pair(): lax.ppermute(value, 'tm', [(i, i + 1) for i in range(1, lax.axis_size('tm...  2.58 us
  transfers between devices with their start and end apart: 6, of which 3 were waited for; matrix products, arithmetic and copies ran while one was open for 0% of the time, Pallas kernels for 66%

profile of v7, /device:TPU:8, one launch (start us, length us, event | category | flops | bytes accessed | tf_op | source)
XLA Modules:
  0.0 41.3 jit_solution(11946045015831141344)
XLA Ops:
  0.0 0.1 first_sent.1
  0.1 1.3 %collective-permute-start.1 = (bf16[8,192,256]{2,1,0:T(8,128)(2,1)S(1)}, bf16[8,192,256]{2,1,0:T(8,128)(2,1)S(1)}, u32[]{:S(2)}, u32[]{:S(2)}) collective-permute-start(bf16[8,192,256]{2,1,0:T(8,128)(2,1)S(1)} %get-tuple-element.29.a_ref), channel_id=1, source_target_pairs={{1,2},{3,4},{5,6},{7,8},{9,10},{11,12},{13,14},{17,18},{19,20},{21... | collective-permute-start | bytes 2359304 | tf_op jit(solution)/shard_map/ppermute | solution.py:28
  1.4 3.5 %rest_sent.1 = (bf16[5184,192]{1,0:T(8,128)(2,1)S(1)}, bf16[8,192,256]{2,1,0:T(8,128)(2,1)S(1)}, bf16[8,192,256]{2,1,0:T(8,128)(2,1)S(1)}) custom-call(bf16[8,192,256]{2,1,0:T(8,128)(2,1)S(1)} %get-tuple-element.29.a_ref, bf16[192,8,256]{2,1,0:T(8,128)(2,1)S(1)} %get-tuple-element.30.raw0_ref, ...), custom_call_target="tpu_custom_call", output_to_operand_aliasing={{0}: (3, {})} | custom-call | flops 30000001024 | bytes 10000000 | tf_op jit(solution)/shard_map/rest_sent/pallas_call | solution.py:445
  4.9 2.3 %collective-permute-start.2 = (bf16[8,192,256]{2,1,0:T(8,128)(2,1)S(1)}, bf16[8,192,256]{2,1,0:T(8,128)(2,1)S(1)}, u32[]{:S(2)}, u32[]{:S(2)}) collective-permute-start(bf16[8,192,256]{2,1,0:T(8,128)(2,1)S(1)} %get-tuple-element.34.a1_ref), channel_id=1, source_target_pairs={{0,1},{2,3},{4,5},{6,7},{8,9},{10,11},{12,13},{14,15},{16,17},{18,... | collective-permute-start | bytes 2359304 | tf_op jit(solution)/shard_map/ppermute | solution.py:32
  7.2 1.9 %collective-permute-start = (bf16[8,192,256]{2,1,0:T(8,128)(2,1)S(1)}, bf16[8,192,256]{2,1,0:T(8,128)(2,1)S(1)}, u32[]{:S(2)}, u32[]{:S(2)}) collective-permute-start(bf16[8,192,256]{2,1,0:T(8,128)(2,1)S(1)} %get-tuple-element.33.a0_ref), channel_id=1, source_target_pairs={{0,1},{1,2},{2,3},{3,4},{4,5},{5,6},{6,7},{7,8},{8,9},{9,10},{10,1... | collective-permute-start | bytes 2359304 | tf_op jit(solution)/shard_map/ppermute | solution.py:24
  9.1 4.3 %own_frames.1 = (f32[8,192,256]{2,1,0:T(8,128)S(1)}, bf16[576,1728]{1,0:T(8,128)(2,1)S(1)}, bf16[576,1728]{1,0:T(8,128)(2,1)S(1)}, f32[8,256]{1,0:T(8,128)S(1)},...) custom-call(bf16[8,192,256]{2,1,0:T(8,128)(2,1)S(1)} %get-tuple-element.33.a0_ref, ...), custom_call_target="tpu_custom_call" | custom-call | flops 30000001024 | bytes 10000000 | tf_op jit(solution)/shard_map/own_frames/pallas_call | solution.py:455
  13.5 0.0 collective-permute-done.2.near_ref
  13.5 0.8 %collective-permute-done.1.far_ref = bf16[8,192,256]{2,1,0:T(8,128)(2,1)S(1)} collective-permute-done((bf16[8,192,256]{2,1,0:T(8,128)(2,1)S(1)}, bf16[8,192,256]{2,1,0:T(8,128)(2,1)S(1)}, u32[]{:S(2)}, u32[]{:S(2)}) %collective-permute-start.1) | collective-permute-done | bytes 786464 | tf_op jit(solution)/shard_map/ppermute | solution.py:28
  14.3 2.0 %halo_first.1 = (bf16[8,192,256]{2,1,0:T(8,128)(2,1)S(1)}, bf16[5760,256]{1,0:T(8,128)(2,1)S(1)}) custom-call(bf16[8,192,256]{2,1,0:T(8,128)(2,1)S(1)} %collective-permute-done.1.far_ref, bf16[8,192,256]{2,1,0:T(8,128)(2,1)S(1)} %collective-permute-done.2.near_ref, f32[8,192,256]{2,1,0:T(8,128)S(1)} %get-tuple-element.37.o1_ref, ...), custom_call_target="tpu_custom_call" | custom-call | flops 30000001024 | bytes 10000000 | tf_op jit(solution)/shard_map/halo_first/pallas_call | solution.py:462
  16.3 2.9 %collective-permute-start.4 = (bf16[8,192,256]{2,1,0:T(8,128)(2,1)S(1)}, bf16[8,192,256]{2,1,0:T(8,128)(2,1)S(1)}, u32[]{:S(2)}, u32[]{:S(2)}) collective-permute-start(bf16[8,192,256]{2,1,0:T(8,128)(2,1)S(1)} %get-tuple-element.45.s1_ref), channel_id=1, source_target_pairs={{0,1},{1,2},{2,3},{3,4},{4,5},{5,6},{6,7},{7,8},{8,9},{9,10},{10,1... | collective-permute-start | bytes 2359304 | tf_op jit(solution)/shard_map/ppermute | solution.py:24
  19.2 3.0 %halo_middle.1.p_ref = f32[8,192,256]{2,1,0:T(8,128)S(1)} custom-call(bf16[5760,256]{1,0:T(8,128)(2,1)S(1)} %get-tuple-element.36.x0_ref, bf16[5760,256]{1,0:T(8,128)(2,1)S(1)} %get-tuple-element.41.x_ref, bf16[576,1728]{1,0:T(8,128)(2,1)S(1)} %get-tuple-element.38.wt_ref.wt1_ref, f32[8,256]{1,0:T(8,128)S(1)} %get-tuple-element.40.m_ref), custom_call_target="tpu_custom_call" | custom-call | flops 30000001024 | bytes 10000000 | tf_op jit(solution)/shard_map/halo_middle/pallas_call | solution.py:464
  22.3 0.5 %collective-permute-done.h_ref = bf16[8,192,256]{2,1,0:T(8,128)(2,1)S(1)} collective-permute-done((bf16[8,192,256]{2,1,0:T(8,128)(2,1)S(1)}, bf16[8,192,256]{2,1,0:T(8,128)(2,1)S(1)}, u32[]{:S(2)}, u32[]{:S(2)}) %collective-permute-start) | collective-permute-done | bytes 786464 | tf_op jit(solution)/shard_map/ppermute | solution.py:24
  22.7 2.3 %halo_second.1 = (bf16[8,192,256]{2,1,0:T(8,128)(2,1)S(1)}, bf16[5760,256]{1,0:T(8,128)(2,1)S(1)}) custom-call(bf16[8,192,256]{2,1,0:T(8,128)(2,1)S(1)} %collective-permute-done.h_ref, f32[8,192,256]{2,1,0:T(8,128)S(1)} %halo_middle.1.p_ref, bf16[576,1728]{1,0:T(8,128)(2,1)S(1)} %get-tuple-element.38.wt_ref.wt1_ref, ...), custom_call_target="tpu_custom_call" | custom-call | flops 30000001024 | bytes 10000000 | tf_op jit(solution)/shard_map/halo_second/pallas_call | solution.py:465
  25.0 1.3 %collective-permute-start.5 = (bf16[8,192,256]{2,1,0:T(8,128)(2,1)S(1)}, bf16[8,192,256]{2,1,0:T(8,128)(2,1)S(1)}, u32[]{:S(2)}, u32[]{:S(2)}) collective-permute-start(bf16[8,192,256]{2,1,0:T(8,128)(2,1)S(1)} %get-tuple-element.51), channel_id=1, source_target_pairs={{1,2},{3,4},{5,6},{7,8},{9,10},{11,12},{13,14},{17,18},{19,20},{21... | collective-permute-start | bytes 2359304 | tf_op jit(solution)/shard_map/ppermute | solution.py:28
  26.3 4.4 %near_second.1 = (f32[8,192,256]{2,1,0:T(8,128)S(1)}, f32[8,192,256]{2,1,0:T(8,128)S(1)}, bf16[8,192,256]{2,1,0:T(8,128)(2,1)S(1)}) custom-call(bf16[5760,256]{1,0:T(8,128)(2,1)S(1)} %get-tuple-element.43.x0_ref, bf16[576,1728]{1,0:T(8,128)(2,1)S(1)} %get-tuple-element.42.wt2_ref.wt_ref, f32[8,256]{1,0:T(8,128)S(1)} %get-tuple-element.40.m_ref), custom_call_target="tpu_custom_call" | custom-call | flops 10000000000 | bytes 10000000 | tf_op jit(solution)/shard_map/near_second/pallas_call | solution.py:467
  30.8 1.3 %collective-permute-start.3 = (bf16[8,192,256]{2,1,0:T(8,128)(2,1)S(1)}, bf16[8,192,256]{2,1,0:T(8,128)(2,1)S(1)}, u32[]{:S(2)}, u32[]{:S(2)}) collective-permute-start(bf16[8,192,256]{2,1,0:T(8,128)(2,1)S(1)} %get-tuple-element.44), channel_id=1, source_target_pairs={{0,1},{2,3},{4,5},{6,7},{8,9},{10,11},{12,13},{14,15},{16,17},{18,... | collective-permute-start | bytes 2359304 | tf_op jit(solution)/shard_map/ppermute | solution.py:32
  32.1 0.0 copy-start
  32.1 1.9 %local_second.1 = (f32[8,192,256]{2,1,0:T(8,128)S(1)}, f32[8,192,256]{2,1,0:T(8,128)S(1)}) custom-call(bf16[5760,256]{1,0:T(8,128)(2,1)S(1)} %get-tuple-element.43.x0_ref, bf16[8,192,256]{2,1,0:T(8,128)(2,1)S(1)} %get-tuple-element.45.s1_ref, bf16[576,1728]{1,0:T(8,128)(2,1)S(1)} %get-tuple-element.42.wt2_ref.wt_ref, ...), custom_call_target="tpu_custom_call", output_to_operand_aliasing={{0}: (4, {}), {1}: (5, {})} | custom-call | flops 1000000000 | bytes 10000000 | tf_op jit(solution)/shard_map/local_second/pallas_call | solution.py:469
  34.1 0.0 collective-permute-done.4.h_ref
  34.1 4.2 %last_frame.1 = (f32[8,192,256]{2,1,0:T(8,128)S(1)}, bf16[2,192,8,256]{3,2,1,0:T(8,128)(2,1)}) custom-call(bf16[8,192,256]{2,1,0:T(8,128)(2,1)S(1)} %collective-permute-done.4.h_ref, f32[8,192,256]{2,1,0:T(8,128)S(1)} %get-tuple-element.48.o0_ref, f32[8,192,256]{2,1,0:T(8,128)S(1)} %get-tuple-element.49.o1_ref, ...), custom_call_target="tpu_custom_call" | custom-call | flops 1000000000 | bytes 10000000 | tf_op jit(solution)/shard_map/last_frame/pallas_call | solution.py:473
  38.3 1.3 %collective-permute-done.5.d_ref = bf16[8,192,256]{2,1,0:T(8,128)(2,1)S(1)} collective-permute-done((bf16[8,192,256]{2,1,0:T(8,128)(2,1)S(1)}, bf16[8,192,256]{2,1,0:T(8,128)(2,1)S(1)}, u32[]{:S(2)}, u32[]{:S(2)}) %collective-permute-start.5) | collective-permute-done | bytes 786464 | tf_op jit(solution)/shard_map/ppermute | solution.py:28
  39.6 1.5 %from_far.1._ = bf16[2,192,8,256]{3,2,1,0:T(8,128)(2,1)} custom-call(bf16[8,192,256]{2,1,0:T(8,128)(2,1)S(1)} %collective-permute-done.5.d_ref, f32[8,192,256]{2,1,0:T(8,128)S(1)} %get-tuple-element.50.p_ref, f32[8,256]{1,0:T(8,128)S(1)} %get-tuple-element.40.m_ref, bf16[2,192,8,256]{3,2,1,0:T(8,128)(2,1)S(1)} %copy-done, ...), custom_call_target="tpu_custom_call", output_to_operand_aliasing={{}: (4, {})} | custom-call | flops 30000001024 | bytes 10000000 | tf_op jit(solution)/shard_map/from_far/pallas_call | solution.py:477
  41.1 0.0 collective-permute-done.3.d_ref
  41.1 0.1 from_near.1
  (1 shorter events, 0.0 us)
Async XLA Ops:
  0.1 14.2 %collective-permute-start.1 = (bf16[8,192,256]{2,1,0:T(8,128)(2,1)S(1)}, bf16[8,192,256]{2,1,0:T(8,128)(2,1)S(1)}, u32[]{:S(2)}, u32[]{:S(2)}) collective-permute-start(bf16[8,192,256]{2,1,0:T(8,128)(2,1)S(1)} %get-tuple-element.29.a_ref), channel_id=1, source_target_pairs={{1,2},{3,4},{5,6},{7,8},{9,10},{11,12},{13,14},{17,18},{19,20},{21... | collective-permute-start | bytes 2359304 | tf_op jit(solution)/shard_map/ppermute | solution.py:28
  4.9 8.5 %collective-permute-start.2 = (bf16[8,192,256]{2,1,0:T(8,128)(2,1)S(1)}, bf16[8,192,256]{2,1,0:T(8,128)(2,1)S(1)}, u32[]{:S(2)}, u32[]{:S(2)}) collective-permute-start(bf16[8,192,256]{2,1,0:T(8,128)(2,1)S(1)} %get-tuple-element.34.a1_ref), channel_id=1, source_target_pairs={{0,1},{2,3},{4,5},{6,7},{8,9},{10,11},{12,13},{14,15},{16,17},{18,... | collective-permute-start | bytes 2359304 | tf_op jit(solution)/shard_map/ppermute | solution.py:32
  7.2 15.5 %collective-permute-start = (bf16[8,192,256]{2,1,0:T(8,128)(2,1)S(1)}, bf16[8,192,256]{2,1,0:T(8,128)(2,1)S(1)}, u32[]{:S(2)}, u32[]{:S(2)}) collective-permute-start(bf16[8,192,256]{2,1,0:T(8,128)(2,1)S(1)} %get-tuple-element.33.a0_ref), channel_id=1, source_target_pairs={{0,1},{1,2},{2,3},{3,4},{4,5},{5,6},{6,7},{7,8},{8,9},{9,10},{10,1... | collective-permute-start | bytes 2359304 | tf_op jit(solution)/shard_map/ppermute | solution.py:24
  16.3 17.8 %collective-permute-start.4 = (bf16[8,192,256]{2,1,0:T(8,128)(2,1)S(1)}, bf16[8,192,256]{2,1,0:T(8,128)(2,1)S(1)}, u32[]{:S(2)}, u32[]{:S(2)}) collective-permute-start(bf16[8,192,256]{2,1,0:T(8,128)(2,1)S(1)} %get-tuple-element.45.s1_ref), channel_id=1, source_target_pairs={{0,1},{1,2},{2,3},{3,4},{4,5},{5,6},{6,7},{7,8},{8,9},{9,10},{10,1... | collective-permute-start | bytes 2359304 | tf_op jit(solution)/shard_map/ppermute | solution.py:24
  25.0 14.6 %collective-permute-start.5 = (bf16[8,192,256]{2,1,0:T(8,128)(2,1)S(1)}, bf16[8,192,256]{2,1,0:T(8,128)(2,1)S(1)}, u32[]{:S(2)}, u32[]{:S(2)}) collective-permute-start(bf16[8,192,256]{2,1,0:T(8,128)(2,1)S(1)} %get-tuple-element.51), channel_id=1, source_target_pairs={{1,2},{3,4},{5,6},{7,8},{9,10},{11,12},{13,14},{17,18},{19,20},{21... | collective-permute-start | bytes 2359304 | tf_op jit(solution)/shard_map/ppermute | solution.py:28
  30.8 10.3 %collective-permute-start.3 = (bf16[8,192,256]{2,1,0:T(8,128)(2,1)S(1)}, bf16[8,192,256]{2,1,0:T(8,128)(2,1)S(1)}, u32[]{:S(2)}, u32[]{:S(2)}) collective-permute-start(bf16[8,192,256]{2,1,0:T(8,128)(2,1)S(1)} %get-tuple-element.44), channel_id=1, source_target_pairs={{0,1},{2,3},{4,5},{6,7},{8,9},{10,11},{12,13},{14,15},{16,17},{18,... | collective-permute-start | bytes 2359304 | tf_op jit(solution)/shard_map/ppermute | solution.py:32
  32.1 2.0 %copy-start = (bf16[2,192,8,256]{3,2,1,0:T(8,128)(2,1)S(1)}, bf16[2,192,8,256]{3,2,1,0:T(8,128)(2,1)}, u32[]{:S(2)}) copy-start(bf16[2,192,8,256]{3,2,1,0:T(8,128)(2,1)} %f_ref.9) | copy-start | bytes 4718596

commit v8 on v7

--- a/solution.py
+++ b/solution.py
@@ -13,7 +13,7 @@
 SLAB = 3 * C
 DEPTH = 9 * C
 PIECE = 384
-PARTS = 4
+PARTS = 8
 EPS = 1e-06
 VMEM_LIMIT = 18 * 1024 * 1024
 F32 = jnp.float32

time: 41.7 us -> 41.7 us (level)
  no operation moved by 1% of the time
where the time goes in v8:
time: 41.7 us; the launch traced here: 41.4 us
  Pallas kernels  27.4 us (66%)
  starting transfers between devices  11 us (26%)
  waiting for transfers between devices  2.58 us (6%)
    ppermute x2, starting transfers between devices, shifted(): lax.ppermute(value, 'tm', [(i, i + 1) for i in range(lax.axis_size('tm')...  4.83 us
    pallas_call x1, Pallas kernels, per_device(): call(near_second, [VM] * 3, [A_SUM, A_SUM, A_ACT], flops=10 ** 10)  4.44 us
    pallas_call x1, Pallas kernels, per_device(): call(own_frames, [VM] * 3 + [HBM] * 3, [A_SUM, A_TURNED, A_TURNED, A_MASK...  4.3 us
    pallas_call x1, Pallas kernels, per_device(): call(last_frame, [VM] * 6, [A_SUM, whole], [NATURAL, SLABS, FRAME, SEMS],...  4.22 us
    ppermute x2, starting transfers between devices, within_pair(): lax.ppermute(value, 'tm', [(i, i + 1) for i in range(0, lax.axis_size('tm...  3.62 us
    pallas_call x1, Pallas kernels, per_device(): call(rest_sent, [VM] * 4 + [HBM] * 3, [A_WEIGHTS, A_ACT, A_ACT], [GAIN, R...  3.52 us
    pallas_call x1, Pallas kernels, per_device(): part = call(halo_middle, [VM] * 4, A_SUM)(x0, x, wt1, m)  3.04 us
    ppermute x2, starting transfers between devices, to_next_pair(): lax.ppermute(value, 'tm', [(i, i + 1) for i in range(1, lax.axis_size('tm...  2.58 us
  transfers between devices with their start and end apart: 6, of which 3 were waited for; matrix products, arithmetic and copies ran while one was open for 0% of the time, Pallas kernels for 66%

profile of v8, /device:TPU:8, one launch (start us, length us, event | category | flops | bytes accessed | tf_op | source)
XLA Modules:
  0.0 41.4 jit_solution(14101180985363082814)
XLA Ops:
  0.0 0.1 first_sent.1
  0.1 1.3 %collective-permute-start.1 = (bf16[8,192,256]{2,1,0:T(8,128)(2,1)S(1)}, bf16[8,192,256]{2,1,0:T(8,128)(2,1)S(1)}, u32[]{:S(2)}, u32[]{:S(2)}) collective-permute-start(bf16[8,192,256]{2,1,0:T(8,128)(2,1)S(1)} %get-tuple-element.29.a_ref), channel_id=1, source_target_pairs={{1,2},{3,4},{5,6},{7,8},{9,10},{11,12},{13,14},{17,18},{19,20},{21... | collective-permute-start | bytes 2359304 | tf_op jit(solution)/shard_map/ppermute | solution.py:28
  1.4 3.5 %rest_sent.1 = (bf16[5184,192]{1,0:T(8,128)(2,1)S(1)}, bf16[8,192,256]{2,1,0:T(8,128)(2,1)S(1)}, bf16[8,192,256]{2,1,0:T(8,128)(2,1)S(1)}) custom-call(bf16[8,192,256]{2,1,0:T(8,128)(2,1)S(1)} %get-tuple-element.29.a_ref, bf16[192,8,256]{2,1,0:T(8,128)(2,1)S(1)} %get-tuple-element.30.raw0_ref, ...), custom_call_target="tpu_custom_call", output_to_operand_aliasing={{0}: (3, {})} | custom-call | flops 30000001024 | bytes 10000000 | tf_op jit(solution)/shard_map/rest_sent/pallas_call | solution.py:445
  4.9 2.3 %collective-permute-start.2 = (bf16[8,192,256]{2,1,0:T(8,128)(2,1)S(1)}, bf16[8,192,256]{2,1,0:T(8,128)(2,1)S(1)}, u32[]{:S(2)}, u32[]{:S(2)}) collective-permute-start(bf16[8,192,256]{2,1,0:T(8,128)(2,1)S(1)} %get-tuple-element.34.a1_ref), channel_id=1, source_target_pairs={{0,1},{2,3},{4,5},{6,7},{8,9},{10,11},{12,13},{14,15},{16,17},{18,... | collective-permute-start | bytes 2359304 | tf_op jit(solution)/shard_map/ppermute | solution.py:32
  7.2 1.9 %collective-permute-start = (bf16[8,192,256]{2,1,0:T(8,128)(2,1)S(1)}, bf16[8,192,256]{2,1,0:T(8,128)(2,1)S(1)}, u32[]{:S(2)}, u32[]{:S(2)}) collective-permute-start(bf16[8,192,256]{2,1,0:T(8,128)(2,1)S(1)} %get-tuple-element.33.a0_ref), channel_id=1, source_target_pairs={{0,1},{1,2},{2,3},{3,4},{4,5},{5,6},{6,7},{7,8},{8,9},{9,10},{10,1... | collective-permute-start | bytes 2359304 | tf_op jit(solution)/shard_map/ppermute | solution.py:24
  9.1 4.3 %own_frames.1 = (f32[8,192,256]{2,1,0:T(8,128)S(1)}, bf16[576,1728]{1,0:T(8,128)(2,1)S(1)}, bf16[576,1728]{1,0:T(8,128)(2,1)S(1)}, f32[8,256]{1,0:T(8,128)S(1)},...) custom-call(bf16[8,192,256]{2,1,0:T(8,128)(2,1)S(1)} %get-tuple-element.33.a0_ref, ...), custom_call_target="tpu_custom_call" | custom-call | flops 30000001024 | bytes 10000000 | tf_op jit(solution)/shard_map/own_frames/pallas_call | solution.py:455
  13.5 0.0 collective-permute-done.2.near_ref
  13.5 0.8 %collective-permute-done.1.far_ref = bf16[8,192,256]{2,1,0:T(8,128)(2,1)S(1)} collective-permute-done((bf16[8,192,256]{2,1,0:T(8,128)(2,1)S(1)}, bf16[8,192,256]{2,1,0:T(8,128)(2,1)S(1)}, u32[]{:S(2)}, u32[]{:S(2)}) %collective-permute-start.1) | collective-permute-done | bytes 786464 | tf_op jit(solution)/shard_map/ppermute | solution.py:28
  14.3 2.0 %halo_first.1 = (bf16[8,192,256]{2,1,0:T(8,128)(2,1)S(1)}, bf16[5760,256]{1,0:T(8,128)(2,1)S(1)}) custom-call(bf16[8,192,256]{2,1,0:T(8,128)(2,1)S(1)} %collective-permute-done.1.far_ref, bf16[8,192,256]{2,1,0:T(8,128)(2,1)S(1)} %collective-permute-done.2.near_ref, f32[8,192,256]{2,1,0:T(8,128)S(1)} %get-tuple-element.37.o1_ref, ...), custom_call_target="tpu_custom_call" | custom-call | flops 30000001024 | bytes 10000000 | tf_op jit(solution)/shard_map/halo_first/pallas_call | solution.py:462
  16.3 2.9 %collective-permute-start.4 = (bf16[8,192,256]{2,1,0:T(8,128)(2,1)S(1)}, bf16[8,192,256]{2,1,0:T(8,128)(2,1)S(1)}, u32[]{:S(2)}, u32[]{:S(2)}) collective-permute-start(bf16[8,192,256]{2,1,0:T(8,128)(2,1)S(1)} %get-tuple-element.45.s1_ref), channel_id=1, source_target_pairs={{0,1},{1,2},{2,3},{3,4},{4,5},{5,6},{6,7},{7,8},{8,9},{9,10},{10,1... | collective-permute-start | bytes 2359304 | tf_op jit(solution)/shard_map/ppermute | solution.py:24
  19.2 3.0 %halo_middle.1.p_ref = f32[8,192,256]{2,1,0:T(8,128)S(1)} custom-call(bf16[5760,256]{1,0:T(8,128)(2,1)S(1)} %get-tuple-element.36.x0_ref, bf16[5760,256]{1,0:T(8,128)(2,1)S(1)} %get-tuple-element.41.x_ref, bf16[576,1728]{1,0:T(8,128)(2,1)S(1)} %get-tuple-element.38.wt_ref.wt1_ref, f32[8,256]{1,0:T(8,128)S(1)} %get-tuple-element.40.m_ref), custom_call_target="tpu_custom_call" | custom-call | flops 30000001024 | bytes 10000000 | tf_op jit(solution)/shard_map/halo_middle/pallas_call | solution.py:464
  22.3 0.5 %collective-permute-done.h_ref = bf16[8,192,256]{2,1,0:T(8,128)(2,1)S(1)} collective-permute-done((bf16[8,192,256]{2,1,0:T(8,128)(2,1)S(1)}, bf16[8,192,256]{2,1,0:T(8,128)(2,1)S(1)}, u32[]{:S(2)}, u32[]{:S(2)}) %collective-permute-start) | collective-permute-done | bytes 786464 | tf_op jit(solution)/shard_map/ppermute | solution.py:24
  22.7 2.3 %halo_second.1 = (bf16[8,192,256]{2,1,0:T(8,128)(2,1)S(1)}, bf16[5760,256]{1,0:T(8,128)(2,1)S(1)}) custom-call(bf16[8,192,256]{2,1,0:T(8,128)(2,1)S(1)} %collective-permute-done.h_ref, f32[8,192,256]{2,1,0:T(8,128)S(1)} %halo_middle.1.p_ref, bf16[576,1728]{1,0:T(8,128)(2,1)S(1)} %get-tuple-element.38.wt_ref.wt1_ref, ...), custom_call_target="tpu_custom_call" | custom-call | flops 30000001024 | bytes 10000000 | tf_op jit(solution)/shard_map/halo_second/pallas_call | solution.py:465
  25.0 1.3 %collective-permute-start.5 = (bf16[8,192,256]{2,1,0:T(8,128)(2,1)S(1)}, bf16[8,192,256]{2,1,0:T(8,128)(2,1)S(1)}, u32[]{:S(2)}, u32[]{:S(2)}) collective-permute-start(bf16[8,192,256]{2,1,0:T(8,128)(2,1)S(1)} %get-tuple-element.51), channel_id=1, source_target_pairs={{1,2},{3,4},{5,6},{7,8},{9,10},{11,12},{13,14},{17,18},{19,20},{21... | collective-permute-start | bytes 2359304 | tf_op jit(solution)/shard_map/ppermute | solution.py:28
  26.3 4.4 %near_second.1 = (f32[8,192,256]{2,1,0:T(8,128)S(1)}, f32[8,192,256]{2,1,0:T(8,128)S(1)}, bf16[8,192,256]{2,1,0:T(8,128)(2,1)S(1)}) custom-call(bf16[5760,256]{1,0:T(8,128)(2,1)S(1)} %get-tuple-element.43.x0_ref, bf16[576,1728]{1,0:T(8,128)(2,1)S(1)} %get-tuple-element.42.wt2_ref.wt_ref, f32[8,256]{1,0:T(8,128)S(1)} %get-tuple-element.40.m_ref), custom_call_target="tpu_custom_call" | custom-call | flops 10000000000 | bytes 10000000 | tf_op jit(solution)/shard_map/near_second/pallas_call | solution.py:467
  30.8 1.3 %collective-permute-start.3 = (bf16[8,192,256]{2,1,0:T(8,128)(2,1)S(1)}, bf16[8,192,256]{2,1,0:T(8,128)(2,1)S(1)}, u32[]{:S(2)}, u32[]{:S(2)}) collective-permute-start(bf16[8,192,256]{2,1,0:T(8,128)(2,1)S(1)} %get-tuple-element.44), channel_id=1, source_target_pairs={{0,1},{2,3},{4,5},{6,7},{8,9},{10,11},{12,13},{14,15},{16,17},{18,... | collective-permute-start | bytes 2359304 | tf_op jit(solution)/shard_map/ppermute | solution.py:32
  32.1 0.0 copy-start
  32.1 1.9 %local_second.1 = (f32[8,192,256]{2,1,0:T(8,128)S(1)}, f32[8,192,256]{2,1,0:T(8,128)S(1)}) custom-call(bf16[5760,256]{1,0:T(8,128)(2,1)S(1)} %get-tuple-element.43.x0_ref, bf16[8,192,256]{2,1,0:T(8,128)(2,1)S(1)} %get-tuple-element.45.s1_ref, bf16[576,1728]{1,0:T(8,128)(2,1)S(1)} %get-tuple-element.42.wt2_ref.wt_ref, ...), custom_call_target="tpu_custom_call", output_to_operand_aliasing={{0}: (4, {}), {1}: (5, {})} | custom-call | flops 1000000000 | bytes 10000000 | tf_op jit(solution)/shard_map/local_second/pallas_call | solution.py:469
  34.1 0.0 collective-permute-done.4.h_ref
  34.1 4.2 %last_frame.1 = (f32[8,192,256]{2,1,0:T(8,128)S(1)}, bf16[2,192,8,256]{3,2,1,0:T(8,128)(2,1)}) custom-call(bf16[8,192,256]{2,1,0:T(8,128)(2,1)S(1)} %collective-permute-done.4.h_ref, f32[8,192,256]{2,1,0:T(8,128)S(1)} %get-tuple-element.48.o0_ref, f32[8,192,256]{2,1,0:T(8,128)S(1)} %get-tuple-element.49.o1_ref, ...), custom_call_target="tpu_custom_call" | custom-call | flops 1000000000 | bytes 10000000 | tf_op jit(solution)/shard_map/last_frame/pallas_call | solution.py:473
  38.3 1.3 %collective-permute-done.5.d_ref = bf16[8,192,256]{2,1,0:T(8,128)(2,1)S(1)} collective-permute-done((bf16[8,192,256]{2,1,0:T(8,128)(2,1)S(1)}, bf16[8,192,256]{2,1,0:T(8,128)(2,1)S(1)}, u32[]{:S(2)}, u32[]{:S(2)}) %collective-permute-start.5) | collective-permute-done | bytes 786464 | tf_op jit(solution)/shard_map/ppermute | solution.py:28
  39.6 1.5 %from_far.1._ = bf16[2,192,8,256]{3,2,1,0:T(8,128)(2,1)} custom-call(bf16[8,192,256]{2,1,0:T(8,128)(2,1)S(1)} %collective-permute-done.5.d_ref, f32[8,192,256]{2,1,0:T(8,128)S(1)} %get-tuple-element.50.p_ref, f32[8,256]{1,0:T(8,128)S(1)} %get-tuple-element.40.m_ref, bf16[2,192,8,256]{3,2,1,0:T(8,128)(2,1)S(1)} %copy-done, ...), custom_call_target="tpu_custom_call", output_to_operand_aliasing={{}: (4, {})} | custom-call | flops 30000001024 | bytes 10000000 | tf_op jit(solution)/shard_map/from_far/pallas_call | solution.py:477
  41.1 0.0 collective-permute-done.3.d_ref
  41.1 0.1 from_near.1
  (1 shorter events, 0.0 us)
Async XLA Ops:
  0.1 14.2 %collective-permute-start.1 = (bf16[8,192,256]{2,1,0:T(8,128)(2,1)S(1)}, bf16[8,192,256]{2,1,0:T(8,128)(2,1)S(1)}, u32[]{:S(2)}, u32[]{:S(2)}) collective-permute-start(bf16[8,192,256]{2,1,0:T(8,128)(2,1)S(1)} %get-tuple-element.29.a_ref), channel_id=1, source_target_pairs={{1,2},{3,4},{5,6},{7,8},{9,10},{11,12},{13,14},{17,18},{19,20},{21... | collective-permute-start | bytes 2359304 | tf_op jit(solution)/shard_map/ppermute | solution.py:28
  4.9 8.5 %collective-permute-start.2 = (bf16[8,192,256]{2,1,0:T(8,128)(2,1)S(1)}, bf16[8,192,256]{2,1,0:T(8,128)(2,1)S(1)}, u32[]{:S(2)}, u32[]{:S(2)}) collective-permute-start(bf16[8,192,256]{2,1,0:T(8,128)(2,1)S(1)} %get-tuple-element.34.a1_ref), channel_id=1, source_target_pairs={{0,1},{2,3},{4,5},{6,7},{8,9},{10,11},{12,13},{14,15},{16,17},{18,... | collective-permute-start | bytes 2359304 | tf_op jit(solution)/shard_map/ppermute | solution.py:32
  7.2 15.5 %collective-permute-start = (bf16[8,192,256]{2,1,0:T(8,128)(2,1)S(1)}, bf16[8,192,256]{2,1,0:T(8,128)(2,1)S(1)}, u32[]{:S(2)}, u32[]{:S(2)}) collective-permute-start(bf16[8,192,256]{2,1,0:T(8,128)(2,1)S(1)} %get-tuple-element.33.a0_ref), channel_id=1, source_target_pairs={{0,1},{1,2},{2,3},{3,4},{4,5},{5,6},{6,7},{7,8},{8,9},{9,10},{10,1... | collective-permute-start | bytes 2359304 | tf_op jit(solution)/shard_map/ppermute | solution.py:24
  16.3 17.8 %collective-permute-start.4 = (bf16[8,192,256]{2,1,0:T(8,128)(2,1)S(1)}, bf16[8,192,256]{2,1,0:T(8,128)(2,1)S(1)}, u32[]{:S(2)}, u32[]{:S(2)}) collective-permute-start(bf16[8,192,256]{2,1,0:T(8,128)(2,1)S(1)} %get-tuple-element.45.s1_ref), channel_id=1, source_target_pairs={{0,1},{1,2},{2,3},{3,4},{4,5},{5,6},{6,7},{7,8},{8,9},{9,10},{10,1... | collective-permute-start | bytes 2359304 | tf_op jit(solution)/shard_map/ppermute | solution.py:24
  25.0 14.6 %collective-permute-start.5 = (bf16[8,192,256]{2,1,0:T(8,128)(2,1)S(1)}, bf16[8,192,256]{2,1,0:T(8,128)(2,1)S(1)}, u32[]{:S(2)}, u32[]{:S(2)}) collective-permute-start(bf16[8,192,256]{2,1,0:T(8,128)(2,1)S(1)} %get-tuple-element.51), channel_id=1, source_target_pairs={{1,2},{3,4},{5,6},{7,8},{9,10},{11,12},{13,14},{17,18},{19,20},{21... | collective-permute-start | bytes 2359304 | tf_op jit(solution)/shard_map/ppermute | solution.py:28
  30.8 10.3 %collective-permute-start.3 = (bf16[8,192,256]{2,1,0:T(8,128)(2,1)S(1)}, bf16[8,192,256]{2,1,0:T(8,128)(2,1)S(1)}, u32[]{:S(2)}, u32[]{:S(2)}) collective-permute-start(bf16[8,192,256]{2,1,0:T(8,128)(2,1)S(1)} %get-tuple-element.44), channel_id=1, source_target_pairs={{0,1},{2,3},{4,5},{6,7},{8,9},{10,11},{12,13},{14,15},{16,17},{18,... | collective-permute-start | bytes 2359304 | tf_op jit(solution)/shard_map/ppermute | solution.py:32
  32.1 2.0 %copy-start = (bf16[2,192,8,256]{3,2,1,0:T(8,128)(2,1)S(1)}, bf16[2,192,8,256]{3,2,1,0:T(8,128)(2,1)}, u32[]{:S(2)}) copy-start(bf16[2,192,8,256]{3,2,1,0:T(8,128)(2,1)} %f_ref.9) | copy-start | bytes 4718596
